TPU v7x, 32 devices: a whole 2x2x4 slice. The times are simulated.
32 devices in a mesh: fsdp: 8 (over z, y), seq: 4 (over x, core).
Axes of the slice: x: 2, y: 2, z: 4, core: 2. Of those that a mesh axis runs over, the one named last changes fastest.
Arguments:
- tokens: bfloat16 [8, 1024, 2048], P(None, 'fsdp', 'seq'), may hold values from -6 to 6
- cotangent: bfloat16 [8, 1024, 2048], P(None, 'fsdp', 'seq'), may hold values from -6 to 6
- query_weight: bfloat16 [2048, 2048], P('fsdp'), may hold values from -0.125 to 0.125
- key_matrix: bfloat16 [2048, 1024], P('fsdp'), may hold values from -0.125 to 0.125
- value_matrix: bfloat16 [2048, 1024], P('fsdp'), may hold values from -0.125 to 0.125
- output_weight: bfloat16 [2048, 2048], P('fsdp'), may hold values from -1 to 1
- gate_weight: bfloat16 [2048, 8192], P('fsdp'), may hold values from -0.125 to 0.125
- up_weight: bfloat16 [2048, 8192], P('fsdp'), may hold values from -0.125 to 0.125
- down_weight: bfloat16 [8192, 2048], P('fsdp'), may hold values from -0.0625 to 0.0625
- prenorm_gain: bfloat16 [2048], P('fsdp'), may hold values from 0.5 to 1.5
- midnorm_gain: bfloat16 [2048], P('fsdp'), may hold values from 0.5 to 1.5
- seq_len: int32 [8], replicated, may hold values from 512 to 1024, as said below
- stream_order: int32 [8], replicated, may hold values from 0 to 7, each once
Outputs:
- block_output: bfloat16 [8, 1024, 2048], P(None, 'fsdp', 'seq')
- token_gradient: bfloat16 [8, 1024, 2048], P(None, 'fsdp', 'seq')
- query_gradient: float32 [2048, 2048], P('fsdp')
- key_gradient: float32 [2048, 1024], P('fsdp')
- value_gradient: float32 [2048, 1024], P('fsdp')
- output_gradient: float32 [2048, 2048], P('fsdp')
- gate_gradient: float32 [2048, 8192], P('fsdp')
- up_gradient: float32 [2048, 8192], P('fsdp')
- down_gradient: float32 [8192, 2048], P('fsdp')
- prenorm_gradient: float32 [2048], P('fsdp')
- midnorm_gradient: float32 [2048], P('fsdp')
Inputs may be any that keep to these rules, and one draw needn't show every extreme that they name: `seq_len`: in every draw one sequence has 1024 tokens and another 512. `stream_order`: a permutation of the groups.
All inputs are finite; a program needn't handle non-finite values.
Results may differ from a plain program's by a relative error of at most 0.02.
Values may be sent and summed in bfloat16 or wider, within the bound.
No kernel may reach another device: no remote copies, remote signals or barrier semaphores. Data moves between devices by JAX's collectives and lax.ppermute only.
A program may use at most 512 MiB of HBM per device.

v0:
```python
import math

import jax
import jax.numpy as jnp
from jax import lax
from jax.sharding import PartitionSpec as P

QUERY_HEADS = 8
KEY_VALUE_HEADS = 4
HEAD_SIZE = 256
QBLK = 512


EPS_NORM = 1e-06
ROPE_BASE = 1000042.0
MASK_FILL = -1e30


def rope_tables(positions):
    half_dim = HEAD_SIZE // 2
    frequency = jnp.exp(
        jnp.arange(half_dim, dtype=jnp.float32) * (-2.0 * math.log(ROPE_BASE) / HEAD_SIZE)
    )
    angles = positions[:, None] * frequency[None, :]
    return (jnp.cos(angles)[:, None, :], jnp.sin(angles)[:, None, :])


def rotate(vectors, cos_t, sin_t):
    half_dim = vectors.shape[-1] // 2
    front_half = vectors[..., :half_dim]
    behind = vectors[..., half_dim:]
    return jnp.concatenate(
        [front_half * cos_t - behind * sin_t, behind * cos_t + front_half * sin_t], axis=-1
    )


def unrotate(vectors, cos_t, sin_t):
    half_dim = vectors.shape[-1] // 2
    front_half = vectors[..., :half_dim]
    behind = vectors[..., half_dim:]
    return jnp.concatenate(
        [front_half * cos_t + behind * sin_t, behind * cos_t - front_half * sin_t], axis=-1
    )


def norm_forward(hidden, gain_vec):
    factor = lax.rsqrt(jnp.mean(hidden * hidden, axis=-1, keepdims=True) + EPS_NORM)
    return ((hidden * factor * gain_vec).astype(jnp.bfloat16), factor)


def norm_backward(upstream, hidden, factor, gain_vec):
    scaled = upstream * gain_vec
    gain_part = jnp.sum(upstream * hidden * factor, axis=0)
    inner_sum = jnp.mean(scaled * hidden, axis=-1, keepdims=True)
    return (factor * scaled - hidden * (factor * factor * factor) * inner_sum, gain_part)


def stream_tables(seq_len, stream_order, block_rows, groups):
    block_count = (seq_len + block_rows - 1) // block_rows
    member = (stream_order[:, None] == jnp.arange(groups, dtype=jnp.int32)[None, :]).astype(
        jnp.int32
    )
    ordered = jnp.sum(member * block_count[None, :], axis=1)
    firsts = jnp.cumsum(ordered) - ordered
    seq_start = jnp.sum(member * firsts[:, None], axis=0)
    return (block_count, seq_start)


def route_table(seq_start, block_count, group_me, slot_count, groups, per_pair):
    block_ids = jnp.arange(slot_count, dtype=jnp.int32) * groups + group_me
    offsets = block_ids[:, None] - seq_start[None, :]
    inside = (offsets >= 0) & (offsets < block_count[None, :])
    pair_slot = jnp.where(inside, offsets // groups, -1)
    return (pair_slot[:, :, None] == jnp.arange(per_pair, dtype=jnp.int32)[None, None, :]).astype(
        jnp.bfloat16
    )


def into_sequence(received, shift_by, seq_rows):
    rolled = jnp.roll(received, -shift_by, axis=1)
    return rolled.reshape(-1, received.shape[-1])[:seq_rows]


def from_sequence(rows_in, shift_by, per_pair, groups, block_rows):
    pad_rows = per_pair * groups * block_rows - rows_in.shape[0]
    padded = jnp.pad(rows_in, ((0, pad_rows), (0, 0)))
    shaped = padded.reshape(per_pair, groups, block_rows, rows_in.shape[-1])
    return jnp.roll(shaped, shift_by, axis=1)


def body(
    tokens,
    cotangent,
    query_weight,
    key_matrix,
    value_matrix,
    output_weight,
    gate_weight,
    up_weight,
    down_weight,
    prenorm_gain,
    midnorm_gain,
    seq_len,
    stream_order,
):
    groups = lax.axis_size("fsdp")
    seq_parts = lax.axis_size("seq")
    group_me = lax.axis_index("fsdp")
    part_me = lax.axis_index("seq")
    slot_count, block_rows, feature_part = tokens.shape
    seq_rows = slot_count * block_rows
    token_rows = seq_rows // seq_parts
    per_pair = (slot_count + groups - 1) // groups
    block_count, seq_start = stream_tables(seq_len, stream_order, block_rows, groups)
    picked = jnp.arange(groups, dtype=jnp.int32) == group_me
    my_start = jnp.sum(jnp.where(picked, seq_start, 0))
    my_length = jnp.sum(jnp.where(picked, seq_len, 0))
    shift_by = my_start % groups
    routes = route_table(seq_start, block_count, group_me, slot_count, groups, per_pair)
    send_in = jnp.einsum(
        "jgc,jrf->cgrf", routes, tokens, preferred_element_type=jnp.float32
    ).astype(jnp.bfloat16)
    send_cot = jnp.einsum(
        "jgc,jrf->cgrf", routes, cotangent, preferred_element_type=jnp.float32
    ).astype(jnp.bfloat16)
    got_in, got_cot = (
        lax.all_to_all(send_in, "fsdp", split_axis=1, concat_axis=1, tiled=True),
        lax.all_to_all(send_cot, "fsdp", split_axis=1, concat_axis=1, tiled=True),
    )
    seq_in = into_sequence(got_in, shift_by, seq_rows)
    seq_cot = into_sequence(got_cot, shift_by, seq_rows)
    rows_in, rows_cot = (
        lax.all_to_all(seq_in, "seq", split_axis=0, concat_axis=1, tiled=True),
        lax.all_to_all(seq_cot, "seq", split_axis=0, concat_axis=1, tiled=True),
    )
    positions = part_me * token_rows + jnp.arange(token_rows, dtype=jnp.int32)
    valid_rows = (positions < my_length).astype(jnp.float32)[:, None]
    cos_t, sin_t = rope_tables(positions.astype(jnp.float32))
    weight_set = (
        query_weight,
        key_matrix,
        value_matrix,
        output_weight,
        gate_weight,
        up_weight,
        down_weight,
        prenorm_gain,
        midnorm_gain,
    )
    gathered = (
        lax.all_gather(weight_set[0], "fsdp", axis=0, tiled=True),
        lax.all_gather(weight_set[1], "fsdp", axis=0, tiled=True),
        lax.all_gather(weight_set[2], "fsdp", axis=0, tiled=True),
        lax.all_gather(weight_set[3], "fsdp", axis=0, tiled=True),
        lax.all_gather(weight_set[4], "fsdp", axis=0, tiled=True),
        lax.all_gather(weight_set[5], "fsdp", axis=0, tiled=True),
        lax.all_gather(weight_set[6], "fsdp", axis=0, tiled=True),
        lax.all_gather(weight_set[7], "fsdp", axis=0, tiled=True),
        lax.all_gather(weight_set[8], "fsdp", axis=0, tiled=True),
    )
    (
        full_query,
        full_key,
        full_value,
        full_output,
        full_gate,
        full_up,
        full_down,
        full_prenorm,
        full_midnorm,
    ) = gathered
    gain_pre = full_prenorm.astype(jnp.float32)
    gain_mid = full_midnorm.astype(jnp.float32)
    hidden_zero = rows_in.astype(jnp.float32) * valid_rows
    normalized_rows, factor_pre = norm_forward(hidden_zero, gain_pre)
    query_pre = jnp.dot(normalized_rows, full_query, preferred_element_type=jnp.float32).reshape(
        token_rows, QUERY_HEADS, HEAD_SIZE
    )
    key_before_rotation = jnp.dot(
        normalized_rows, full_key, preferred_element_type=jnp.float32
    ).reshape(token_rows, KEY_VALUE_HEADS, HEAD_SIZE)
    queries = rotate(query_pre, cos_t, sin_t).astype(jnp.bfloat16)
    keys_tok = rotate(key_before_rotation, cos_t, sin_t).astype(jnp.bfloat16)
    values_tok = (
        jnp.dot(normalized_rows, full_value, preferred_element_type=jnp.float32)
        .astype(jnp.bfloat16)
        .reshape(token_rows, KEY_VALUE_HEADS, HEAD_SIZE)
    )
    head_q, head_k, head_v = (
        lax.all_to_all(queries, "seq", split_axis=1, concat_axis=0, tiled=True),
        lax.all_to_all(keys_tok, "seq", split_axis=1, concat_axis=0, tiled=True),
        lax.all_to_all(values_tok, "seq", split_axis=1, concat_axis=0, tiled=True),
    )
    heads_per_group = QUERY_HEADS // KEY_VALUE_HEADS
    kv_local = head_k.shape[1]
    q_local = head_q.shape[1]
    grouped_q = head_q.reshape(seq_rows, kv_local, heads_per_group, HEAD_SIZE)
    key_pos = jnp.arange(seq_rows, dtype=jnp.int32)
    key_ok = key_pos < my_length
    factor = 1.0 / math.sqrt(HEAD_SIZE)
    firsts = jnp.arange(seq_rows // QBLK, dtype=jnp.int32) * QBLK

    def block_scores(first_row):
        query_rows = lax.dynamic_slice_in_dim(grouped_q, first_row, QBLK, 0)
        scores = (
            jnp.einsum("qgrd,kgd->grqk", query_rows, head_k, preferred_element_type=jnp.float32)
            * factor
        )
        query_pos = first_row + jnp.arange(QBLK, dtype=jnp.int32)
        allowed = (key_pos[None, :] <= query_pos[:, None]) & key_ok[None, :]
        return (jnp.where(allowed[None, None, :, :], scores, MASK_FILL), query_rows)

    def forward_block(first_row):
        scores, unused = block_scores(first_row)
        row_top = jnp.max(scores, axis=-1, keepdims=True)
        exponent = jnp.exp(scores - row_top)
        totals = jnp.sum(exponent, axis=-1, keepdims=True)
        prob_rows = (exponent / totals).astype(jnp.bfloat16)
        mixed_rows = jnp.einsum(
            "grqk,kgd->qgrd", prob_rows, head_v, preferred_element_type=jnp.float32
        )
        return (mixed_rows.astype(jnp.bfloat16), (row_top + jnp.log(totals))[..., 0])

    mixed_blocks, lse_blocks = lax.map(forward_block, firsts)
    head_mixed = mixed_blocks.reshape(seq_rows, q_local, HEAD_SIZE)
    mixed_tok = lax.all_to_all(head_mixed, "seq", split_axis=0, concat_axis=1, tiled=True).reshape(
        token_rows, QUERY_HEADS * HEAD_SIZE
    )
    hidden_one = hidden_zero + jnp.dot(mixed_tok, full_output, preferred_element_type=jnp.float32)
    normed_two, factor_mid = norm_forward(hidden_one, gain_mid)
    gate_pre = jnp.dot(normed_two, full_gate, preferred_element_type=jnp.float32)
    up_pre = jnp.dot(normed_two, full_up, preferred_element_type=jnp.float32)
    gate_sig = jax.nn.sigmoid(gate_pre)
    gate_act = gate_pre * gate_sig
    activated = (gate_act * up_pre).astype(jnp.bfloat16)
    block_rows_out = (
        (hidden_one + jnp.dot(activated, full_down, preferred_element_type=jnp.float32))
        * valid_rows
    ).astype(jnp.bfloat16)
    back_set = (
        lax.all_gather(weight_set[0], "fsdp", axis=0, tiled=True),
        lax.all_gather(weight_set[1], "fsdp", axis=0, tiled=True),
        lax.all_gather(weight_set[2], "fsdp", axis=0, tiled=True),
        lax.all_gather(weight_set[3], "fsdp", axis=0, tiled=True),
        lax.all_gather(weight_set[4], "fsdp", axis=0, tiled=True),
        lax.all_gather(weight_set[5], "fsdp", axis=0, tiled=True),
        lax.all_gather(weight_set[6], "fsdp", axis=0, tiled=True),
        lax.all_gather(weight_set[7], "fsdp", axis=0, tiled=True),
        lax.all_gather(weight_set[8], "fsdp", axis=0, tiled=True),
    )
    (
        back_query,
        back_key,
        back_value,
        back_output,
        back_gate,
        back_up,
        back_down,
        back_prenorm,
        back_midnorm,
    ) = back_set
    upstream = rows_cot.astype(jnp.float32) * valid_rows
    down_in = upstream.astype(jnp.bfloat16)
    down_part = jnp.einsum("tf,td->fd", activated, down_in, preferred_element_type=jnp.float32)
    act_grad = jnp.einsum("td,fd->tf", down_in, back_down, preferred_element_type=jnp.float32)
    gate_in = (act_grad * up_pre * gate_sig * (1.0 + gate_pre * (1.0 - gate_sig))).astype(
        jnp.bfloat16
    )
    up_in = (act_grad * gate_act).astype(jnp.bfloat16)
    gate_part = jnp.einsum("td,tf->df", normed_two, gate_in, preferred_element_type=jnp.float32)
    up_part = jnp.einsum("td,tf->df", normed_two, up_in, preferred_element_type=jnp.float32)
    normed_two_grad = jnp.einsum(
        "tf,df->td", gate_in, back_gate, preferred_element_type=jnp.float32
    ) + jnp.einsum("tf,df->td", up_in, back_up, preferred_element_type=jnp.float32)
    mid_upstream, midnorm_part = norm_backward(
        normed_two_grad, hidden_one, factor_mid, back_midnorm.astype(jnp.float32)
    )
    hidden_one_grad = upstream + mid_upstream
    attn_in = hidden_one_grad.astype(jnp.bfloat16)
    output_part = jnp.einsum("td,te->de", mixed_tok, attn_in, preferred_element_type=jnp.float32)
    mixed_grad = (
        jnp.einsum("te,de->td", attn_in, back_output, preferred_element_type=jnp.float32)
        .astype(jnp.bfloat16)
        .reshape(token_rows, QUERY_HEADS, HEAD_SIZE)
    )
    head_dmix = lax.all_to_all(mixed_grad, "seq", split_axis=1, concat_axis=0, tiled=True)
    grouped_dmix = head_dmix.reshape(seq_rows, kv_local, heads_per_group, HEAD_SIZE)

    def backward_block(carry_pair, block_in):
        key_acc, value_acc = carry_pair
        first_row, lse_rows = block_in
        scores, query_rows = block_scores(first_row)
        prob_rows = jnp.exp(scores - lse_rows[..., None])
        prob_low = prob_rows.astype(jnp.bfloat16)
        dmix_rows = lax.dynamic_slice_in_dim(grouped_dmix, first_row, QBLK, 0)
        value_acc = value_acc + jnp.einsum(
            "grqk,qgrd->kgd", prob_low, dmix_rows, preferred_element_type=jnp.float32
        )
        prob_grad = jnp.einsum(
            "qgrd,kgd->grqk", dmix_rows, head_v, preferred_element_type=jnp.float32
        )
        inner_sum = jnp.sum(prob_grad * prob_rows, axis=-1, keepdims=True)
        score_grad = (prob_rows * (prob_grad - inner_sum)).astype(jnp.bfloat16) * factor
        query_grad_rows = jnp.einsum(
            "grqk,kgd->qgrd", score_grad, head_k, preferred_element_type=jnp.float32
        ).astype(jnp.bfloat16)
        key_acc = key_acc + jnp.einsum(
            "grqk,qgrd->kgd", score_grad, query_rows, preferred_element_type=jnp.float32
        )
        return ((key_acc, value_acc), query_grad_rows)

    empty_kv = jnp.zeros((seq_rows, kv_local, HEAD_SIZE), jnp.float32)
    kv_sums, query_grad_blocks = lax.scan(
        backward_block, (empty_kv, empty_kv), (firsts, lse_blocks)
    )
    head_dq = query_grad_blocks.reshape(seq_rows, q_local, HEAD_SIZE)
    head_dk = kv_sums[0].astype(jnp.bfloat16)
    head_dv = kv_sums[1].astype(jnp.bfloat16)
    tok_dq, tok_dk, token_value_gradient = (
        lax.all_to_all(head_dq, "seq", split_axis=0, concat_axis=1, tiled=True),
        lax.all_to_all(head_dk, "seq", split_axis=0, concat_axis=1, tiled=True),
        lax.all_to_all(head_dv, "seq", split_axis=0, concat_axis=1, tiled=True),
    )
    query_pre_grad = (
        unrotate(tok_dq.astype(jnp.float32), cos_t, sin_t)
        .astype(jnp.bfloat16)
        .reshape(token_rows, QUERY_HEADS * HEAD_SIZE)
    )
    key_pre_grad = (
        unrotate(tok_dk.astype(jnp.float32), cos_t, sin_t)
        .astype(jnp.bfloat16)
        .reshape(token_rows, KEY_VALUE_HEADS * HEAD_SIZE)
    )
    incoming_value_gradient = token_value_gradient.reshape(token_rows, KEY_VALUE_HEADS * HEAD_SIZE)
    query_part = jnp.einsum(
        "td,te->de", normalized_rows, query_pre_grad, preferred_element_type=jnp.float32
    )
    key_part = jnp.einsum(
        "td,te->de", normalized_rows, key_pre_grad, preferred_element_type=jnp.float32
    )
    value_part = jnp.einsum(
        "td,te->de", normalized_rows, incoming_value_gradient, preferred_element_type=jnp.float32
    )
    normed_grad = jnp.einsum(
        "te,de->td", query_pre_grad, back_query, preferred_element_type=jnp.float32
    )
    normed_grad = normed_grad + jnp.einsum(
        "te,de->td", key_pre_grad, back_key, preferred_element_type=jnp.float32
    )
    normed_grad = normed_grad + jnp.einsum(
        "te,de->td", incoming_value_gradient, back_value, preferred_element_type=jnp.float32
    )
    pre_upstream, prenorm_part = norm_backward(
        normed_grad, hidden_zero, factor_pre, back_prenorm.astype(jnp.float32)
    )
    token_rows_grad = ((hidden_one_grad + pre_upstream) * valid_rows).astype(jnp.bfloat16)
    back_out, back_grad = (
        lax.all_to_all(block_rows_out, "seq", split_axis=1, concat_axis=0, tiled=True),
        lax.all_to_all(token_rows_grad, "seq", split_axis=1, concat_axis=0, tiled=True),
    )
    send_out = from_sequence(back_out, shift_by, per_pair, groups, block_rows)
    send_grad = from_sequence(back_grad, shift_by, per_pair, groups, block_rows)
    home_out, home_grad = (
        lax.all_to_all(send_out, "fsdp", split_axis=1, concat_axis=1, tiled=True),
        lax.all_to_all(send_grad, "fsdp", split_axis=1, concat_axis=1, tiled=True),
    )
    out_tokens = jnp.einsum(
        "jgc,cgrf->jrf", routes, home_out, preferred_element_type=jnp.float32
    ).astype(jnp.bfloat16)
    grad_tokens_out = jnp.einsum(
        "jgc,cgrf->jrf", routes, home_grad, preferred_element_type=jnp.float32
    ).astype(jnp.bfloat16)
    partials = (
        query_part,
        key_part,
        value_part,
        output_part,
        gate_part,
        up_part,
        down_part,
        prenorm_part,
        midnorm_part,
    )
    owned = (
        lax.psum_scatter(
            partials[0].astype(jnp.bfloat16), "fsdp", scatter_dimension=0, tiled=True
        ).astype(jnp.float32),
        lax.psum_scatter(
            partials[1].astype(jnp.bfloat16), "fsdp", scatter_dimension=0, tiled=True
        ).astype(jnp.float32),
        lax.psum_scatter(
            partials[2].astype(jnp.bfloat16), "fsdp", scatter_dimension=0, tiled=True
        ).astype(jnp.float32),
        lax.psum_scatter(
            partials[3].astype(jnp.bfloat16), "fsdp", scatter_dimension=0, tiled=True
        ).astype(jnp.float32),
        lax.psum_scatter(
            partials[4].astype(jnp.bfloat16), "fsdp", scatter_dimension=0, tiled=True
        ).astype(jnp.float32),
        lax.psum_scatter(
            partials[5].astype(jnp.bfloat16), "fsdp", scatter_dimension=0, tiled=True
        ).astype(jnp.float32),
        lax.psum_scatter(
            partials[6].astype(jnp.bfloat16), "fsdp", scatter_dimension=0, tiled=True
        ).astype(jnp.float32),
        lax.psum_scatter(
            partials[7].astype(jnp.bfloat16), "fsdp", scatter_dimension=0, tiled=True
        ).astype(jnp.float32),
        lax.psum_scatter(
            partials[8].astype(jnp.bfloat16), "fsdp", scatter_dimension=0, tiled=True
        ).astype(jnp.float32),
    )
    totals = (
        lax.psum(owned[0].astype(jnp.bfloat16), "seq").astype(jnp.float32),
        lax.psum(owned[1].astype(jnp.bfloat16), "seq").astype(jnp.float32),
        lax.psum(owned[2].astype(jnp.bfloat16), "seq").astype(jnp.float32),
        lax.psum(owned[3].astype(jnp.bfloat16), "seq").astype(jnp.float32),
        lax.psum(owned[4].astype(jnp.bfloat16), "seq").astype(jnp.float32),
        lax.psum(owned[5].astype(jnp.bfloat16), "seq").astype(jnp.float32),
        lax.psum(owned[6].astype(jnp.bfloat16), "seq").astype(jnp.float32),
        lax.psum(owned[7].astype(jnp.bfloat16), "seq").astype(jnp.float32),
        lax.psum(owned[8].astype(jnp.bfloat16), "seq").astype(jnp.float32),
    )
    return (
        out_tokens,
        grad_tokens_out,
        totals[0],
        totals[1],
        totals[2],
        totals[3],
        totals[4],
        totals[5],
        totals[6],
        totals[7],
        totals[8],
    )


def solution(mesh):
    return jax.shard_map(
        body,
        mesh=mesh,
        in_specs=(
            P(None, "fsdp", "seq"),
            P(None, "fsdp", "seq"),
            P("fsdp", None),
            P("fsdp", None),
            P("fsdp", None),
            P("fsdp", None),
            P("fsdp", None),
            P("fsdp", None),
            P("fsdp", None),
            P("fsdp"),
            P("fsdp"),
            P(),
            P(),
        ),
        out_specs=(
            P(None, "fsdp", "seq"),
            P(None, "fsdp", "seq"),
            P("fsdp", None),
            P("fsdp", None),
            P("fsdp", None),
            P("fsdp", None),
            P("fsdp", None),
            P("fsdp", None),
            P("fsdp", None),
            P("fsdp"),
            P("fsdp"),
        ),
        check_vma=False,
    )
```

profile of v0, /device:TPU:0, one launch (start us, length us, event | category | flops | bytes accessed | tf_op | source)
XLA Modules:
  0.0 4951.0 jit_solution(15295774710404185649)
XLA Ops:
  25.1 45.0 all-gather
  122.3 120.1 %all-gather.10.cloned.1.call-done = bf16[2048,2048]{1,0:T(8,128)(2,1)} async-done(((bf16[256,2048]{1,0:T(8,128)(2,1)}), bf16[2048,2048]{1,0:T(8,128)(2,1)}) %all-gather.10.cloned.1.call-update) | async-done | bytes 8388624 | tf_op jit(solution)/shard_map/all_gather | solution.py:151
  278.9 37.2 all-gather.14.cloned.1.call-done
  349.5 21.0 while.28
  378.1 18.4 all-gather.1
  404.1 37.4 all-gather.16.cloned.1.call-done
  449.3 629.5 %all-gather.18.cloned.1.call-done = bf16[2048,8192]{1,0:T(8,128)(2,1)} async-done(((bf16[256,8192]{1,0:T(8,128)(2,1)}), bf16[2048,8192]{1,0:T(8,128)(2,1)}) %all-gather.18.cloned.1.call-update) | async-done | bytes 33554448 | tf_op jit(solution)/shard_map/all_gather | solution.py:155
  1078.8 18.6 fusion.122
  1097.4 620.5 %all-gather.20.cloned.1.call-done = bf16[2048,8192]{1,0:T(8,128)(2,1)} async-done(((bf16[256,8192]{1,0:T(8,128)(2,1)}), bf16[2048,8192]{1,0:T(8,128)(2,1)}) %all-gather.20.cloned.1.call-update) | async-done | bytes 33554448 | tf_op jit(solution)/shard_map/all_gather | solution.py:156
  1717.9 19.1 fusion.123
  1737.0 620.1 %all-gather.22.cloned.1.call-done = bf16[8192,2048]{1,0:T(8,128)(2,1)} async-done(((bf16[1024,2048]{1,0:T(8,128)(2,1)}), bf16[8192,2048]{1,0:T(8,128)(2,1)}) %all-gather.22.cloned.1.call-update) | async-done | bytes 33554448 | tf_op jit(solution)/shard_map/all_gather | solution.py:157
  2357.2 23.4 multiply_convert_fusion
  2442.6 40.6 while.29
  2612.0 69.9 %reduce-scatter.12.cloned.1.call-done = bf16[256,1024]{1,0:T(8,128)(2,1)} async-done(((bf16[2048,1024]{1,0:T(8,128)(2,1)}), bf16[256,1024]{1,0:T(8,128)(2,1)}) %reduce-scatter.12.cloned.1.call-update) | async-done | bytes 524304 | tf_op jit(solution)/shard_map/reduce_scatter | solution.py:391
  2681.9 152.8 %reduce-scatter.14.cloned.1.call-done = bf16[256,2048]{1,0:T(8,128)(2,1)} async-done(((bf16[2048,2048]{1,0:T(8,128)(2,1)}), bf16[256,2048]{1,0:T(8,128)(2,1)}) %reduce-scatter.14.cloned.1.call-update) | async-done | bytes 1048592 | tf_op jit(solution)/shard_map/reduce_scatter | solution.py:394
  2834.7 152.7 %reduce-scatter.8.cloned.1.call-done = bf16[256,2048]{1,0:T(8,128)(2,1)} async-done(((bf16[2048,2048]{1,0:T(8,128)(2,1)}), bf16[256,2048]{1,0:T(8,128)(2,1)}) %reduce-scatter.8.cloned.1.call-update) | async-done | bytes 1048592 | tf_op jit(solution)/shard_map/reduce_scatter | solution.py:385
  2987.4 545.9 %reduce-scatter.16.cloned.1.call-done = bf16[256,8192]{1,0:T(8,128)(2,1)} async-done(((bf16[2048,8192]{1,0:T(8,128)(2,1)}), bf16[256,8192]{1,0:T(8,128)(2,1)}) %reduce-scatter.16.cloned.1.call-update) | async-done | bytes 4194320 | tf_op jit(solution)/shard_map/reduce_scatter | solution.py:397
  3533.2 545.9 %reduce-scatter.18.cloned.1.call-done = bf16[256,8192]{1,0:T(8,128)(2,1)} async-done(((bf16[2048,8192]{1,0:T(8,128)(2,1)}), bf16[256,8192]{1,0:T(8,128)(2,1)}) %reduce-scatter.18.cloned.1.call-update) | async-done | bytes 4194320 | tf_op jit(solution)/shard_map/reduce_scatter | solution.py:400
  4079.1 545.7 %reduce-scatter.20.cloned.1.call-done = bf16[1024,2048]{1,0:T(8,128)(2,1)} async-done(((bf16[8192,2048]{1,0:T(8,128)(2,1)}), bf16[1024,2048]{1,0:T(8,128)(2,1)}) %reduce-scatter.20.cloned.1.call-update) | async-done | bytes 4194320 | tf_op jit(solution)/shard_map/reduce_scatter | solution.py:403
  4626.4 17.7 fusion.77
  4679.9 24.6 all-to-all-done.14
  4709.6 24.4 all-to-all-done.7
  4738.9 31.7 all-reduce.2
  4782.7 140.7 %all-reduce.7.cloned.1.call-done = (bf16[256,2048]{1,0:T(8,128)(2,1)}, bf16[256,1024]{1,0:T(8,128)(2,1)}, bf16[256,1024]{1,0:T(8,128)(2,1)}, bf16[256,2048]{1,0:...) async-done(((bf16[256,2048]{1,0:T(8,128)(2,1)}, bf16[256,1024]{1,0:T(8,128)(2,1)}, bf16[256,1024]{1,0:T(8,128)(2,1)}, ...) | async-done | bytes 15728656 | tf_op jit(solution)/shard_map/psum | solution.py:414
  (352 shorter events, 483.8 us)
Async XLA Ops:
  7.2 104.2 %all-gather.12.cloned.1.call-start = ((), (), s32[]{:S(2)}) async-start(), calls=%async_computation.24 | async-start | bytes 4718592 | tf_op jit(solution)/shard_map/all_gather | solution.py:152
  7.9 234.4 %all-gather.10.cloned.1.call-start = ((), (), s32[]{:S(2)}) async-start(), calls=%async_computation.23 | async-start | bytes 9437184 | tf_op jit(solution)/shard_map/all_gather | solution.py:151
  8.7 307.4 %all-gather.14.cloned.1.call-start = ((), (), s32[]{:S(2)}) async-start(), calls=%async_computation.25 | async-start | bytes 4718592 | tf_op jit(solution)/shard_map/all_gather | solution.py:153
  9.4 432.1 %all-gather.16.cloned.1.call-start = ((), (), s32[]{:S(2)}) async-start(), calls=%async_computation.26 | async-start | bytes 9437184 | tf_op jit(solution)/shard_map/all_gather | solution.py:154
  10.0 1068.8 %all-gather.18.cloned.1.call-start = ((), (), s32[]{:S(2)}) async-start(), calls=%async_computation.27 | async-start | bytes 37748736 | tf_op jit(solution)/shard_map/all_gather | solution.py:155
  10.6 1707.3 %all-gather.20.cloned.1.call-start = ((), (), s32[]{:S(2)}) async-start(), calls=%async_computation.28 | async-start | bytes 37748736 | tf_op jit(solution)/shard_map/all_gather | solution.py:156
  11.2 2346.0 %all-gather.22.cloned.1.call-start = ((), (), s32[]{:S(2)}) async-start(), calls=%async_computation.29 | async-start | bytes 37748736 | tf_op jit(solution)/shard_map/all_gather | solution.py:157
  15.2 54.9 %all-to-all-start = ((bf16[1,8,128,512]{3,2,0,1:T(8,128)(2,1)}), bf16[1,8,128,512]{3,2,0,1:T(8,128)(2,1)S(1)}, u32[]{:S(2)}, u32[]{:S(2)}) async-start(bf16[1,8,128,512]{3,2,0,1:T(8,128)(2,1)} %copy.149), calls=%async_computation | async-start | bytes 2097152 | tf_op jit(solution)/shard_map/all_to_all | solution.py:127
  89.5 172.2 %all-to-all-start.8 = ((bf16[1,8,128,512]{3,2,0,1:T(8,128)(2,1)}), bf16[1,8,128,512]{3,2,0,1:T(8,128)(2,1)S(1)}, u32[]{:S(2)}, u32[]{:S(2)}) async-start(bf16[1,8,128,512]{3,2,0,1:T(8,128)(2,1)} %copy.170), calls=%async_computation.8 | async-start | bytes 2097152 | tf_op jit(solution)/shard_map/all_to_all | solution.py:128
  274.0 46.5 all-to-all-start.2
  344.2 29.6 all-to-all-start.9
  373.8 25.8 all-to-all-start.5
  2426.1 185.9 %reduce-scatter.10.cloned.1.call-start = ((), (), s32[]{:S(2)}) async-start(), calls=%async_computation.31 | async-start | bytes 4718592 | tf_op jit(solution)/shard_map/reduce_scatter | solution.py:388
  2503.0 178.9 %reduce-scatter.12.cloned.1.call-start = ((), (), s32[]{:S(2)}) async-start(), calls=%async_computation.32 | async-start | bytes 4718592 | tf_op jit(solution)/shard_map/reduce_scatter | solution.py:391
  2521.8 312.9 %reduce-scatter.14.cloned.1.call-start = ((), (), s32[]{:S(2)}) async-start(), calls=%async_computation.33 | async-start | bytes 9437184 | tf_op jit(solution)/shard_map/reduce_scatter | solution.py:394
  2530.4 457.0 %reduce-scatter.8.cloned.1.call-start = ((), (), s32[]{:S(2)}) async-start(), calls=%async_computation.30 | async-start | bytes 9437184 | tf_op jit(solution)/shard_map/reduce_scatter | solution.py:385
  2560.3 972.9 %reduce-scatter.16.cloned.1.call-start = ((), (), s32[]{:S(2)}) async-start(), calls=%async_computation.34 | async-start | bytes 37748736 | tf_op jit(solution)/shard_map/reduce_scatter | solution.py:397
  2577.8 1501.3 %reduce-scatter.18.cloned.1.call-start = ((), (), s32[]{:S(2)}) async-start(), calls=%async_computation.35 | async-start | bytes 37748736 | tf_op jit(solution)/shard_map/reduce_scatter | solution.py:400
  2594.2 2030.6 %reduce-scatter.20.cloned.1.call-start = ((), (), s32[]{:S(2)}) async-start(), calls=%async_computation.36 | async-start | bytes 37748736 | tf_op jit(solution)/shard_map/reduce_scatter | solution.py:403
  2611.9 2311.4 %all-reduce.7.cloned.1.call-start = ((), (), s32[]{:S(2)}) async-start(), calls=%async_computation.37 | async-start | bytes 31457280 | tf_op jit(solution)/shard_map/psum | solution.py:414
  4645.2 29.7 all-to-all-start.6
  4674.9 29.6 all-to-all-start.14
  4704.5 29.5 all-to-all-start.7
  4734.0 46.6 all-to-all-start.15
  (73 other events, 3839.0 us)
Sparse Core Ops, SparseCore 0:
  10.2 101.2 all-gather.11
  113.5 128.7 all-gather.9
  244.5 71.5 all-gather.13
  318.1 123.3 all-gather.15
  442.8 635.8 all-gather.17
  1080.2 637.6 all-gather.19
  1719.4 637.6 all-gather.21
  2503.1 86.9 reduce-scatter.9
  2594.2 87.6 reduce-scatter.11
  2686.0 148.6 reduce-scatter.13
  2839.3 147.9 reduce-scatter.7
  2991.0 542.1 reduce-scatter.15
  3537.0 542.0 reduce-scatter.17
  4082.7 542.0 reduce-scatter.19
  4627.9 295.3 all-reduce.6
where the time goes:
time: 4960 us; the launch traced here: 4950 us
  waiting for transfers between devices  4330 us (87%)
  matrix products  255 us (5%)
  blocking collectives  141 us (3%)
  local copies, waits for them, and re-layouts  71.5 us (1%)
  starting transfers between devices  68 us (1%)
  other arithmetic  58.8 us (1%)
    all_gather x1, waiting for transfers between devices, body(): lax.all_gather(weight_set[4], 'fsdp', axis=0, tiled=True)  630 us
    all_gather x1, waiting for transfers between devices, body(): lax.all_gather(weight_set[5], 'fsdp', axis=0, tiled=True)  621 us
    all_gather x1, waiting for transfers between devices, body(): lax.all_gather(weight_set[6], 'fsdp', axis=0, tiled=True)  620 us
    reduce_scatter x1, waiting for transfers between devices, body(): lax.psum_scatter(partials[5].astype(jnp.bfloat16), 'fsdp', scatter_dimens...  546 us
    reduce_scatter x1, waiting for transfers between devices, body(): lax.psum_scatter(partials[4].astype(jnp.bfloat16), 'fsdp', scatter_dimens...  546 us
    reduce_scatter x1, waiting for transfers between devices, body(): lax.psum_scatter(partials[6].astype(jnp.bfloat16), 'fsdp', scatter_dimens...  546 us
    reduce_scatter x1, waiting for transfers between devices, body(): lax.psum_scatter(partials[3].astype(jnp.bfloat16), 'fsdp', scatter_dimens...  153 us
    reduce_scatter x1, waiting for transfers between devices, body(): lax.psum_scatter(partials[0].astype(jnp.bfloat16), 'fsdp', scatter_dimens...  153 us
  transfers between devices with their start and end apart: 28, of which 21 were waited for; matrix products, arithmetic and copies ran while one was open for 5% of the time, Pallas kernels for 0%

commit v1 on v0

v1 whole, which is shorter than its diff:
```python
import math

import jax
import jax.numpy as jnp
from jax import lax
from jax.sharding import Mesh
from jax.sharding import PartitionSpec as P

QUERY_HEADS = 8
KEY_VALUE_HEADS = 4
HEAD_SIZE = 256

EPS_NORM = 1e-06
ROPE_BASE = 1000042.0
MASK_FILL = -1e30
AXES = ("z", "y", "x", "c")
F32 = jnp.float32
BF16 = jnp.bfloat16


def dot(a, b, dims):
    return lax.dot_general(a, b, (dims, ((), ())), preferred_element_type=F32)


def mm(a, b):
    return dot(a, b, ((1,), (0,)))


def mm_nt(a, b):
    return dot(a, b, ((1,), (1,)))


def mm_tn(a, b):
    return dot(a, b, ((0,), (0,)))


class Links:
    def __init__(self, planes):
        self.planes = planes

        def pairs(move):
            out = []
            for z in range(planes):
                for y in range(2):
                    for x in range(2):
                        for c in range(2):
                            a, b, d, e = move(z, y, x, c)
                            out.append((((z * 2 + y) * 2 + x) * 2 + c, ((a * 2 + b) * 2 + d) * 2 + e))
            return out

        self.px = pairs(lambda z, y, x, c: (z, y, 1 - x, c))
        self.py = pairs(lambda z, y, x, c: (z, 1 - y, x, c))
        self.pc = pairs(lambda z, y, x, c: (z, y, x, 1 - c))
        self.pz = pairs(lambda z, y, x, c: ((z + 1) % planes, y, x, c))

    def x(self, a):
        return lax.ppermute(a, AXES, self.px)

    def y(self, a):
        return lax.ppermute(a, AXES, self.py)

    def c(self, a):
        return lax.ppermute(a, AXES, self.pc)

    def z(self, a):
        return lax.ppermute(a, AXES, self.pz)

    def gather_rows(self, a):
        n = a.shape[0]
        ax = self.x(a)
        ay = self.y(a)
        dx = self.x(ay[: n // 2])
        dy = self.y(ax[n // 2 :])
        return jnp.concatenate([a, ax, ay, dx, dy], axis=0)

    def scatter_rows(self, part):
        n, d = part.shape[0] // 4, part.shape[1]
        h = d // 2
        p = part.reshape(4, n, d)
        left, right = p[:, :, :h], p[:, :, h:]
        gl = self.x(jnp.stack([left[1], left[3]]).astype(BF16))
        gr = self.y(jnp.stack([right[2], right[3]]).astype(BF16))
        l_far = self.y((left[2] + gl[1]).astype(BF16))
        r_far = self.x((right[1] + gr[1]).astype(BF16))
        l_own = left[0] + gl[0] + l_far
        r_own = right[0] + gr[0] + r_far
        return jnp.concatenate([l_own, r_own], axis=1)

    def gather_planes(self, a):
        if self.planes > 4:
            return lax.all_gather(a, "z", axis=0, tiled=True)
        me = lax.axis_index("z")
        out = jnp.zeros((self.planes,) + a.shape, a.dtype)
        now = a
        for k in range(self.planes):
            if k:
                now = self.z(now)
            out = lax.dynamic_update_slice(
                out, now[None], (lax.rem(me - k + self.planes, self.planes), 0, 0)
            )
        return out.reshape(self.planes * a.shape[0], a.shape[1])


def pair(bit, own, other):
    return jnp.stack([jnp.where(bit == 0, own, other), jnp.where(bit == 0, other, own)])


def rope_tables(positions):
    half_dim = HEAD_SIZE // 2
    frequency = jnp.exp(jnp.arange(half_dim, dtype=F32) * (-2.0 * math.log(ROPE_BASE) / HEAD_SIZE))
    angles = positions.astype(F32)[:, None] * frequency[None, :]
    return jnp.cos(angles), jnp.sin(angles)


def rotate(v, cos_t, sin_t):
    h = HEAD_SIZE // 2
    a, b = v[:, :h], v[:, h:]
    return jnp.concatenate([a * cos_t - b * sin_t, b * cos_t + a * sin_t], axis=-1).astype(BF16)


def unrotate(v, cos_t, sin_t):
    h = HEAD_SIZE // 2
    a, b = v[:, :h], v[:, h:]
    return jnp.concatenate([a * cos_t + b * sin_t, b * cos_t - a * sin_t], axis=-1).astype(BF16)


def norm_factor(hidden):
    return lax.rsqrt(jnp.mean(hidden * hidden, axis=-1, keepdims=True) + EPS_NORM)


def norm_backward(upstream, hidden, factor, gain_vec):
    scaled = upstream * gain_vec
    gain_part = jnp.sum(upstream * hidden * factor, axis=0)
    inner_sum = jnp.mean(scaled * hidden, axis=-1, keepdims=True)
    return (factor * scaled - hidden * (factor * factor * factor) * inner_sum, gain_part)


def make_body(planes):
    links = Links(planes)

    def body(
        tokens,
        cotangent,
        query_weight,
        key_matrix,
        value_matrix,
        output_weight,
        gate_weight,
        up_weight,
        down_weight,
        prenorm_gain,
        midnorm_gain,
        seq_len,
        stream_order,
    ):
        groups = 2 * planes
        z_me = lax.axis_index("z")
        y_me = lax.axis_index("y")
        x_me = lax.axis_index("x")
        c_me = lax.axis_index("c")
        slots, blk, quarter = tokens.shape
        width = 4 * quarter
        rank = 4 * y_me + 2 * x_me + c_me
        head = 2 * y_me + x_me
        shard = query_weight.shape[0]
        ff = gate_weight.shape[1]
        piece = ff // groups // 4

        nblk = (seq_len + blk - 1) // blk
        member = (stream_order[:, None] == jnp.arange(groups, dtype=jnp.int32)[None, :]).astype(
            jnp.int32
        )
        ordered = jnp.sum(member * nblk[None, :], axis=1)
        firsts = jnp.cumsum(ordered) - ordered
        seq_start = jnp.sum(member * firsts[:, None], axis=0)
        group_me = 2 * z_me + y_me
        offset = lax.rem(group_me - lax.rem(seq_start, groups) + groups, groups)
        has = offset < nblk
        slot_of = jnp.where(has, (seq_start + offset) // groups, -1)
        routes = (jnp.arange(slots, dtype=jnp.int32)[:, None] == slot_of[None, :]).astype(BF16)

        mine = 2 * z_me + c_me
        picked = jnp.arange(groups, dtype=jnp.int32) == mine
        my_start = jnp.sum(jnp.where(picked, seq_start, 0))
        my_len = jnp.sum(jnp.where(picked, seq_len, 0))

        def block_places(y):
            first = lax.rem(y + my_start, 2)
            plane = lax.rem((my_start + first) // 2, planes)
            k = jnp.arange(4, dtype=jnp.int32)
            if planes == 4:
                k = lax.rem(k - plane + planes, planes)
            return first + 2 * k, plane

        places_own, plane_own = block_places(y_me)
        places_far, _ = block_places(1 - y_me)

        def row_positions(places, x):
            two = lax.dynamic_slice(places, (2 * x,), (2,))
            return (two[:, None] * blk + jnp.arange(blk, dtype=jnp.int32)[None, :]).reshape(-1)

        positions = row_positions(places_own, x_me)
        positions_all = jnp.concatenate(
            [
                positions,
                row_positions(places_own, 1 - x_me),
                row_positions(places_far, x_me),
                row_positions(places_far, 1 - x_me),
            ]
        )
        valid = (positions < my_len).astype(F32)[:, None]
        seq_rows = 8 * blk
        rows = 2 * blk

        def route_in(stream):
            send = jnp.einsum("jg,jrf->grf", routes, stream, preferred_element_type=F32).astype(BF16)
            got = lax.all_to_all(send, ("z", "c"), split_axis=0, concat_axis=0, tiled=True)
            got = got.reshape(planes, 2, blk, quarter)
            if planes > 4:
                got = jnp.roll(got, -plane_own, axis=0)[:4]
            got = lax.all_to_all(got, "x", split_axis=0, concat_axis=1, tiled=True)
            return jnp.transpose(got, (0, 2, 1, 3)).reshape(rows, width)

        def route_out(out_rows):
            send = lax.all_to_all(
                out_rows.reshape(2, blk, width), "x", split_axis=2, concat_axis=0, tiled=True
            )
            send = jnp.transpose(send.reshape(4, blk, 2, quarter), (0, 2, 1, 3))
            if planes > 4:
                send = jnp.pad(send, ((0, planes - 4), (0, 0), (0, 0), (0, 0)))
                send = jnp.roll(send, plane_own, axis=0)
            send = send.reshape(groups, blk, quarter)
            got = lax.all_to_all(send, ("z", "c"), split_axis=0, concat_axis=0, tiled=True)
            return jnp.einsum("jg,grf->jrf", routes, got, preferred_element_type=F32).astype(BF16)

        def plane_rows(own_part, far_part):
            got = links.y(far_part)
            both = pair(y_me, own_part, got)
            return both.reshape(2 * own_part.shape[0], own_part.shape[1])

        def attn_columns(r):
            q = lax.dynamic_slice(query_weight, (0, r * HEAD_SIZE), (shard, HEAD_SIZE))
            j = r // 2
            k = lax.dynamic_slice(key_matrix, (0, j * HEAD_SIZE), (shard, HEAD_SIZE))
            v = lax.dynamic_slice(value_matrix, (0, j * HEAD_SIZE), (shard, HEAD_SIZE))
            return jnp.concatenate([q, jnp.where(c_me == 0, k, v)], axis=1)

        def out_columns(r):
            at = lax.rem(r, 2) * (width // 2) + (r // 2) * (width // 8)
            return lax.dynamic_slice(output_weight, (0, at), (output_weight.shape[0], width // 8))

        def ff_columns(w, r):
            return jnp.concatenate(
                [
                    lax.dynamic_slice(w, (0, p * 8 * piece + r * piece), (shard, piece))
                    for p in range(planes)
                ],
                axis=1,
            )

        far = rank + 4 - 8 * y_me
        gain_rows = jnp.stack([prenorm_gain, midnorm_gain])
        gains = lax.all_gather(gain_rows, ("z", "y"), axis=1, tiled=True).astype(F32)
        gain_pre, gain_mid = gains[0], gains[1]

        rows_in = route_in(tokens)
        w_qkv = links.gather_planes(plane_rows(attn_columns(rank), attn_columns(far)))
        w_qkv_far = links.c(w_qkv)
        w_o_cols = links.gather_planes(plane_rows(out_columns(rank), out_columns(far)))
        w_o = lax.all_to_all(w_o_cols, ("y", "x"), split_axis=0, concat_axis=1, tiled=True)
        w_o_far = links.c(w_o)
        rows_cot = route_in(cotangent)
        w_gate = links.gather_planes(plane_rows(ff_columns(gate_weight, rank), ff_columns(gate_weight, far)))
        w_gate_far = links.c(w_gate)
        w_up = links.gather_planes(plane_rows(ff_columns(up_weight, rank), ff_columns(up_weight, far)))
        w_up_far = links.c(w_up)
        w_down = links.gather_planes(
            lax.dynamic_slice(down_weight, ((2 * x_me + c_me) * piece, 0), (piece, width))
        )
        w_down_far = links.c(w_down)

        hidden_zero = rows_in.astype(F32) * valid
        factor_pre = norm_factor(hidden_zero)
        normed = links.gather_rows((hidden_zero * factor_pre * gain_pre).astype(BF16))
        cos_t, sin_t = rope_tables(positions_all)
        pre_own = mm(normed, w_qkv)
        pre_far = mm(normed, w_qkv_far)
        first = c_me == 0
        even = jnp.where(first, pre_own, pre_far)
        odd = jnp.where(first, pre_far, pre_own)
        queries = (
            rotate(even[:, :HEAD_SIZE], cos_t, sin_t),
            rotate(odd[:, :HEAD_SIZE], cos_t, sin_t),
        )
        keys = rotate(even[:, HEAD_SIZE:], cos_t, sin_t)
        values = odd[:, HEAD_SIZE:].astype(BF16)
        factor = 1.0 / math.sqrt(HEAD_SIZE)
        allowed = (positions_all[None, :] <= positions_all[:, None]) & (
            positions_all[None, :] < my_len
        )

        def head_forward(q):
            scores = jnp.where(allowed, mm_nt(q, keys) * factor, MASK_FILL)
            top = jnp.max(scores, axis=-1, keepdims=True)
            exponent = jnp.exp(scores - top)
            total = jnp.sum(exponent, axis=-1, keepdims=True)
            probs = (exponent / total).astype(BF16)
            return mm(probs, values).astype(BF16), top + jnp.log(total)

        heads = [head_forward(q) for q in queries]
        mixed = jnp.concatenate([heads[0][0], heads[1][0]], axis=1)

        out_own = mm(mixed, w_o)
        out_far = mm(mixed, w_o_far)
        attn_part = jnp.concatenate(
            [jnp.where(first, out_own, out_far), jnp.where(first, out_far, out_own)], axis=1
        ).astype(BF16)
        hidden_one = hidden_zero + links.scatter_rows(attn_part)
        factor_mid = norm_factor(hidden_one)
        normed_two = links.gather_rows((hidden_one * factor_mid * gain_mid).astype(BF16))

        upstream = rows_cot.astype(F32) * valid
        down_in = links.gather_rows(upstream.astype(BF16))

        def ff_half(wg, wu, wd):
            gate_pre = mm(normed_two, wg)
            up_pre = mm(normed_two, wu)
            sig = jax.nn.sigmoid(gate_pre)
            gate_act = gate_pre * sig
            activated = (gate_act * up_pre).astype(BF16)
            act_grad = mm_nt(down_in, wd)
            gate_in = (act_grad * up_pre * sig * (1.0 + gate_pre * (1.0 - sig))).astype(BF16)
            up_in = (act_grad * gate_act).astype(BF16)
            return activated, gate_in, up_in

        act, gate_in, up_in = ff_half(w_gate, w_up, w_down)
        act_far, gate_in_far, up_in_far = ff_half(w_gate_far, w_up_far, w_down_far)
        dn_part = (
            mm_nt(gate_in, w_gate)
            + mm_nt(up_in, w_up)
            + mm_nt(gate_in_far, w_gate_far)
            + mm_nt(up_in_far, w_up_far)
        ).astype(BF16)
        normed_two_grad = links.scatter_rows(dn_part)
        ff_part = (mm(act, w_down) + mm(act_far, w_down_far)).astype(BF16)

        def both_cores(own_left, far_left, own_right, far_right):
            got = links.c(mm_tn(far_left, far_right).astype(BF16))
            return (mm_tn(own_left, own_right) + got).astype(BF16)

        def over_planes(g):
            return lax.psum_scatter(g, "z", scatter_dimension=0, tiled=True)

        g_down = over_planes(both_cores(act, act_far, down_in, down_in))
        g_gate = over_planes(both_cores(normed_two, normed_two, gate_in, gate_in_far))
        g_up = over_planes(both_cores(normed_two, normed_two, up_in, up_in_far))

        ff_out = links.scatter_rows(ff_part)
        block_rows = ((hidden_one + ff_out) * valid).astype(BF16)
        out_tokens = route_out(block_rows)

        mid_upstream, midnorm_part = norm_backward(normed_two_grad, hidden_one, factor_mid, gain_mid)
        hidden_one_grad = upstream + mid_upstream
        attn_in = links.gather_rows(hidden_one_grad.astype(BF16))
        half = width // 2
        attn_own = jnp.where(first, attn_in[:, :half], attn_in[:, half:])
        attn_far = jnp.where(first, attn_in[:, half:], attn_in[:, :half])
        mixed_grad = (mm_nt(attn_own, w_o) + mm_nt(attn_far, w_o_far)).astype(BF16)
        g_out = both_cores(mixed, mixed, attn_own, attn_far)

        dk = 0.0
        dv = 0.0
        dq = []
        for i in range(2):
            dmix = mixed_grad[:, i * HEAD_SIZE : (i + 1) * HEAD_SIZE]
            scores = jnp.where(allowed, mm_nt(queries[i], keys) * factor, MASK_FILL)
            probs = jnp.exp(scores - heads[i][1])
            dv = dv + mm_tn(probs.astype(BF16), dmix)
            prob_grad = mm_nt(dmix, values)
            inner = jnp.sum(prob_grad * probs, axis=-1, keepdims=True)
            score_grad = (probs * (prob_grad - inner)).astype(BF16) * factor
            dq.append(mm(score_grad, keys).astype(BF16))
            dk = dk + mm_tn(score_grad, queries[i])
        dk = dk.astype(BF16)
        dv = dv.astype(BF16)
        dq = [unrotate(t.astype(F32), cos_t, sin_t) for t in dq]
        dk = unrotate(dk.astype(F32), cos_t, sin_t)
        grad_even = jnp.concatenate([dq[0], dk], axis=1)
        grad_odd = jnp.concatenate([dq[1], dv], axis=1)
        d_own = jnp.where(first, grad_even, grad_odd)
        d_far = jnp.where(first, grad_odd, grad_even)
        g_qkv = both_cores(normed, normed, d_own, d_far)
        g_o_cols = lax.all_to_all(g_out, ("y", "x"), split_axis=1, concat_axis=0, tiled=True)
        g_attn = over_planes(jnp.concatenate([g_qkv, g_o_cols], axis=1))

        normed_grad = links.scatter_rows((mm_nt(d_own, w_qkv) + mm_nt(d_far, w_qkv_far)).astype(BF16))
        pre_upstream, prenorm_part = norm_backward(normed_grad, hidden_zero, factor_pre, gain_pre)
        token_rows = ((hidden_one_grad + pre_upstream) * valid).astype(BF16)
        grad_tokens = route_out(token_rows)

        def by_rank(g):
            n = g.shape[1]
            two = g.reshape(2, shard, n)
            own = jnp.where(y_me == 0, two[0], two[1])
            other = jnp.where(y_me == 0, two[1], two[0])
            got = pair(y_me, own, links.y(other))
            got = pair(x_me, got, links.x(got))
            got = pair(c_me, got, links.c(got))
            return jnp.transpose(got, (2, 1, 0, 3, 4)).reshape(8, shard, n)

        def ff_gradient(g):
            t = by_rank(g).reshape(8, shard, planes, piece)
            return jnp.transpose(t, (1, 2, 0, 3)).reshape(shard, ff).astype(F32)

        gate_gradient = ff_gradient(g_gate)
        up_gradient = ff_gradient(g_up)
        down_all = pair(x_me, g_down, links.x(g_down))
        down_all = pair(c_me, down_all, links.c(down_all))
        down_gradient = (
            jnp.transpose(down_all, (1, 0, 2, 3)).reshape(4 * piece, width).astype(F32)
        )
        t = by_rank(g_attn)

        def columns(a):
            return jnp.transpose(a, (1, 0, 2)).reshape(shard, -1).astype(F32)

        query_gradient = columns(t[:, :, :HEAD_SIZE])
        key_gradient = columns(t[0::2, :, HEAD_SIZE : 2 * HEAD_SIZE])
        value_gradient = columns(t[1::2, :, HEAD_SIZE : 2 * HEAD_SIZE])
        out_t = t[:, :, 2 * HEAD_SIZE :].reshape(4, 2, shard, width // 8)
        output_gradient = jnp.transpose(out_t, (2, 1, 0, 3)).reshape(shard, width).astype(F32)

        norm_parts = lax.psum(jnp.stack([prenorm_part, midnorm_part]), AXES)
        norm_own = lax.dynamic_slice(
            norm_parts, (0, group_me * prenorm_gain.shape[0]), (2, prenorm_gain.shape[0])
        )
        return (
            out_tokens,
            grad_tokens,
            query_gradient,
            key_gradient,
            value_gradient,
            output_gradient,
            gate_gradient,
            up_gradient,
            down_gradient,
            norm_own[0],
            norm_own[1],
        )

    return body


def solution(mesh):
    planes = mesh.shape["fsdp"] // 2
    grid = Mesh(mesh.devices.reshape(planes, 2, 2, 2), AXES)
    rows = ("z", "y")
    stream = P(None, rows, ("x", "c"))
    weight = P(rows, None)
    gain = P(rows)
    return jax.shard_map(
        make_body(planes),
        mesh=grid,
        in_specs=(stream, stream) + (weight,) * 7 + (gain, gain, P(), P()),
        out_specs=(stream, stream) + (weight,) * 7 + (gain, gain),
        check_vma=False,
    )
```

time: 4960 us -> 1220 us (0.25)
  waiting for transfers between devices: 4330 us -> 377 us
  local copies, waits for them, and re-layouts: 71.5 us -> 221 us
  other arithmetic: 58.8 us -> 155 us
  matrix products: 255 us -> 204 us
    all_gather x7 -> x0, waiting for transfers between devices: 2080 us -> none  [the longest x1 630 us: body(): lax.all_gather(weight_set[4], 'fsdp', axis=0, tiled=True)]
    reduce_scatter x7 -> x4, waiting for transfers between devices: 2010 us -> 0.03 us  [over_planes(): return lax.psum_scatter(g, 'z', scatter_dimension=0, tiled=True)]
    ppermute x0 -> x72, waiting for transfers between devices: none -> 287 us  [the longest x20 139 us: x(): return lax.ppermute(a, AXES, self.px)]
    psum x1 -> x0, waiting for transfers between devices: 141 us -> none  [body(): lax.psum(owned[0].astype(jnp.bfloat16), 'seq').astype(jnp.float32)]
    ppermute x0 -> x72, starting transfers between devices: none -> 76.5 us  [the longest x20 26.4 us: x(): return lax.ppermute(a, AXES, self.px)]
    convert_element_type x8 -> x20, local copies, waits for them, and re-layouts: 8.45 us -> 79.2 us  [the longest x4 32.6 us: ff_gradient(): return jnp.transpose(t, (1, 2, 0, 3)).reshape(shard, ff).astype(F32)]
    psum x1, blocking collectives: 6.72 us -> 69.5 us  [body(): norm_parts = lax.psum(jnp.stack([prenorm_part, midnorm_part]), AXES)]
    dot_general x39 -> x46, matrix products: 255 us -> 204 us  [the longest x42 201 us: dot(): return lax.dot_general(a, b, (dims, ((), ())), preferred_element_type=F32)]
  transfers between devices with their start and end apart: 28 -> 85, of which waited for: 21 -> 33; matrix products, arithmetic and copies ran while one was open for 5% -> 38% of each run, Pallas kernels for 0% -> 0%
where the time goes in v1:
time: 1220 us; the launch traced here: 1210 us
  waiting for transfers between devices  377 us (31%)
  local copies, waits for them, and re-layouts  221 us (18%)
  matrix products  204 us (17%)
  other arithmetic  155 us (13%)
  starting transfers between devices  117 us (10%)
  blocking collectives  113 us (9%)
  between operations  18.8 us (2%)
    dot_general x42, matrix products, dot(): return lax.dot_general(a, b, (dims, ((), ())), preferred_element_type=F32)  201 us
    ppermute x20, waiting for transfers between devices, x(): return lax.ppermute(a, AXES, self.px)  139 us
    ppermute x23, waiting for transfers between devices, y(): return lax.ppermute(a, AXES, self.py)  88.8 us
    psum x1, blocking collectives, body(): norm_parts = lax.psum(jnp.stack([prenorm_part, midnorm_part]), AXES)  69.5 us
    unnamed x274, local copies, waits for them, and re-layouts  50.9 us
    all_to_all x2, waiting for transfers between devices, route_out(): lax.all_to_all(send, ('z', 'c'), split_axis=0, concat_axis=0, tiled=True)  46.9 us
    ppermute x15, waiting for transfers between devices, z(): return lax.ppermute(a, AXES, self.pz)  45.8 us
    dynamic_update_slice x20, local copies, waits for them, and re-layouts, gather_planes(): lax.dynamic_update_slice(out, now[None], (lax.rem(me - k + self.planes, s...  38.3 us
  transfers between devices with their start and end apart: 85, of which 33 were waited for; matrix products, arithmetic and copies ran while one was open for 38% of the time, Pallas kernels for 0%

profile of v1, /device:TPU:0, one launch (start us, length us, event | category | flops | bytes accessed | tf_op | source)
XLA Modules:
  0.0 1206.3 jit_solution(13100703748445873209)
XLA Ops:
  48.1 26.3 %all_gather.3 = bf16[2,2048]{1,0:T(2,128)(2,1)S(1)} all-gather(bf16[2,256]{1,0:T(2,128)(2,1)S(1)} %pad_maximum_fusion.34), channel_id=1, replica_groups=mesh['z'=4,'y'=2,'x'=2,'c'=2] {'z','y'}, dimensions={1}, use_global_device_ids=true | all-gather | bytes 9216 | tf_op jit(solution)/shard_map/all_gather | solution.py:263
  121.8 43.9 %collective-permute-done.6 = bf16[512,512]{1,0:T(8,128)(2,1)} collective-permute-done((bf16[512,512]{1,0:T(8,128)(2,1)}, bf16[512,512]{1,0:T(8,128)(2,1)}, u32[]{:S(2)}, u32[]{:S(2)}) %collective-permute-start.6) | collective-permute-done | bytes 524320 | tf_op jit(solution)/shard_map/ppermute | solution.py:66
  197.1 14.6 %collective-permute-done.1 = bf16[256,2048]{1,0:T(8,128)(2,1)S(1)} collective-permute-done((bf16[256,2048]{1,0:T(8,128)(2,1)}, bf16[256,2048]{1,0:T(8,128)(2,1)S(1)}, u32[]{:S(2)}, u32[]{:S(2)}) %collective-permute-start.1) | collective-permute-done | bytes 1048608 | tf_op jit(solution)/shard_map/ppermute | solution.py:60
  214.2 32.8 %all-to-all-done.5 = bf16[8,128,512]{2,1,0:T(8,128)(2,1)} async-done(((bf16[8,128,512]{2,1,0:T(8,128)(2,1)}), bf16[8,128,512]{2,1,0:T(8,128)(2,1)}, u32[]{:S(2)}, u32[]{:S(2)}) %all-to-all-start.5) | async-done | bytes 1048608 | tf_op jit(solution)/shard_map/all_to_all | solution.py:217
  265.6 11.0 collective-permute-done.2
  380.2 14.7 %collective-permute-done.41 = bf16[256,2048]{1,0:T(8,128)(2,1)S(1)} collective-permute-done((bf16[256,2048]{1,0:T(8,128)(2,1)S(1)}, bf16[256,2048]{1,0:T(8,128)(2,1)S(1)}, u32[]{:S(2)}, u32[]{:S(2)}) %collective-permute-start.41) | collective-permute-done | bytes 1048608 | tf_op jit(solution)/shard_map/ppermute | solution.py:60
  396.1 20.1 %collective-permute-done.18 = bf16[256,2048]{1,0:T(8,128)(2,1)S(1)} collective-permute-done((bf16[256,2048]{1,0:T(8,128)(2,1)S(1)}, bf16[256,2048]{1,0:T(8,128)(2,1)S(1)}, u32[]{:S(2)}, u32[]{:S(2)}) %collective-permute-start.18) | collective-permute-done | bytes 1048608 | tf_op jit(solution)/shard_map/ppermute | solution.py:57
  428.2 9.8 fusion.169
  438.1 9.7 fusion.166
  447.8 10.8 multiply_convert_fusion.5
  458.6 10.5 fusion.170
  501.6 13.4 %add_convert_fusion.4 = bf16[1024,2048]{1,0:T(8,128)(2,1)} fusion(f32[1024,2048]{1,0:T(8,128)} %fusion.173, f32[1024,2048]{1,0:T(8,128)} %fusion.172, f32[1024,2048]{1,0:T(8,128)} %fusion.170, bf16[1024,1024]{1,0:T(8,128)(2,1)S(1)} %get-tuple-element.106, bf16[2048,1024]{1,0:T(8,128)(2,1)} %bitcast.56), kind=kOutput, calls=%fused_computation.7 | convolution fusion | flops 4303355904 | bytes 35651584 | tf_op jit(solution)/shard_map/dot_general | solution.py:22
  519.5 20.6 %collective-permute-done.44 = bf16[2,256,1024]{2,1,0:T(8,128)(2,1)S(1)} collective-permute-done((bf16[2,256,1024]{2,1,0:T(8,128)(2,1)S(1)}, bf16[2,256,1024]{2,1,0:T(8,128)(2,1)S(1)}, u32[]{:S(2)}, u32[]{:S(2)}) %collective-permute-start.44) | collective-permute-done | bytes 1048608 | tf_op jit(solution)/shard_map/ppermute | solution.py:57
  570.8 19.2 %collective-permute-done.49 = bf16[256,2048]{1,0:T(8,128)(2,1)S(1)} collective-permute-done((bf16[256,2048]{1,0:T(8,128)(2,1)S(1)}, bf16[256,2048]{1,0:T(8,128)(2,1)S(1)}, u32[]{:S(2)}, u32[]{:S(2)}) %collective-permute-start.49) | collective-permute-done | bytes 1048608 | tf_op jit(solution)/shard_map/ppermute | solution.py:60
  631.5 17.2 %all_to_all.109 = bf16[512,4,256]{0,2,1:T(8,128)(2,1)S(1)} all-to-all(bf16[512,4,256]{0,2,1:T(8,128)(2,1)S(1)} %bitcast.427), channel_id=1, replica_groups=mesh['z'=4,'y'=2,'x'=2,'c'=2] {'y','x'}, dimensions={1} | all-to-all | bytes 2097152 | tf_op jit(solution)/shard_map/all_to_all | solution.py:393
  760.3 20.8 %collective-permute-done.37 = bf16[256,1024]{1,0:T(8,128)(2,1)} collective-permute-done((bf16[256,1024]{1,0:T(8,128)(2,1)}, bf16[256,1024]{1,0:T(8,128)(2,1)}, u32[]{:S(2)}, u32[]{:S(2)}) %collective-permute-start.37) | collective-permute-done | bytes 524320 | tf_op jit(solution)/shard_map/ppermute | solution.py:60
  800.4 11.8 multiply_convert_fusion.8
  834.0 22.1 %fusion.23 = bf16[2,128,2048]{1,0,2:T(2,128)(2,1)} fusion(f32[2,128,4,512]{1,0,3,2:T(2,128)S(1)} %copy-done.18, f32[2,128,4,512]{1,0,3,2:T(2,128)S(1)} %copy-done.11, f32[2048]{0:T(1024)S(1)} %bitcast.446, f32[2048]{0:T(1024)S(1)} %bitcast.444, bf16[2,128,1024]{1,0,2:T(2,128)(2,1)} %copy.250, bf16[2,128,1024]{1,0,2:T(2,128)(2,1)} %copy.249, ...), kind=kLoop, calls=%fused_computation.91 | loop fusion | flops 12058624 | bytes 8412160 | tf_op jit(solution)/shard_map/convert_element_type | solution.py:398
  862.5 9.9 all-to-all-done.7
  879.8 46.9 %all-to-all-done.4 = bf16[8,128,512]{2,1,0:T(8,128)(2,1)S(1)} async-done(((bf16[8,128,512]{2,1,0:T(8,128)(2,1)}), bf16[8,128,512]{2,1,0:T(8,128)(2,1)S(1)}, u32[]{:S(2)}, u32[]{:S(2)}) %all-to-all-start.4) | async-done | bytes 1048608 | tf_op jit(solution)/shard_map/all_to_all | solution.py:233
  935.6 69.5 %psum.7 = f32[2,2048]{1,0:T(2,128)S(1)} all-reduce(f32[2,2048]{1,0:T(2,128)S(1)} %pad_maximum_fusion.33), channel_id=1, replica_groups=mesh['z'=4,'y'=2,'x'=2,'c'=2] {'z','y','x','c'}, use_global_device_ids=true, to_apply=%region_21.22 | all-reduce | flops 4096 | bytes 32768 | tf_op jit(solution)/shard_map/psum | solution.py:433
  1037.5 11.0 collective-permute-done.70
  1050.7 20.3 %collective-permute-done.63 = bf16[2,256,1024]{2,1,0:T(8,128)(2,1)S(1)} collective-permute-done((bf16[2,256,1024]{2,1,0:T(8,128)(2,1)S(1)}, bf16[2,256,1024]{2,1,0:T(8,128)(2,1)S(1)}, u32[]{:S(2)}, u32[]{:S(2)}) %collective-permute-start.63) | collective-permute-done | bytes 1048608 | tf_op jit(solution)/shard_map/ppermute | solution.py:57
  1072.8 18.4 %collective-permute-done.67 = bf16[2,256,1024]{2,1,0:T(8,128)(2,1)S(1)} collective-permute-done((bf16[2,256,1024]{2,1,0:T(8,128)(2,1)S(1)}, bf16[2,256,1024]{2,1,0:T(8,128)(2,1)S(1)}, u32[]{:S(2)}, u32[]{:S(2)}) %collective-permute-start.67) | collective-permute-done | bytes 1048608 | tf_op jit(solution)/shard_map/ppermute | solution.py:57
  (672 shorter events, 682.4 us)
Async XLA Ops:
  13.0 99.5 %all-to-all-start = ((bf16[8,128,512]{2,1,0:T(8,128)(2,1)}), bf16[8,128,512]{2,1,0:T(8,128)(2,1)S(1)}, u32[]{:S(2)}, u32[]{:S(2)}) async-start(bf16[8,128,512]{2,1,0:T(8,128)(2,1)} %copy.229), calls=%async_computation | async-start | bytes 2097152 | tf_op jit(solution)/shard_map/all_to_all | solution.py:217
  31.4 157.8 %collective-permute-start.30 = (bf16[256,2048]{1,0:T(8,128)(2,1)}, bf16[256,2048]{1,0:T(8,128)(2,1)}, u32[]{:S(2)}, u32[]{:S(2)}) collective-permute-start(bf16[256,2048]{1,0:T(8,128)(2,1)} %get-tuple-element.99), channel_id=1, source_target_pairs={{0,8},{1,9},{2,10},{3,11},{4,12},{5,13},{6,14},{7,15},{8,16},{9,17... | collective-permute-start | bytes 3145736 | tf_op jit(solution)/shard_map/ppermute | solution.py:66
  96.9 96.1 %collective-permute-start.27 = (bf16[512,1024]{1,0:T(8,128)(2,1)}, bf16[512,1024]{1,0:T(8,128)(2,1)}, u32[]{:S(2)}, u32[]{:S(2)}) collective-permute-start(bf16[512,1024]{1,0:T(8,128)(2,1)} %bitcast.60), channel_id=1, source_target_pairs={{0,8},{1,9},{2,10},{3,11},{4,12},{5,13},{6,14},{7,15},{8,16},{9,17... | collective-permute-start | bytes 3145736 | tf_op jit(solution)/shard_map/ppermute | solution.py:66
  99.4 151.8 %collective-permute-start.23 = (bf16[512,1024]{1,0:T(8,128)(2,1)}, bf16[512,1024]{1,0:T(8,128)(2,1)}, u32[]{:S(2)}, u32[]{:S(2)}) collective-permute-start(bf16[512,1024]{1,0:T(8,128)(2,1)} %bitcast.52), channel_id=1, source_target_pairs={{0,8},{1,9},{2,10},{3,11},{4,12},{5,13},{6,14},{7,15},{8,16},{9,17... | collective-permute-start | bytes 3145736 | tf_op jit(solution)/shard_map/ppermute | solution.py:66
  110.2 78.0 %collective-permute-start.12 = (bf16[512,256]{0,1:T(8,128)(2,1)}, bf16[512,256]{0,1:T(8,128)(2,1)S(1)}, u32[]{:S(2)}, u32[]{:S(2)}) collective-permute-start(bf16[512,256]{0,1:T(8,128)(2,1)} %collective-permute-done.11), channel_id=1, source_target_pairs={{0,8},{1,9},{2,10},{3,11},{4,12},{5,13},{6,14},{7,15},{8,16},{9,17... | collective-permute-start | bytes 786440 | tf_op jit(solution)/shard_map/ppermute | solution.py:66
  168.5 78.5 %all-to-all-start.5 = ((bf16[8,128,512]{2,1,0:T(8,128)(2,1)}), bf16[8,128,512]{2,1,0:T(8,128)(2,1)}, u32[]{:S(2)}, u32[]{:S(2)}) async-start(bf16[8,128,512]{2,1,0:T(8,128)(2,1)} %copy.245), calls=%async_computation.5 | async-start | bytes 2097152 | tf_op jit(solution)/shard_map/all_to_all | solution.py:217
  188.3 94.9 %collective-permute-start.8 = (bf16[2048,512]{1,0:T(8,128)(2,1)}, bf16[2048,512]{1,0:T(8,128)(2,1)}, u32[]{:S(2)}, u32[]{:S(2)}) collective-permute-start(bf16[2048,512]{1,0:T(8,128)(2,1)} %bitcast.23), channel_id=1, source_target_pairs={{0,1},{1,0},{2,3},{3,2},{4,5},{5,4},{6,7},{7,6},{8,9},{9,8},{10,11... | collective-permute-start | bytes 6291464 | tf_op jit(solution)/shard_map/ppermute | solution.py:63
  189.2 69.5 %collective-permute-start = (bf16[256,2048]{1,0:T(8,128)(2,1)}, bf16[256,2048]{1,0:T(8,128)(2,1)}, u32[]{:S(2)}, u32[]{:S(2)}) collective-permute-start(bf16[256,2048]{1,0:T(8,128)(2,1)} %get-tuple-element.105), channel_id=1, source_target_pairs={{0,2},{1,3},{2,0},{3,1},{4,6},{5,7},{6,4},{7,5},{8,10},{9,11},{10,... | collective-permute-start | bytes 3145736 | tf_op jit(solution)/shard_map/ppermute | solution.py:57
  193.0 88.0 %collective-permute-start.31 = (bf16[256,2048]{1,0:T(8,128)(2,1)}, bf16[256,2048]{1,0:T(8,128)(2,1)}, u32[]{:S(2)}, u32[]{:S(2)}) collective-permute-start(bf16[256,2048]{1,0:T(8,128)(2,1)} %collective-permute-done.30), channel_id=1, source_target_pairs={{0,8},{1,9},{2,10},{3,11},{4,12},{5,13},{6,14},{7,15},{8,16},{9,17... | collective-permute-start | bytes 3145736 | tf_op jit(solution)/shard_map/ppermute | solution.py:66
  211.7 116.5 %collective-permute-start.28 = (bf16[512,1024]{1,0:T(8,128)(2,1)}, bf16[512,1024]{1,0:T(8,128)(2,1)}, u32[]{:S(2)}, u32[]{:S(2)}) collective-permute-start(bf16[512,1024]{1,0:T(8,128)(2,1)} %collective-permute-done.27), channel_id=1, source_target_pairs={{0,8},{1,9},{2,10},{3,11},{4,12},{5,13},{6,14},{7,15},{8,16},{9,17... | collective-permute-start | bytes 3145736 | tf_op jit(solution)/shard_map/ppermute | solution.py:66
  281.0 649.7 %reduce-scatter.5.cloned.1.call-start = ((), (), s32[]{:S(2)}) async-start(), calls=%async_computation.14 | async-start | bytes 3932160 | tf_op jit(solution)/shard_map/reduce_scatter | solution.py:352
  281.1 89.4 %collective-permute-start.32 = (bf16[256,2048]{1,0:T(8,128)(2,1)}, bf16[256,2048]{1,0:T(8,128)(2,1)}, u32[]{:S(2)}, u32[]{:S(2)}) collective-permute-start(bf16[256,2048]{1,0:T(8,128)(2,1)} %collective-permute-done.31), channel_id=1, source_target_pairs={{0,8},{1,9},{2,10},{3,11},{4,12},{5,13},{6,14},{7,15},{8,16},{9,17... | collective-permute-start | bytes 3145736 | tf_op jit(solution)/shard_map/ppermute | solution.py:66
  377.9 91.1 %collective-permute-start.35 = (bf16[1024,2048]{1,0:T(8,128)(2,1)}, bf16[1024,2048]{1,0:T(8,128)(2,1)S(1)}, u32[]{:S(2)}, u32[]{:S(2)}) collective-permute-start(bf16[1024,2048]{1,0:T(8,128)(2,1)} %bitcast.69), channel_id=1, source_target_pairs={{0,1},{1,0},{2,3},{3,2},{4,5},{5,4},{6,7},{7,6},{8,9},{9,8},{10,11... | collective-permute-start | bytes 12582920 | tf_op jit(solution)/shard_map/ppermute | solution.py:63
  394.9 80.3 %collective-permute-start.34 = (bf16[2048,1024]{1,0:T(8,128)(2,1)}, bf16[2048,1024]{1,0:T(8,128)(2,1)S(1)}, u32[]{:S(2)}, u32[]{:S(2)}) collective-permute-start(bf16[2048,1024]{1,0:T(8,128)(2,1)} %bitcast.64), channel_id=1, source_target_pairs={{0,1},{1,0},{2,3},{3,2},{4,5},{5,4},{6,7},{7,6},{8,9},{9,8},{10,11... | collective-permute-start | bytes 12582920 | tf_op jit(solution)/shard_map/ppermute | solution.py:63
  656.1 354.1 %reduce-scatter.7.cloned.1.call-start = ((), (), s32[]{:S(2)}) async-start(), calls=%async_computation.15 | async-start | bytes 5242880 | tf_op jit(solution)/shard_map/reduce_scatter | solution.py:352
  677.7 335.5 %reduce-scatter.9.cloned.1.call-start = ((), (), s32[]{:S(2)}) async-start(), calls=%async_computation.16 | async-start | bytes 5242880 | tf_op jit(solution)/shard_map/reduce_scatter | solution.py:352
  699.0 317.3 %reduce-scatter.11.cloned.1.call-start = ((), (), s32[]{:S(2)}) async-start(), calls=%async_computation.17 | async-start | bytes 5242880 | tf_op jit(solution)/shard_map/reduce_scatter | solution.py:352
  708.8 81.3 %collective-permute-start.69 = (bf16[1024,2048]{1,0:T(8,128)(2,1)}, bf16[1024,2048]{1,0:T(8,128)(2,1)}, u32[]{:S(2)}, u32[]{:S(2)}) collective-permute-start(bf16[1024,2048]{1,0:T(8,128)(2,1)} %convolution_convert_fusion), channel_id=1, source_target_pairs={{0,1},{1,0},{2,3},{3,2},{4,5},{5,4},{6,7},{7,6},{8,9},{9,8},{10,11... | collective-permute-start | bytes 12582920 | tf_op jit(solution)/shard_map/ppermute | solution.py:63
  926.7 81.6 %all-to-all-start.8 = ((bf16[8,128,512]{2,1,0:T(8,128)(2,1)}), bf16[8,128,512]{2,1,0:T(8,128)(2,1)S(1)}, u32[]{:S(2)}, u32[]{:S(2)}) async-start(bf16[8,128,512]{2,1,0:T(8,128)(2,1)} %copy.255), calls=%async_computation.8 | async-start | bytes 2097152 | tf_op jit(solution)/shard_map/all_to_all | solution.py:233
  932.6 72.5 %collective-permute-start.58 = (bf16[256,768]{0,1:T(8,128)(2,1)}, bf16[256,768]{0,1:T(8,128)(2,1)S(1)}, u32[]{:S(2)}, u32[]{:S(2)}) collective-permute-start(bf16[256,768]{0,1:T(8,128)(2,1)} %broadcast_select_fusion.10), channel_id=1, source_target_pairs={{0,4},{1,5},{2,6},{3,7},{4,0},{5,1},{6,2},{7,3},{8,12},{9,13},{10,... | collective-permute-start | bytes 1179656 | tf_op jit(solution)/shard_map/ppermute | solution.py:60
  1026.3 66.6 %collective-permute-start.60 = (bf16[2,2,256,768]{2,3,1,0:T(8,128)(2,1)S(1)}, bf16[2,2,256,768]{2,3,1,0:T(8,128)(2,1)S(1)}, u32[]{:S(2)}, u32[]{:S(2)}) collective-permute-start(bf16[2,2,256,768]{2,3,1,0:T(8,128)(2,1)S(1)} %pad_maximum_fusion.4), channel_id=1, source_target_pairs={{0,1},{1,0},{2,3},{3,2},{4,5},{5,4},{6,7},{7,6},{8,9},{9,8},{10,11... | collective-permute-start | bytes 4718600 | tf_op jit(solution)/shard_map/ppermute | solution.py:63
  1050.7 79.6 %collective-permute-start.71 = (bf16[2,256,2048]{2,1,0:T(8,128)(2,1)}, bf16[2,256,2048]{2,1,0:T(8,128)(2,1)}, u32[]{:S(2)}, u32[]{:S(2)}) collective-permute-start(bf16[2,256,2048]{2,1,0:T(8,128)(2,1)} %pad_maximum_fusion.3), channel_id=1, source_target_pairs={{0,1},{1,0},{2,3},{3,2},{4,5},{5,4},{6,7},{7,6},{8,9},{9,8},{10,11... | collective-permute-start | bytes 6291464 | tf_op jit(solution)/shard_map/ppermute | solution.py:63
  1072.8 64.5 %collective-permute-start.64 = (bf16[2,2,256,1024]{3,2,1,0:T(8,128)(2,1)}, bf16[2,2,256,1024]{3,2,1,0:T(8,128)(2,1)}, u32[]{:S(2)}, u32[]{:S(2)}) collective-permute-start(bf16[2,2,256,1024]{3,2,1,0:T(8,128)(2,1)} %pad_maximum_fusion.1), channel_id=1, source_target_pairs={{0,1},{1,0},{2,3},{3,2},{4,5},{5,4},{6,7},{7,6},{8,9},{9,8},{10,11... | collective-permute-start | bytes 6291464 | tf_op jit(solution)/shard_map/ppermute | solution.py:63
  1092.9 75.6 %collective-permute-start.68 = (bf16[2,2,256,1024]{3,2,1,0:T(8,128)(2,1)}, bf16[2,2,256,1024]{3,2,1,0:T(8,128)(2,1)}, u32[]{:S(2)}, u32[]{:S(2)}) collective-permute-start(bf16[2,2,256,1024]{3,2,1,0:T(8,128)(2,1)} %pad_maximum_fusion.2), channel_id=1, source_target_pairs={{0,1},{1,0},{2,3},{3,2},{4,5},{5,4},{6,7},{7,6},{8,9},{9,8},{10,11... | collective-permute-start | bytes 6291464 | tf_op jit(solution)/shard_map/ppermute | solution.py:63
  (186 other events, 3215.6 us)
Sparse Core Ops, SparseCore 0:
  656.2 60.8 reduce-scatter.4
  720.0 76.7 reduce-scatter.6
  799.2 77.2 reduce-scatter.8
  879.2 109.8 reduce-scatter.10

commit v2 on v1

v2 whole, which is shorter than its diff:
```python
import math

import jax
import jax.numpy as jnp
from jax import lax
from jax.experimental import pallas as pl
from jax.experimental.pallas import tpu as pltpu
from jax.sharding import Mesh
from jax.sharding import PartitionSpec as P

QUERY_HEADS = 8
KEY_VALUE_HEADS = 4
HEAD_SIZE = 256

EPS_NORM = 1e-06
ROPE_BASE = 1000042.0
MASK_FILL = -1e30
AXES = ("z", "y", "x", "c")
F32 = jnp.float32
BF16 = jnp.bfloat16


def dot(a, b, dims):
    return lax.dot_general(a, b, (dims, ((), ())), preferred_element_type=F32)


def mm(a, b):
    return dot(a, b, ((1,), (0,)))


def mm_nt(a, b):
    return dot(a, b, ((1,), (1,)))


def mm_tn(a, b):
    return dot(a, b, ((0,), (0,)))


def sync(*values):
    return lax.optimization_barrier(values)


def after(value, *others):
    return lax.optimization_barrier((value,) + others)[0]


class Links:
    def __init__(self, planes):
        self.planes = planes

        def pairs(move):
            out = []
            for z in range(planes):
                for y in range(2):
                    for x in range(2):
                        for c in range(2):
                            a, b, d, e = move(z, y, x, c)
                            out.append((((z * 2 + y) * 2 + x) * 2 + c, ((a * 2 + b) * 2 + d) * 2 + e))
            return out

        self.px = pairs(lambda z, y, x, c: (z, y, 1 - x, c))
        self.py = pairs(lambda z, y, x, c: (z, 1 - y, x, c))
        self.pxy = pairs(lambda z, y, x, c: (z, 1 - y, 1 - x, c))
        self.pc = pairs(lambda z, y, x, c: (z, y, x, 1 - c))
        self.pz = [
            pairs(lambda z, y, x, c, k=k: ((z + k) % planes, y, x, c)) for k in range(planes)
        ]
        self.pz_swap = []
        k = 1
        while k < planes:
            self.pz_swap.append(pairs(lambda z, y, x, c, k=k: (z ^ k, y, x, c)))
            k *= 2

    def x(self, a):
        return lax.ppermute(a, AXES, self.px)

    def y(self, a):
        return lax.ppermute(a, AXES, self.py)

    def c(self, a):
        return lax.ppermute(a, AXES, self.pc)

    def swap_chips(self, chunks):
        return [
            chunks[0],
            self.x(chunks[1]),
            self.y(chunks[2]),
            lax.ppermute(chunks[3], AXES, self.pxy),
        ]

    def sum_plane(self, a):
        for p in (self.pc, self.px, self.py):
            a = a + lax.ppermute(a, AXES, p)
        return a

    def sum_planes(self, a):
        for p in self.pz_swap:
            a = a + lax.ppermute(a, AXES, p)
        return a

    def gather_one(self, a):
        return self.x(a), self.y(a)

    def gather_two(self, ax, ay):
        m = ax.shape[0] // 2
        return self.x(ay[:m]), self.y(ax[m:])

    def scatter_one(self, left, right):
        n = left.shape[0] // 4
        l4 = left.reshape(4, n, left.shape[1])
        return self.x(jnp.stack([l4[1], l4[3]])), self.y(right[2 * n :].reshape(2, n, right.shape[1]))

    def scatter_two(self, left, right, gl, gr):
        n = left.shape[0] // 4
        l_far = self.y((left[2 * n : 3 * n].astype(F32) + gl[1]).astype(BF16))
        r_far = self.x((right[n : 2 * n].astype(F32) + gr[1]).astype(BF16))
        return l_far, r_far

    def scatter_end(self, left, right, gl, gr, l_far, r_far):
        n = left.shape[0] // 4
        l_own = left[:n].astype(F32) + gl[0] + l_far
        r_own = right[:n].astype(F32) + gr[0] + r_far
        return jnp.concatenate([l_own, r_own], axis=1)

    def gather_planes(self, a):
        got = lax.all_gather(a, ("c", "z"), axis=0, tiled=True)
        return got.reshape(2, self.planes * a.shape[0], a.shape[1])

    def gather_gains(self, a):
        n = a.shape[1]
        y_me = lax.axis_index("y")
        z_me = lax.axis_index("z")
        two = pair(y_me, a, self.y(a))
        out = jnp.zeros((self.planes,) + two.shape, a.dtype)
        for k in range(self.planes):
            part = two if k == 0 else lax.ppermute(two, AXES, self.pz[k])
            at = lax.rem(z_me - k + self.planes, self.planes)
            out = lax.dynamic_update_slice(out, part[None], (at, 0, 0, 0))
        return jnp.transpose(out, (2, 0, 1, 3)).reshape(2, 2 * self.planes * n)


def pair(bit, own, other):
    return jnp.stack([jnp.where(bit == 0, own, other), jnp.where(bit == 0, other, own)])


def estimate(flops, bytes_accessed, transcendentals):
    return pl.CostEstimate(
        flops=flops // 16,
        bytes_accessed=bytes_accessed // 16,
        transcendentals=transcendentals // 16,
    )


def rank_scalar(rank):
    return jnp.reshape(rank, (1,)).astype(jnp.int32)


def place_columns(rank, parts, planes, piece, side):
    n = parts[0].shape[0]
    width = planes * piece
    total = 8 * width
    if piece % 128:
        parts = [t[:, side * width : (side + 1) * width] for t in parts]
        out = jnp.zeros((n, planes, 8, piece), F32)
        for p, part in enumerate(parts):
            part = part.reshape(n, planes, 1, piece).astype(F32)
            out = lax.dynamic_update_slice(out, part, (0, 0, jnp.bitwise_xor(rank, p), 0))
        return out.reshape(n, total)
    tile = min(n, 64)

    def kernel(rank_ref, *refs):
        out = refs[8]
        for p in range(8):
            t = jnp.bitwise_xor(rank_ref[0], p)
            for z in range(planes):
                at = pl.multiple_of(z * 8 * piece + t * piece, 128)
                out[:, pl.ds(at, piece)] = refs[p][:, z * piece : (z + 1) * piece].astype(F32)

    return pl.pallas_call(
        kernel,
        out_shape=jax.ShapeDtypeStruct((n, total), F32),
        grid_spec=pltpu.PrefetchScalarGridSpec(
            num_scalar_prefetch=1,
            grid=(n // tile,),
            in_specs=[pl.BlockSpec((tile, width), lambda i, r: (i, side))] * 8,
            out_specs=pl.BlockSpec((tile, total), lambda i, r: (i, 0)),
        ),
        cost_estimate=estimate(flops=0, bytes_accessed=6 * n * total, transcendentals=0),
    )(rank_scalar(rank), *parts)


def place_rows(order, parts):
    n, d = parts[0].shape
    tile = min(d, 256)

    def kernel(order_ref, *refs):
        out = refs[4]
        for p in range(4):
            t = jnp.bitwise_xor(order_ref[0], p)
            out[pl.ds(pl.multiple_of(t * n, 8), n), :] = refs[p][...].astype(F32)

    return pl.pallas_call(
        kernel,
        out_shape=jax.ShapeDtypeStruct((4 * n, d), F32),
        grid_spec=pltpu.PrefetchScalarGridSpec(
            num_scalar_prefetch=1,
            grid=(d // tile,),
            in_specs=[pl.BlockSpec((n, tile), lambda i, r: (0, i))] * 4,
            out_specs=pl.BlockSpec((4 * n, tile), lambda i, r: (0, i)),
        ),
        cost_estimate=estimate(flops=0, bytes_accessed=24 * n * d, transcendentals=0),
    )(rank_scalar(order), *parts)


def place_attention(rank, parts):
    n, width = parts[0].shape
    h = HEAD_SIZE
    o = width - 2 * h
    tile = min(n, 64)

    def kernel(rank_ref, *refs):
        q_out, k_out, v_out, o_out = refs[8:]
        for p in range(8):
            t = jnp.bitwise_xor(rank_ref[0], p)
            j = t // 2
            core = t - 2 * j
            q_out[:, pl.ds(pl.multiple_of(t * h, 128), h)] = refs[p][:, :h].astype(F32)
            at = pl.ds(pl.multiple_of(j * h, 128), h)

            @pl.when(core == 0)
            def _():
                k_out[:, at] = refs[p][:, h : 2 * h].astype(F32)

            @pl.when(core == 1)
            def _():
                v_out[:, at] = refs[p][:, h : 2 * h].astype(F32)

            to = pl.multiple_of(core * 4 * o + j * o, 128)
            o_out[:, pl.ds(to, o)] = refs[p][:, 2 * h :].astype(F32)

    widths = (8 * h, 4 * h, 4 * h, 8 * o)
    return pl.pallas_call(
        kernel,
        out_shape=tuple(jax.ShapeDtypeStruct((n, w), F32) for w in widths),
        grid_spec=pltpu.PrefetchScalarGridSpec(
            num_scalar_prefetch=1,
            grid=(n // tile,),
            in_specs=[pl.BlockSpec((tile, width), lambda i, r: (i, 0))] * 8,
            out_specs=tuple(pl.BlockSpec((tile, w), lambda i, r: (i, 0)) for w in widths),
        ),
        cost_estimate=estimate(flops=0, bytes_accessed=48 * n * width, transcendentals=0),
    )(rank_scalar(rank), *parts)


def back_product(core, lefts, weight):
    m, k = lefts[0].shape
    n = weight.shape[1]
    tile = min(n // 2, 256)
    steps = n // 2 // tile

    def kernel(core_ref, a0, a1, l0, l1, r0, r1, left, right):
        left[...] = (mm_nt(a0[...], l0[...]) + mm_nt(a1[...], l1[...])).astype(BF16)
        right[...] = (mm_nt(a0[...], r0[...]) + mm_nt(a1[...], r1[...])).astype(BF16)

    whole = pl.BlockSpec((m, k), lambda i, r: (0, 0))
    out = pl.BlockSpec((m, tile), lambda i, r: (0, i))
    return pl.pallas_call(
        kernel,
        out_shape=(jax.ShapeDtypeStruct((m, n // 2), BF16),) * 2,
        grid_spec=pltpu.PrefetchScalarGridSpec(
            num_scalar_prefetch=1,
            grid=(steps,),
            in_specs=[
                whole,
                whole,
                pl.BlockSpec((None, tile, k), lambda i, r: (r[0], i, 0)),
                pl.BlockSpec((None, tile, k), lambda i, r: (1 - r[0], i, 0)),
                pl.BlockSpec((None, tile, k), lambda i, r: (r[0], i + steps, 0)),
                pl.BlockSpec((None, tile, k), lambda i, r: (1 - r[0], i + steps, 0)),
            ],
            out_specs=(out, out),
        ),
        compiler_params=pltpu.CompilerParams(vmem_limit_bytes=48 << 20),
        cost_estimate=estimate(
            flops=4 * m * k * n, bytes_accessed=4 * (m + n) * k + 2 * m * n, transcendentals=0
        ),
    )(rank_scalar(core), *lefts, weight, weight, weight, weight)


def ff_front(half, n2, weight):
    m, d = n2.shape
    f = weight.shape[2] // 2
    tile = 256
    steps = f // tile

    def kernel(half_ref, x, wg, wu, gate_out, up_out, act_out):
        gate = mm(x[...], wg[...])
        up = mm(x[...], wu[...])
        gate_out[...] = gate
        up_out[...] = up
        act_out[...] = (gate * jax.nn.sigmoid(gate) * up).astype(BF16)

    out = pl.BlockSpec((m, tile), lambda i, r: (0, i))
    return pl.pallas_call(
        kernel,
        out_shape=(
            jax.ShapeDtypeStruct((m, f), F32),
            jax.ShapeDtypeStruct((m, f), F32),
            jax.ShapeDtypeStruct((m, f), BF16),
        ),
        grid_spec=pltpu.PrefetchScalarGridSpec(
            num_scalar_prefetch=1,
            grid=(steps,),
            in_specs=[
                pl.BlockSpec((m, d), lambda i, r: (0, 0)),
                pl.BlockSpec((None, d, tile), lambda i, r: (r[0], 0, i)),
                pl.BlockSpec((None, d, tile), lambda i, r: (r[0], 0, i + steps)),
            ],
            out_specs=(out, out, out),
        ),
        compiler_params=pltpu.CompilerParams(vmem_limit_bytes=48 << 20),
        cost_estimate=estimate(
            flops=4 * m * d * f, bytes_accessed=2 * m * d + 4 * d * f + 10 * m * f, transcendentals=m * f
        ),
    )(rank_scalar(half), n2, weight, weight)


def ff_back(half, d_in, weight, gate_pre, up_pre):
    m, d = d_in.shape
    f = weight.shape[1]
    tile = 256
    steps = f // tile

    def kernel(half_ref, g, w, gate_ref, up_ref, out, kept):
        i = pl.program_id(0)

        @pl.when(i < steps)
        def _():
            act_grad = mm_nt(g[...], w[...])
            gate = gate_ref[...]
            sig = jax.nn.sigmoid(gate)
            out[...] = (act_grad * up_ref[...] * sig * (1.0 + gate * (1.0 - sig))).astype(BF16)
            kept[i] = (act_grad * (gate * sig)).astype(BF16)

        @pl.when(i >= steps)
        def _():
            out[...] = kept[i - steps]

    last = steps - 1
    pre = pl.BlockSpec((m, tile), lambda i, r: (0, jnp.minimum(i, last)))
    return pl.pallas_call(
        kernel,
        out_shape=jax.ShapeDtypeStruct((m, 2 * f), BF16),
        grid_spec=pltpu.PrefetchScalarGridSpec(
            num_scalar_prefetch=1,
            grid=(2 * steps,),
            in_specs=[
                pl.BlockSpec((m, d), lambda i, r: (0, 0)),
                pl.BlockSpec((None, tile, d), lambda i, r: (r[0], jnp.minimum(i, last), 0)),
                pre,
                pre,
            ],
            out_specs=pl.BlockSpec((m, tile), lambda i, r: (0, i)),
            scratch_shapes=[pltpu.VMEM((steps, m, tile), BF16)],
        ),
        compiler_params=pltpu.CompilerParams(vmem_limit_bytes=48 << 20),
        cost_estimate=estimate(
            flops=2 * m * d * f, bytes_accessed=2 * (m + f) * d + 12 * m * f, transcendentals=m * f
        ),
    )(rank_scalar(half), d_in, weight, gate_pre, up_pre)


def forward_product(core, lefts, weight):
    m, k = lefts[0].shape
    n = weight.shape[2]
    tile = 256
    steps = n // 2 // tile

    def kernel(core_ref, a0, a1, l0, l1, r0, r1, left, right):
        left[...] = (mm(a0[...], l0[...]) + mm(a1[...], l1[...])).astype(BF16)
        right[...] = (mm(a0[...], r0[...]) + mm(a1[...], r1[...])).astype(BF16)

    whole = pl.BlockSpec((m, k), lambda i, r: (0, 0))
    out = pl.BlockSpec((m, tile), lambda i, r: (0, i))
    return pl.pallas_call(
        kernel,
        out_shape=(jax.ShapeDtypeStruct((m, n // 2), BF16),) * 2,
        grid_spec=pltpu.PrefetchScalarGridSpec(
            num_scalar_prefetch=1,
            grid=(steps,),
            in_specs=[
                whole,
                whole,
                pl.BlockSpec((None, k, tile), lambda i, r: (r[0], 0, i)),
                pl.BlockSpec((None, k, tile), lambda i, r: (1 - r[0], 0, i)),
                pl.BlockSpec((None, k, tile), lambda i, r: (r[0], 0, i + steps)),
                pl.BlockSpec((None, k, tile), lambda i, r: (1 - r[0], 0, i + steps)),
            ],
            out_specs=(out, out),
        ),
        compiler_params=pltpu.CompilerParams(vmem_limit_bytes=40 << 20),
        cost_estimate=estimate(
            flops=4 * m * k * n, bytes_accessed=4 * (m + n) * k + 2 * m * n, transcendentals=0
        ),
    )(rank_scalar(core), *lefts, weight, weight, weight, weight)


def send_blocks(slot, has, streams):
    groups = slot.shape[0]
    _, r, f = streams[0].shape
    count = len(streams)

    def kernel(slot_ref, has_ref, *refs):
        keep = has_ref[pl.program_id(0)] > 0
        for i in range(count):
            v = refs[i][0]
            refs[count][0, i] = jnp.where(keep, v, jnp.zeros_like(v))

    return pl.pallas_call(
        kernel,
        out_shape=jax.ShapeDtypeStruct((groups, count, r, f), BF16),
        grid_spec=pltpu.PrefetchScalarGridSpec(
            num_scalar_prefetch=2,
            grid=(groups,),
            in_specs=[pl.BlockSpec((1, r, f), lambda g, s, h: (s[g], 0, 0))] * count,
            out_specs=pl.BlockSpec((1, count, r, f), lambda g, s, h: (g, 0, 0, 0)),
        ),
        cost_estimate=estimate(
            flops=0, bytes_accessed=4 * count * groups * r * f, transcendentals=0
        ),
    )(slot, has, *streams)


def assemble_rows(info, pieces, gain=None):
    _, _, r, f = pieces[0].shape
    width = 4 * f

    def block(i, n):
        return 2 * jnp.bitwise_xor(n[0], (i // 2) % 2) + i % 2

    def kernel(info_ref, *refs):
        own, ax, ay, dx, dy = refs[:5]
        i = pl.program_id(0)
        x = info_ref[0]
        near = i < 4
        low = block(i, info_ref) < 2
        same = jnp.where(near, own[0], ay[0])
        other = jnp.where(near, ax[0], jnp.where(low, dx[0], dy[0]))
        at = info_ref[2 + i] * r + lax.broadcasted_iota(jnp.int32, (r, f), 0)
        inside = at < info_ref[1]
        parts = []
        for h, v in ((x, same), (1 - x, other)):
            for c in range(2):
                t = jnp.where(inside, v[c].astype(F32), 0.0)
                parts.append((2 * h + c, t))
        if gain is None:
            for q, t in parts:
                refs[5][:, pl.ds(pl.multiple_of(q * f, 128), f)] = t.astype(BF16)
            return
        gain_ref, normed, rows = refs[5:]
        total = sum(jnp.sum(t * t, axis=1, keepdims=True) for _, t in parts)
        factor = lax.rsqrt(total * (1.0 / width) + EPS_NORM)
        for q, t in parts:
            g = gain_ref[pl.ds(q, 1), :]
            normed[:, pl.ds(pl.multiple_of(q * f, 128), f)] = (t * factor * g).astype(BF16)

        @pl.when(i < 2)
        def _():
            for q, t in parts:
                rows[:, pl.ds(pl.multiple_of(q * f, 128), f)] = t.astype(BF16)

    whole = pl.BlockSpec((1, 2, r, f), lambda i, n: (block(i, n), 0, 0, 0))
    specs = [
        whole,
        whole,
        whole,
        pl.BlockSpec((1, 2, r, f), lambda i, n: (jnp.minimum(block(i, n), 1), 0, 0, 0)),
        pl.BlockSpec((1, 2, r, f), lambda i, n: (jnp.maximum(block(i, n) - 2, 0), 0, 0, 0)),
    ]
    shape = [jax.ShapeDtypeStruct((8 * r, width), BF16)]
    outs = [pl.BlockSpec((r, width), lambda i, n: (i, 0))]
    args = list(pieces)
    if gain is not None:
        specs.append(pl.BlockSpec((4, f), lambda i, n: (0, 0)))
        args.append(gain)
        shape.append(jax.ShapeDtypeStruct((2 * r, width), BF16))
        outs.append(pl.BlockSpec((r, width), lambda i, n: (jnp.minimum(i, 1), 0)))
    got = pl.pallas_call(
        kernel,
        out_shape=tuple(shape),
        grid_spec=pltpu.PrefetchScalarGridSpec(
            num_scalar_prefetch=1, grid=(8,), in_specs=specs, out_specs=tuple(outs)
        ),
        cost_estimate=estimate(
            flops=16 * r * width, bytes_accessed=40 * r * width, transcendentals=0
        ),
    )(info, *args)
    return got[0] if gain is None else got


def turn(v, cos_t, sin_t, sign):
    h = v.shape[-1] // 2
    a, b = v[:, :h], v[:, h:]
    s = sin_t * sign
    return jnp.concatenate([a * cos_t - b * s, b * cos_t + a * s], axis=-1).astype(BF16)


def project(normed, w_attn, cos_t, sin_t):
    rows, width = normed.shape
    h = HEAD_SIZE
    tile = 256

    def kernel(x_ref, w_ref, c_ref, s_ref, q0, q1, k, v):
        even = mm(x_ref[...], w_ref[0])
        odd = mm(x_ref[...], w_ref[1])
        cos_t, sin_t = c_ref[...], s_ref[...]
        q0[...] = turn(even[:, :h], cos_t, sin_t, 1.0)
        k[...] = turn(even[:, h:], cos_t, sin_t, 1.0)
        q1[...] = turn(odd[:, :h], cos_t, sin_t, 1.0)
        v[...] = odd[:, h:].astype(BF16)

    out = pl.BlockSpec((tile, h), lambda i: (i, 0))
    table = pl.BlockSpec((tile, h // 2), lambda i: (i, 0))
    return pl.pallas_call(
        kernel,
        out_shape=(jax.ShapeDtypeStruct((rows, h), BF16),) * 4,
        grid=(rows // tile,),
        in_specs=[
            pl.BlockSpec((tile, width), lambda i: (i, 0)),
            pl.BlockSpec((2, width, 2 * h), lambda i: (0, 0, 0)),
            table,
            table,
        ],
        out_specs=(out,) * 4,
        compiler_params=pltpu.CompilerParams(vmem_limit_bytes=40 << 20),
        cost_estimate=estimate(
            flops=8 * rows * width * h, bytes_accessed=2 * rows * width + 8 * width * h, transcendentals=0
        ),
    )(normed, w_attn, cos_t, sin_t)


def attend(q0, q1, keys, values, w_o, at_q, at_k):
    rows, h = q0.shape
    half = w_o.shape[2]
    tile = 256
    factor = 1.0 / math.sqrt(HEAD_SIZE)

    def kernel(q0_ref, q1_ref, k_ref, v_ref, w_ref, aq_ref, ak_ref, mixed, lse, left, right):
        allowed = ak_ref[...] <= aq_ref[...]
        for i, q_ref in enumerate((q0_ref, q1_ref)):
            scores = jnp.where(allowed, mm_nt(q_ref[...], k_ref[...]) * factor, MASK_FILL)
            top = jnp.max(scores, axis=-1, keepdims=True)
            e = jnp.exp(scores - top)
            total = jnp.sum(e, axis=-1, keepdims=True)
            probs = (e * (1.0 / total)).astype(BF16)
            mixed[:, i * h : (i + 1) * h] = mm(probs, v_ref[...]).astype(BF16)
            lse[i] = top + jnp.log(total)
        left[...] = mm(mixed[...], w_ref[0]).astype(BF16)
        right[...] = mm(mixed[...], w_ref[1]).astype(BF16)

    q_spec = pl.BlockSpec((tile, h), lambda i: (i, 0))
    kv_spec = pl.BlockSpec((rows, h), lambda i: (0, 0))
    out_spec = pl.BlockSpec((tile, half), lambda i: (i, 0))
    return pl.pallas_call(
        kernel,
        out_shape=(
            jax.ShapeDtypeStruct((rows, 2 * h), BF16),
            jax.ShapeDtypeStruct((2, rows, 1), F32),
            jax.ShapeDtypeStruct((rows, half), BF16),
            jax.ShapeDtypeStruct((rows, half), BF16),
        ),
        grid=(rows // tile,),
        in_specs=[
            q_spec,
            q_spec,
            kv_spec,
            kv_spec,
            pl.BlockSpec((2, 2 * h, half), lambda i: (0, 0, 0)),
            pl.BlockSpec((tile, 1), lambda i: (i, 0)),
            pl.BlockSpec((1, rows), lambda i: (0, 0)),
        ],
        out_specs=(
            pl.BlockSpec((tile, 2 * h), lambda i: (i, 0)),
            pl.BlockSpec((2, tile, 1), lambda i: (0, i, 0)),
            out_spec,
            out_spec,
        ),
        compiler_params=pltpu.CompilerParams(vmem_limit_bytes=40 << 20),
        cost_estimate=estimate(
            flops=8 * rows * rows * h + 8 * rows * h * half,
            bytes_accessed=12 * rows * h + 8 * h * half + 4 * rows * half,
            transcendentals=2 * rows * rows,
        ),
    )(q0, q1, keys, values, w_o, at_q, at_k)


def attend_back(attn_in, w_o, q0, q1, keys, values, lse, at_q, at_k, cos_t, sin_t):
    rows, h = q0.shape
    half = w_o.shape[2]
    tile = 256
    steps = rows // tile
    factor = 1.0 / math.sqrt(HEAD_SIZE)

    def kernel(
        g_ref, w_ref, q0_ref, q1_ref, k_ref, v_ref, lse_ref, aq_ref, ak_ref, c_ref, s_ref, ca_ref,
        sa_ref, dq0, dq1, dk, dv, k_sum, v_sum,
    ):
        step = pl.program_id(0)

        @pl.when(step == 0)
        def _():
            k_sum[...] = jnp.zeros_like(k_sum)
            v_sum[...] = jnp.zeros_like(v_sum)

        g = g_ref[...]
        dmix = (mm_nt(g[:, :half], w_ref[0]) + mm_nt(g[:, half:], w_ref[1])).astype(BF16)
        allowed = ak_ref[...] <= aq_ref[...]
        for i, (q_ref, dq) in enumerate(((q0_ref, dq0), (q1_ref, dq1))):
            d = dmix[:, i * h : (i + 1) * h]
            scores = jnp.where(allowed, mm_nt(q_ref[...], k_ref[...]) * factor, MASK_FILL)
            probs = jnp.exp(scores - lse_ref[i])
            v_sum[...] += mm_tn(probs.astype(BF16), d)
            prob_grad = mm_nt(d, v_ref[...])
            inner = jnp.sum(prob_grad * probs, axis=-1, keepdims=True)
            score_grad = (probs * (prob_grad - inner)).astype(BF16)
            k_sum[...] += mm_tn(score_grad, q_ref[...])
            rot = (mm(score_grad, k_ref[...]) * factor).astype(BF16).astype(F32)
            dq[...] = turn(rot, c_ref[...], s_ref[...], -1.0)

        @pl.when(step == steps - 1)
        def _():
            rot = (k_sum[...] * factor).astype(BF16).astype(F32)
            dk[...] = turn(rot, ca_ref[...], sa_ref[...], -1.0)
            dv[...] = v_sum[...].astype(BF16)

    q_spec = pl.BlockSpec((tile, h), lambda i: (i, 0))
    kv_spec = pl.BlockSpec((rows, h), lambda i: (0, 0))
    table = pl.BlockSpec((tile, h // 2), lambda i: (i, 0))
    all_table = pl.BlockSpec((rows, h // 2), lambda i: (0, 0))
    return pl.pallas_call(
        kernel,
        out_shape=(jax.ShapeDtypeStruct((rows, h), BF16),) * 4,
        grid=(steps,),
        in_specs=[
            pl.BlockSpec((tile, 2 * half), lambda i: (i, 0)),
            pl.BlockSpec((2, 2 * h, half), lambda i: (0, 0, 0)),
            q_spec,
            q_spec,
            kv_spec,
            kv_spec,
            pl.BlockSpec((2, tile, 1), lambda i: (0, i, 0)),
            pl.BlockSpec((tile, 1), lambda i: (i, 0)),
            pl.BlockSpec((1, rows), lambda i: (0, 0)),
            table,
            table,
            all_table,
            all_table,
        ],
        out_specs=(q_spec, q_spec, kv_spec, kv_spec),
        scratch_shapes=[pltpu.VMEM((rows, h), F32), pltpu.VMEM((rows, h), F32)],
        compiler_params=pltpu.CompilerParams(vmem_limit_bytes=48 << 20),
        cost_estimate=estimate(
            flops=20 * rows * rows * h + 8 * rows * h * half,
            bytes_accessed=20 * rows * h + 8 * h * half + 4 * rows * half,
            transcendentals=2 * rows * rows,
        ),
    )(attn_in, w_o, q0, q1, keys, values, lse, at_q, at_k, cos_t, sin_t, cos_t, sin_t)


def rope_tables(positions):
    half_dim = HEAD_SIZE // 2
    frequency = jnp.exp(jnp.arange(half_dim, dtype=F32) * (-2.0 * math.log(ROPE_BASE) / HEAD_SIZE))
    angles = positions.astype(F32)[:, None] * frequency[None, :]
    return jnp.cos(angles), jnp.sin(angles)


def norm_factor(hidden):
    return lax.rsqrt(jnp.mean(hidden * hidden, axis=-1, keepdims=True) + EPS_NORM)


def norm_backward(upstream, hidden, factor, gain_vec):
    scaled = upstream * gain_vec
    gain_part = jnp.sum(upstream * hidden * factor, axis=0)
    inner_sum = jnp.mean(scaled * hidden, axis=-1, keepdims=True)
    return (factor * scaled - hidden * (factor * factor * factor) * inner_sum, gain_part)


def make_body(planes):
    links = Links(planes)

    def body(
        tokens,
        cotangent,
        query_weight,
        key_matrix,
        value_matrix,
        output_weight,
        gate_weight,
        up_weight,
        down_weight,
        prenorm_gain,
        midnorm_gain,
        seq_len,
        stream_order,
    ):
        groups = 2 * planes
        z_me = lax.axis_index("z")
        y_me = lax.axis_index("y")
        x_me = lax.axis_index("x")
        c_me = lax.axis_index("c")
        slots, blk, quarter = tokens.shape
        width = 4 * quarter
        rank = 4 * y_me + 2 * x_me + c_me
        head = 2 * y_me + x_me
        shard = query_weight.shape[0]
        ff = gate_weight.shape[1]
        piece = ff // groups // 4

        nblk = (seq_len + blk - 1) // blk
        member = (stream_order[:, None] == jnp.arange(groups, dtype=jnp.int32)[None, :]).astype(
            jnp.int32
        )
        ordered = jnp.sum(member * nblk[None, :], axis=1)
        firsts = jnp.cumsum(ordered) - ordered
        seq_start = jnp.sum(member * firsts[:, None], axis=0)
        group_me = 2 * z_me + y_me
        offset = lax.rem(group_me - lax.rem(seq_start, groups) + groups, groups)
        has = offset < nblk
        slot_of = jnp.where(has, (seq_start + offset) // groups, 0)
        block_ids = jnp.arange(slots, dtype=jnp.int32) * groups + group_me
        ahead = block_ids[:, None] - seq_start[None, :]
        covers = ((ahead >= 0) & (ahead < nblk[None, :])).astype(jnp.int32)
        seq_of = jnp.sum(covers * jnp.arange(groups, dtype=jnp.int32)[None, :], axis=1)
        taken = jnp.sum(covers, axis=1)

        mine = 2 * z_me + c_me
        picked = jnp.arange(groups, dtype=jnp.int32) == mine
        my_start = jnp.sum(jnp.where(picked, seq_start, 0))
        my_len = jnp.sum(jnp.where(picked, seq_len, 0))

        def block_places(y):
            first = lax.rem(y + my_start, 2)
            plane = lax.rem((my_start + first) // 2, planes)
            k = jnp.arange(4, dtype=jnp.int32)
            if planes == 4:
                k = lax.rem(k - plane + planes, planes)
            return first + 2 * k, plane

        places_own, plane_own = block_places(y_me)
        places_far, _ = block_places(1 - y_me)

        def two_places(places, x):
            return lax.dynamic_slice(places, (2 * x,), (2,))

        places = jnp.concatenate(
            [
                two_places(places_own, x_me),
                two_places(places_own, 1 - x_me),
                two_places(places_far, x_me),
                two_places(places_far, 1 - x_me),
            ]
        )
        info = jnp.concatenate([jnp.stack([x_me, my_len]), places]).astype(jnp.int32)
        positions = (places[:, None] * blk + jnp.arange(blk, dtype=jnp.int32)[None, :]).reshape(-1)
        at_q = positions[:, None]
        at_k = jnp.where(positions < my_len, positions, 1 << 30)[None, :]
        rows = 2 * blk
        valid = (positions[:rows] < my_len).astype(F32)[:, None]

        def send_layout(out_rows):
            left, right = out_rows[:, : 2 * quarter], out_rows[:, 2 * quarter :]
            keep = jnp.where(x_me == 0, left, right)
            got = links.x(jnp.where(x_me == 0, right, left))
            send = pair(x_me, keep, got).reshape(4, blk, 2, quarter)
            send = jnp.transpose(send, (0, 2, 1, 3))
            if planes > 4:
                send = jnp.pad(send, ((0, planes - 4), (0, 0), (0, 0), (0, 0)))
                send = jnp.roll(send, plane_own, axis=0)
            return send.reshape(groups, blk, quarter)

        def to_stream(got):
            return send_blocks(seq_of, taken, [got])[:, 0]

        def by_rank(g):
            n = g.shape[1]
            own = lax.dynamic_slice(g, (y_me * shard, 0), (shard, n))
            other = lax.dynamic_slice(g, ((1 - y_me) * shard, 0), (shard, n))
            parts = links.swap_chips([own, own, other, other])
            return [links.c(parts[p // 2]) if p % 2 else parts[p // 2] for p in range(8)]

        def plane_rows(own_part, far_part):
            got = links.y(far_part)
            both = pair(y_me, own_part, got)
            return both.reshape(2 * own_part.shape[0], own_part.shape[1])

        def ff_columns(w, r):
            return jnp.concatenate(
                [
                    lax.dynamic_slice(w, (0, p * 8 * piece + r * piece), (shard, piece))
                    for p in range(planes)
                ],
                axis=1,
            )

        far = rank + 4 - 8 * y_me
        def attn_columns(r, ws):
            q = lax.dynamic_slice(ws[0], (0, r * HEAD_SIZE), (shard, HEAD_SIZE))
            j = r // 2
            k = lax.dynamic_slice(ws[1], (0, j * HEAD_SIZE), (shard, HEAD_SIZE))
            v = lax.dynamic_slice(ws[2], (0, j * HEAD_SIZE), (shard, HEAD_SIZE))
            at = lax.rem(r, 2) * (width // 2) + (r // 2) * (width // 8)
            o = lax.dynamic_slice(ws[3], (0, at), (shard, width // 8))
            return jnp.concatenate([q, jnp.where(c_me == 0, k, v), o], axis=1)

        gains = links.gather_gains(jnp.stack([prenorm_gain, midnorm_gain])).astype(F32)

        def to_sequences(stream):
            send = send_blocks(slot_of, has.astype(jnp.int32), [stream])
            return send[:, 0]

        def arranged(got):
            got = got.reshape(planes, 2, blk, quarter)
            if planes > 4:
                got = jnp.roll(got, -plane_own, axis=0)[:4]
            return got

        def exchange(send):
            return lax.all_to_all(send, ("z", "c"), split_axis=0, concat_axis=0, tiled=True)

        send_tokens = to_sequences(tokens)
        got_tokens = exchange(send_tokens)
        *attn_ws, gate_weight, up_weight, down_weight, _ = sync(
            query_weight,
            key_matrix,
            value_matrix,
            output_weight,
            gate_weight,
            up_weight,
            down_weight,
            send_tokens,
        )
        attn_share = plane_rows(attn_columns(rank, attn_ws), attn_columns(far, attn_ws))

        def ff_share(r):
            return jnp.concatenate([ff_columns(gate_weight, r), ff_columns(up_weight, r)], axis=1)

        ff_own, ff_far_rows = ff_share(rank), ff_share(far)
        down_share = lax.dynamic_slice(
            down_weight, ((2 * x_me + c_me) * piece, 0), (piece, width)
        )
        got_tokens, attn_share, ff_own, ff_far_rows, down_share, gains = sync(
            got_tokens, attn_share, ff_own, ff_far_rows, down_share, gains
        )
        w_attn = links.gather_planes(attn_share)
        own = arranged(got_tokens)
        ax, ay = sync(*links.gather_one(own))
        ff_two = plane_rows(ff_own, after(ff_far_rows, own))
        gain_pre, gain_mid = gains[0], gains[1]
        eighth = width // 8

        def spread(chunk_of):
            return links.swap_chips([chunk_of(jnp.bitwise_xor(head, p)) for p in range(4)])

        cos_t, sin_t = rope_tables(positions)
        dx, dy, cos_t, sin_t, ff_two = sync(*links.gather_two(ax, ay), cos_t, sin_t, ff_two)
        w_ff = links.gather_planes(ff_two)
        w_down = links.gather_planes(after(down_share, ff_two))
        normed, rows_in = assemble_rows(info, (own, ax, ay, dx, dy), gain_pre.reshape(4, quarter))
        send_cot = to_sequences(after(cotangent, dx))
        w_attn, normed, send_cot = sync(w_attn, normed, send_cot)
        got_cot = exchange(send_cot)
        w_o_cols = lax.dynamic_index_in_dim(w_attn, c_me, 0, keepdims=False)[:, 2 * HEAD_SIZE :]
        w_o = jnp.zeros((2 * HEAD_SIZE, 4 * eighth), BF16)
        for p, part in enumerate(
            spread(
                lambda t: lax.dynamic_slice(
                    w_o_cols, (t * 2 * HEAD_SIZE, 0), (2 * HEAD_SIZE, eighth)
                )
            )
        ):
            w_o = lax.dynamic_update_slice(w_o, part, (0, jnp.bitwise_xor(head, p) * eighth))
        w_o = pair(c_me, w_o, links.c(w_o))

        q0, q1, keys, values = project(normed, w_attn, cos_t, sin_t)
        mixed, lse, attn_left, attn_right = attend(q0, q1, keys, values, w_o, at_q, at_k)
        hidden_zero = rows_in.astype(F32)
        factor_pre = norm_factor(hidden_zero)
        gl, gr = sync(*links.scatter_one(attn_left, attn_right))
        l_far, r_far = sync(*links.scatter_two(attn_left, attn_right, gl, gr))
        hidden_one = hidden_zero + links.scatter_end(attn_left, attn_right, gl, gr, l_far, r_far)
        factor_mid = norm_factor(hidden_one)
        n_own = (hidden_one * factor_mid * gain_mid).astype(BF16)
        ax, ay, got_cot = sync(*links.gather_one(n_own), got_cot)
        dx, dy = sync(*links.gather_two(ax, ay))
        normed_two = jnp.concatenate([n_own, ax, ay, dx, dy], axis=0)
        own = after(arranged(got_cot), normed_two)
        n_ff = w_ff.shape[2] // 2
        far_gate, far_up, act_far = ff_front(1 - c_me, normed_two, w_ff)
        ax, ay, act_far = sync(*links.gather_one(own), act_far)
        own_gate, own_up, act_own = ff_front(c_me, after(normed_two, ax), w_ff)
        turned = sync(jnp.transpose(after(normed_two, act_own)))[0]
        dx, dy, act_own, turned = sync(*links.gather_two(ax, ay), act_own, turned)
        down_in = assemble_rows(info, (own, ax, ay, dx, dy))

        def far_part(left, right):
            return mm_tn(left, right).astype(BF16)

        def both_cores(left, right, got):
            return (mm_tn(left, right) + got).astype(BF16)

        def over_planes(g):
            return lax.psum_scatter(g, "z", scatter_dimension=0, tiled=True)

        half = width // 2
        down_far = far_part(act_far, down_in)
        sum_down = both_cores(act_own, down_in, links.c(down_far))
        w_down, d_in = sync(w_down, down_in, sum_down)[:2]
        in_far = ff_back(1 - c_me, d_in, w_down, far_gate, far_up)
        ff_far = mm(turned, in_far).astype(BF16)
        in_own = ff_back(c_me, after(d_in, ff_far), w_down, own_gate, own_up)
        ff_left, ff_right = forward_product(c_me, (after(act_own, in_own), act_far), w_down)
        in_own, ff_left, ff_right, ff_got = sync(in_own, ff_left, ff_right, links.c(ff_far))
        ff_l, ff_r = links.scatter_one(ff_left, ff_right)
        sum_ff = (mm(turned, in_own) + ff_got).astype(BF16)
        g_ff = over_planes(sum_ff)
        ff_l, ff_r, in_own, sum_ff = sync(ff_l, ff_r, in_own, sum_ff)
        ff_lf, ff_rf = links.scatter_two(ff_left, ff_right, ff_l, ff_r)
        g_down = over_planes(after(sum_down, sum_ff))
        dn_left, dn_right = back_product(c_me, (in_own, in_far), w_ff)
        dn_left, dn_right, ff_lf, ff_rf = sync(dn_left, dn_right, ff_lf, ff_rf)
        out_rows = (
            (hidden_one + links.scatter_end(ff_left, ff_right, ff_l, ff_r, ff_lf, ff_rf)) * valid
        ).astype(BF16)
        dn_l, dn_r, out_rows = sync(*links.scatter_one(dn_left, dn_right), out_rows)
        dn_lf, dn_rf = sync(*links.scatter_two(dn_left, dn_right, dn_l, dn_r))
        normed_two_grad = links.scatter_end(dn_left, dn_right, dn_l, dn_r, dn_lf, dn_rf)

        mid_upstream, midnorm_part = norm_backward(normed_two_grad, hidden_one, factor_mid, gain_mid)
        hidden_one_grad = down_in[:rows].astype(F32) + mid_upstream
        a_own = hidden_one_grad.astype(BF16)
        ax, ay = sync(*links.gather_one(a_own))
        dx, dy = sync(*links.gather_two(ax, ay))
        attn_in = jnp.concatenate([a_own, ax, ay, dx, dy], axis=0)
        attn_in, out_rows = sync(attn_in, out_rows)
        out_send = send_layout(out_rows)
        ff_parts = by_rank(after(g_ff, attn_in))
        first = c_me == 0
        attn_own = jnp.where(first, attn_in[:, :half], attn_in[:, half:])
        attn_far = jnp.where(first, attn_in[:, half:], attn_in[:, :half])
        out_far = far_part(mixed, attn_far)
        dq0, dq1, dk, dv = attend_back(
            after(attn_in, out_far), w_o, q0, q1, keys, values, lse, at_q, at_k, cos_t, sin_t
        )
        g_out = both_cores(mixed, after(attn_own, dq0), links.c(out_far))
        grad_even = jnp.concatenate([dq0, dk], axis=1)
        grad_odd = jnp.concatenate([dq1, dv], axis=1)
        normed_part = (
            mm_nt(after(grad_even, g_out), w_attn[0, :, : 2 * HEAD_SIZE])
            + mm_nt(grad_odd, w_attn[1, :, : 2 * HEAD_SIZE])
        ).astype(BF16)
        o_parts = spread(lambda t: lax.dynamic_slice(g_out, (0, t * eighth), (2 * HEAD_SIZE, eighth)))
        normed_part, out_send, grad_even, grad_odd, *o_parts = sync(
            normed_part, out_send, grad_even, grad_odd, *o_parts
        )
        np_left, np_right = normed_part[:, :half], normed_part[:, half:]
        np_l, np_r = links.scatter_one(np_left, np_right)
        got_out = exchange(out_send)
        g_o_cols = jnp.zeros((8 * HEAD_SIZE, eighth), BF16)
        for p, part in enumerate(o_parts):
            g_o_cols = lax.dynamic_update_slice(
                g_o_cols, part, (jnp.bitwise_xor(head, p) * 2 * HEAD_SIZE, 0)
            )
        d_own = jnp.where(first, grad_even, grad_odd)
        d_far = jnp.where(first, grad_odd, grad_even)
        g_qkv = both_cores(normed, d_own, links.c(far_part(normed, d_far)))
        attn_sum = jnp.concatenate([g_qkv, g_o_cols], axis=1)
        g_attn = over_planes(attn_sum)
        np_l, np_r, attn_sum, *ff_parts = sync(np_l, np_r, attn_sum, *ff_parts)
        np_lf, np_rf, got_out = sync(*links.scatter_two(np_left, np_right, np_l, np_r), got_out)
        normed_grad = links.scatter_end(np_left, np_right, np_l, np_r, np_lf, np_rf)
        pre_upstream, prenorm_part = norm_backward(normed_grad, hidden_zero, factor_pre, gain_pre)
        token_rows = ((hidden_one_grad + pre_upstream) * valid).astype(BF16)
        norm_plane = links.sum_plane(jnp.stack([prenorm_part, midnorm_part]))
        token_send, norm_plane = sync(send_layout(token_rows), norm_plane)
        got_grad = exchange(token_send)
        g_down = after(g_down, token_send)
        down_x = links.x(g_down)
        gate_gradient = place_columns(rank, ff_parts, planes, piece, 0)
        up_gradient = place_columns(rank, ff_parts, planes, piece, 1)
        out_tokens = to_stream(got_out)
        g_attn, down_x, gate_gradient, up_gradient, out_tokens = sync(
            g_attn, down_x, gate_gradient, up_gradient, out_tokens
        )
        attn_parts = by_rank(g_attn)
        norm_parts = links.sum_planes(norm_plane)
        down_gradient = place_rows(
            2 * x_me + c_me, [g_down, links.c(g_down), down_x, links.c(down_x)]
        )
        query_gradient, key_gradient, value_gradient, output_gradient = place_attention(
            rank, attn_parts
        )
        grad_tokens = to_stream(after(got_grad, down_gradient))
        norm_own = lax.dynamic_slice(
            norm_parts, (0, group_me * prenorm_gain.shape[0]), (2, prenorm_gain.shape[0])
        )
        return (
            out_tokens,
            grad_tokens,
            query_gradient,
            key_gradient,
            value_gradient,
            output_gradient,
            gate_gradient,
            up_gradient,
            down_gradient,
            norm_own[0],
            norm_own[1],
        )

    return body


def solution(mesh):
    planes = mesh.shape["fsdp"] // 2
    grid = Mesh(mesh.devices.reshape(planes, 2, 2, 2), AXES)
    rows = ("z", "y")
    stream = P(None, rows, ("x", "c"))
    weight = P(rows, None)
    gain = P(rows)
    return jax.shard_map(
        make_body(planes),
        mesh=grid,
        in_specs=(stream, stream) + (weight,) * 7 + (gain, gain, P(), P()),
        out_specs=(stream, stream) + (weight,) * 7 + (gain, gain),
        check_vma=False,
    )
```

time: 1220 us -> 860 us (0.70)
  Pallas kernels: 0 us -> 181 us
  matrix products: 204 us -> 61.3 us
  local copies, waits for them, and re-layouts: 221 us -> 79.6 us
  blocking collectives: 113 us -> 0 us
  other arithmetic: 155 us -> 46.2 us
  starting transfers between devices: 117 us -> 89.9 us
    pallas_call x0 -> x19, Pallas kernels: none -> 181 us  [the longest x2 28.2 us: ff_front(): pl.pallas_call(kernel, out_shape=(jax.ShapeDtypeStruct((m, f), F32), jax....]
    dot_general x42 -> x10, matrix products: 201 us -> 61.3 us  [dot(): return lax.dot_general(a, b, (dims, ((), ())), preferred_element_type=F32)]
    convert_element_type x20 -> x1, local copies, waits for them, and re-layouts: 79.2 us -> 0.02 us  [body(): links.gather_gains(jnp.stack([prenorm_gain, midnorm_gain])).astype(F32)]
    psum x1 -> x0, blocking collectives: 69.5 us -> none  [body(): norm_parts = lax.psum(jnp.stack([prenorm_part, midnorm_part]), AXES)]
    dynamic_update_slice x20 -> x11, local copies, waits for them, and re-layouts: 38.3 us -> 3 us  [the longest x4 2.88 us: body(): lax.dynamic_update_slice(g_o_cols, part, (jnp.bitwise_xor(head, p) * 2 *...]
    convert_element_type x15 -> x11, other arithmetic: 35 us -> 8.21 us  [the longest x4 4.27 us: scatter_two(): r_far = self.x((right[n:2 * n].astype(F32) + gr[1]).astype(BF16))]
    all_gather x1 -> x0, blocking collectives: 26.3 us -> none  [body(): lax.all_gather(gain_rows, ('z', 'y'), axis=1, tiled=True).astype(F32)]
    all_gather x0 -> x3, waiting for transfers between devices: none -> 25.2 us  [gather_planes(): got = lax.all_gather(a, ('c', 'z'), axis=0, tiled=True)]
  transfers between devices with their start and end apart: 85 -> 83, of which waited for: 33 -> 43; matrix products, arithmetic and copies ran while one was open for 38% -> 17% of each run, Pallas kernels for 0% -> 19%
where the time goes in v2:
time: 860 us; the launch traced here: 847 us
  waiting for transfers between devices  371 us (43%)
  Pallas kernels  181 us (21%)
  starting transfers between devices  89.9 us (10%)
  local copies, waits for them, and re-layouts  79.6 us (9%)
  matrix products  61.3 us (7%)
  other arithmetic  46.2 us (5%)
  between operations  18.5 us (2%)
    ppermute x23, waiting for transfers between devices, x(): return lax.ppermute(a, AXES, self.px)  117 us
    ppermute x23, waiting for transfers between devices, y(): return lax.ppermute(a, AXES, self.py)  99.3 us
    all_to_all x4, waiting for transfers between devices, exchange(): lax.all_to_all(send, ('z', 'c'), split_axis=0, concat_axis=0, tiled=True)  72.6 us
    dot_general x10, matrix products, dot(): return lax.dot_general(a, b, (dims, ((), ())), preferred_element_type=F32)  61.3 us
    unnamed x166, local copies, waits for them, and re-layouts  35 us
    pallas_call x2, Pallas kernels, ff_front(): pl.pallas_call(kernel, out_shape=(jax.ShapeDtypeStruct((m, f), F32), jax....  28.2 us
    ppermute x23, starting transfers between devices, x(): return lax.ppermute(a, AXES, self.px)  26.9 us
    all_gather x3, waiting for transfers between devices, gather_planes(): got = lax.all_gather(a, ('c', 'z'), axis=0, tiled=True)  25.2 us
  transfers between devices with their start and end apart: 83, of which 43 were waited for; matrix products, arithmetic and copies ran while one was open for 17% of the time, Pallas kernels for 19%

profile of v2, /device:TPU:0, one launch (start us, length us, event | category | flops | bytes accessed | tf_op | source)
XLA Modules:
  0.0 846.9 jit_solution(13083176871710881688)
XLA Ops:
  63.4 17.6 %collective-permute-done.6.refs_2_ = bf16[4,2,128,512]{3,2,1,0:T(8,128)(2,1)S(1)} collective-permute-done((bf16[4,2,128,512]{3,2,1,0:T(8,128)(2,1)S(1)}, bf16[4,2,128,512]{3,2,1,0:T(8,128)(2,1)S(1)}, u32[]{:S(2)}, u32[]{:S(2)}) %collective-permute-start.6) | collective-permute-done | bytes 1048608 | tf_op jit(solution)/shard_map/ppermute | solution.py:78
  84.9 18.6 %collective-permute-done.9 = bf16[256,2048]{1,0:T(8,128)(2,1)} collective-permute-done((bf16[256,2048]{1,0:T(8,128)(2,1)}, bf16[256,2048]{1,0:T(8,128)(2,1)}, u32[]{:S(2)}, u32[]{:S(2)}) %collective-permute-start.9) | collective-permute-done | bytes 1048608 | tf_op jit(solution)/shard_map/ppermute | solution.py:78
  116.0 9.8 %shard_map.213 = (bf16[1024,2048]{1,0:T(8,128)(2,1)}, bf16[256,2048]{1,0:T(8,128)(2,1)}) custom-call(s32[10]{0:T(128)} %concatenate.54.info_ref, bf16[4,2,128,512]{3,2,1,0:T(8,128)(2,1)} %bitcast.188, bf16[4,2,128,512]{3,2,1,0:T(8,128)(2,1)} %collective-permute-done.5.refs_1_, bf16[4,2,128,512]{3,2,1,0:T(8,128)(2,1)} %copy-done.42, ...), custom_call_target="tpu_custom_call" | custom-call | flops 262144 | bytes 655360 | tf_op jit(solution)/shard_map/pallas_call | solution.py:488
  174.6 23.6 %collective-permute-done.14 = bf16[2,256,1024]{2,1,0:T(8,128)(2,1)S(1)} collective-permute-done((bf16[2,256,1024]{2,1,0:T(8,128)(2,1)S(1)}, bf16[2,256,1024]{2,1,0:T(8,128)(2,1)S(1)}, u32[]{:S(2)}, u32[]{:S(2)}) %collective-permute-start.14) | collective-permute-done | bytes 1048608 | tf_op jit(solution)/shard_map/ppermute | solution.py:75
  223.7 38.9 %all-to-all-done.1 = bf16[8,128,512]{2,1,0:T(8,128)(2,1)} async-done(((bf16[8,128,512]{2,1,0:T(8,128)(2,1)}), bf16[8,128,512]{2,1,0:T(8,128)(2,1)}, u32[]{:S(2)}, u32[]{:S(2)}) %all-to-all-start.1) | async-done | bytes 1048608 | tf_op jit(solution)/shard_map/all_to_all | solution.py:828
  282.5 9.8 %all-gather.6.cloned.1.call-done = bf16[4096,2048]{1,0:T(8,128)(2,1)} async-done(((bf16[512,2048]{1,0:T(8,128)(2,1)}), bf16[4096,2048]{1,0:T(8,128)(2,1)}) %all-gather.6.cloned.1.call-update) | async-done | bytes 16777232 | tf_op jit(solution)/shard_map/all_gather | solution.py:126
  292.3 14.3 %shard_map.217 = (f32[1024,1024]{1,0:T(8,128)}, f32[1024,1024]{1,0:T(8,128)}, bf16[1024,1024]{1,0:T(8,128)(2,1)S(1)}) custom-call(s32[1]{0:T(128)} %bitcast.36.half_ref, bf16[1024,2048]{1,0:T(8,128)(2,1)} %constant_dynamic-update-slice_fusion.x, bf16[2,2048,2048]{2,1,0:T(8,128)(2,1)} %bitcast.169, bf16[2,2048,2048]{2,1,0:T(8,128)(2,1)} %bitcast.170), custom_call_target="tpu_custom_call" | custom-call | flops 536870912 | bytes 1441792 | tf_op jit(solution)/shard_map/pallas_call | solution.py:304
  313.2 13.9 %shard_map.218 = (f32[1024,1024]{1,0:T(8,128)}, f32[1024,1024]{1,0:T(8,128)}, bf16[1024,1024]{1,0:T(8,128)(2,1)S(1)}) custom-call(s32[1]{0:T(128)} %bitcast.38.half_ref.core_ref, bf16[1024,2048]{1,0:T(8,128)(2,1)} %constant_dynamic-update-slice_fusion.x, bf16[2,2048,2048]{2,1,0:T(8,128)(2,1)} %bitcast.171, bf16[2,2048,2048]{2,1,0:T(8,128)(2,1)} %bitcast.172), custom_call_target="tpu_custom_call" | custom-call | flops 536870912 | bytes 1441792 | tf_op jit(solution)/shard_map/pallas_call | solution.py:304
  358.8 15.4 %all-gather.8.cloned.1.call-done = bf16[2048,2048]{1,0:T(8,128)(2,1)} async-done(((bf16[256,2048]{1,0:T(8,128)(2,1)}), bf16[2048,2048]{1,0:T(8,128)(2,1)}) %all-gather.8.cloned.1.call-update) | async-done | bytes 8388624 | tf_op jit(solution)/shard_map/all_gather | solution.py:126
  374.1 10.8 %shard_map.220.a1 = bf16[1024,2048]{1,0:T(8,128)(2,1)S(1)} custom-call(s32[1]{0:T(128)} %bitcast.36.half_ref, bf16[1024,2048]{1,0:T(8,128)(2,1)} %shard_map.219.g, bf16[2,1024,2048]{2,1,0:T(8,128)(2,1)} %bitcast.177, f32[1024,1024]{1,0:T(8,128)} %get-tuple-element.201.gate_ref, f32[1024,1024]{1,0:T(8,128)} %get-tuple-element.202.up_ref), custom_call_target="tpu_custom_call" | custom-call | flops 268435456 | bytes 1310720 | tf_op jit(solution)/shard_map/pallas_call | solution.py:351
  384.9 11.6 %convolution_convert_fusion = bf16[2048,2048]{1,0:T(8,128)(2,1)} fusion(bf16[2048,1024]{0,1:T(8,128)(2,1)S(1)} %bitcast.183, bf16[1024,2048]{1,0:T(8,128)(2,1)S(1)} %shard_map.220.a1), kind=kOutput, calls=%fused_computation.3 | convolution fusion | flops 8594128896 | bytes 16777216 | tf_op jit(solution)/shard_map/dot_general | solution.py:24
  396.7 10.8 %shard_map.221.a0 = bf16[1024,2048]{1,0:T(8,128)(2,1)S(1)} custom-call(s32[1]{0:T(128)} %bitcast.38.half_ref.core_ref, bf16[1024,2048]{1,0:T(8,128)(2,1)} %shard_map.219.g, bf16[2,1024,2048]{2,1,0:T(8,128)(2,1)} %bitcast.178, f32[1024,1024]{1,0:T(8,128)} %get-tuple-element.204.gate_ref, f32[1024,1024]{1,0:T(8,128)} %get-tuple-element.205.up_ref), custom_call_target="tpu_custom_call" | custom-call | flops 268435456 | bytes 1310720 | tf_op jit(solution)/shard_map/pallas_call | solution.py:351
  407.5 13.1 %shard_map.222 = (bf16[1024,1024]{1,0:T(8,128)(2,1)S(1)}, bf16[1024,1024]{1,0:T(8,128)(2,1)S(1)}) custom-call(s32[1]{0:T(128)} %bitcast.38.half_ref.core_ref, bf16[1024,1024]{1,0:T(8,128)(2,1)S(1)} %copy-done.11, bf16[1024,1024]{1,0:T(8,128)(2,1)S(1)} %copy-done.8, bf16[2,1024,2048]{2,1,0:T(8,128)(2,1)} %bitcast.179, bf16[2,1024,2048]{2,1,0:T(8,128)(2,1)} %bitcast.180, ...), custom_call_target="tpu_custom_call" | custom-call | flops 536870912 | bytes 1048576 | tf_op jit(solution)/shard_map/pallas_call | solution.py:385
  423.3 13.7 %add_convert_fusion = bf16[2048,2048]{1,0:T(8,128)(2,1)} fusion(bf16[2048,2048]{1,0:T(8,128)(2,1)} %collective-permute-done.27, bf16[2048,1024]{0,1:T(8,128)(2,1)S(1)} %bitcast.184, bf16[1024,2048]{1,0:T(8,128)(2,1)S(1)} %shard_map.221.a0), kind=kOutput, calls=%fused_computation | convolution fusion | flops 8602517504 | bytes 25165824 | tf_op jit(solution)/shard_map/dot_general | solution.py:24
  442.6 22.3 %collective-permute-done.28 = bf16[2,256,1024]{2,1,0:T(8,128)(2,1)S(1)} collective-permute-done((bf16[2,256,1024]{2,1,0:T(8,128)(2,1)S(1)}, bf16[2,256,1024]{2,1,0:T(8,128)(2,1)S(1)}, u32[]{:S(2)}, u32[]{:S(2)}) %collective-permute-start.28) | collective-permute-done | bytes 1048608 | tf_op jit(solution)/shard_map/ppermute | solution.py:75
  469.4 23.9 %shard_map.223 = (bf16[1024,1024]{1,0:T(8,128)(2,1)S(1)}, bf16[1024,1024]{1,0:T(8,128)(2,1)S(1)}) custom-call(s32[1]{0:T(128)} %bitcast.38.half_ref.core_ref, bf16[1024,2048]{1,0:T(8,128)(2,1)} %copy-done.2, bf16[1024,2048]{1,0:T(8,128)(2,1)} %copy-done.1, bf16[2,2048,2048]{2,1,0:T(8,128)(2,1)} %bitcast.173, bf16[2,2048,2048]{2,1,0:T(8,128)(2,1)} %bitcast.174, ...), custom_call_target="tpu_custom_call" | custom-call | flops 1073741824 | bytes 1835008 | tf_op jit(solution)/shard_map/pallas_call | solution.py:267
  498.7 19.5 %collective-permute-done.32 = bf16[2,256,1024]{2,1,0:T(8,128)(2,1)S(1)} collective-permute-done((bf16[2,256,1024]{2,1,0:T(8,128)(2,1)S(1)}, bf16[2,256,1024]{2,1,0:T(8,128)(2,1)S(1)}, u32[]{:S(2)}, u32[]{:S(2)}) %collective-permute-start.32) | collective-permute-done | bytes 1048608 | tf_op jit(solution)/shard_map/ppermute | solution.py:75
  521.0 10.3 %collective-permute-done.35 = bf16[256,1024]{1,0:T(8,128)(2,1)S(1)} collective-permute-done((bf16[256,1024]{1,0:T(8,128)(2,1)S(1)}, bf16[256,1024]{1,0:T(8,128)(2,1)S(1)}, u32[]{:S(2)}, u32[]{:S(2)}) %collective-permute-start.35) | collective-permute-done | bytes 524320 | tf_op jit(solution)/shard_map/ppermute | solution.py:75
  538.2 19.6 %collective-permute-done.37 = bf16[256,2048]{1,0:T(8,128)(2,1)S(1)} collective-permute-done((bf16[256,2048]{1,0:T(8,128)(2,1)S(1)}, bf16[256,2048]{1,0:T(8,128)(2,1)S(1)}, u32[]{:S(2)}, u32[]{:S(2)}) %collective-permute-start.37) | collective-permute-done | bytes 1048608 | tf_op jit(solution)/shard_map/ppermute | solution.py:78
  581.8 13.1 %shard_map.224 = (bf16[1024,256]{1,0:T(8,128)(2,1)S(1)}, bf16[1024,256]{1,0:T(8,128)(2,1)S(1)}, bf16[1024,256]{1,0:T(8,128)(2,1)S(1)}, bf16[1024,256]{1,0:T(8,128)(2,1)S(1)}) custom-call(bf16[1024,2048]{1,0:T(8,128)(2,1)} %constant_dynamic-update-slice_fusion.5.g_ref, bf16[2,512,1024]{2,1,0:T(8,128)(2,1)} %copy-done, bf16[1024,256]{1,0:T(8,128)(2,1)S(1)} %copy-done.19, ...), custom_call_target="tpu_custom_call" | custom-call | flops 469762048 | bytes 720896 | tf_op jit(solution)/shard_map/pallas_call | solution.py:640
  653.2 23.2 %collective-permute-done.53.refs_6_ = bf16[256,2048]{1,0:T(8,128)(2,1)S(1)} collective-permute-done((bf16[256,2048]{1,0:T(8,128)(2,1)}, bf16[256,2048]{1,0:T(8,128)(2,1)S(1)}, u32[]{:S(2)}, u32[]{:S(2)}) %collective-permute-start.53) | collective-permute-done | bytes 1048608 | tf_op jit(solution)/shard_map/ppermute | solution.py:88
  685.2 12.4 %collective-permute-done.49.refs_2_ = bf16[256,2048]{1,0:T(8,128)(2,1)} collective-permute-done((bf16[256,2048]{1,0:T(8,128)(2,1)S(1)}, bf16[256,2048]{1,0:T(8,128)(2,1)}, u32[]{:S(2)}, u32[]{:S(2)}) %collective-permute-start.49) | collective-permute-done | bytes 1048608 | tf_op jit(solution)/shard_map/ppermute | solution.py:75
  711.5 33.7 %all-to-all-done.2.refs_0_ = bf16[8,128,512]{2,1,0:T(8,128)(2,1)} async-done(((bf16[8,128,512]{2,1,0:T(8,128)(2,1)}), bf16[8,128,512]{2,1,0:T(8,128)(2,1)}, u32[]{:S(2)}, u32[]{:S(2)}) %all-to-all-start.2) | async-done | bytes 1048608 | tf_op jit(solution)/shard_map/all_to_all | solution.py:828
  751.9 12.1 %collective-permute-done.59 = f32[2,2048]{1,0:T(2,128)S(1)} collective-permute-done((f32[2,2048]{1,0:T(2,128)S(1)}, f32[2,2048]{1,0:T(2,128)S(1)}, u32[]{:S(2)}, u32[]{:S(2)}) %collective-permute-start.59) | collective-permute-done | bytes 16416 | tf_op jit(solution)/shard_map/ppermute | solution.py:93
  (473 shorter events, 416.6 us)
Async XLA Ops:
  8.5 32.7 %collective-permute-start.1 = (bf16[2,256]{1,0:T(2,128)(2,1)S(1)}, bf16[2,256]{1,0:T(2,128)(2,1)S(1)}, u32[]{:S(2)}, u32[]{:S(2)}) collective-permute-start(bf16[2,256]{1,0:T(2,128)(2,1)S(1)} %pad_maximum_fusion.16), channel_id=1, source_target_pairs={{0,4},{1,5},{2,6},{3,7},{4,0},{5,1},{6,2},{7,3},{8,12},{9,13},{10,... | collective-permute-start | bytes 3080 | tf_op jit(solution)/shard_map/ppermute | solution.py:78
  22.3 32.5 %all-to-all-start = ((bf16[8,128,512]{2,1,0:T(8,128)(2,1)}), bf16[8,128,512]{2,1,0:T(8,128)(2,1)S(1)}, u32[]{:S(2)}, u32[]{:S(2)}) async-start(bf16[8,128,512]{2,1,0:T(8,128)(2,1)} %bitcast.190), calls=%async_computation | async-start | bytes 2097152 | tf_op jit(solution)/shard_map/all_to_all | solution.py:828
  26.8 105.0 %all-gather.4.cloned.1.call-start = ((), (), s32[]{:S(2)}) async-start(), calls=%async_computation.7 | async-start | bytes 7077888 | tf_op jit(solution)/shard_map/all_gather | solution.py:126
  54.8 237.5 %all-gather.6.cloned.1.call-start = ((), (), s32[]{:S(2)}) async-start(), calls=%async_computation.8 | async-start | bytes 18874368 | tf_op jit(solution)/shard_map/all_gather | solution.py:126
  57.3 46.3 %collective-permute-start.9 = (bf16[256,2048]{1,0:T(8,128)(2,1)}, bf16[256,2048]{1,0:T(8,128)(2,1)}, u32[]{:S(2)}, u32[]{:S(2)}) collective-permute-start(bf16[256,2048]{1,0:T(8,128)(2,1)} %get-tuple-element.157), channel_id=1, source_target_pairs={{0,4},{1,5},{2,6},{3,7},{4,0},{5,1},{6,2},{7,3},{8,12},{9,13},{10,... | collective-permute-start | bytes 3145736 | tf_op jit(solution)/shard_map/ppermute | solution.py:78
  84.0 29.4 %collective-permute-start.8 = (bf16[2,2,128,512]{3,2,1,0:T(8,128)(2,1)S(1)}, bf16[2,2,128,512]{3,2,1,0:T(8,128)(2,1)}, u32[]{:S(2)}, u32[]{:S(2)}) collective-permute-start(bf16[2,2,128,512]{3,2,1,0:T(8,128)(2,1)S(1)} %slice.238), channel_id=1, source_target_pairs={{0,4},{1,5},{2,6},{3,7},{4,0},{5,1},{6,2},{7,3},{8,12},{9,13},{10,... | collective-permute-start | bytes 1572872 | tf_op jit(solution)/shard_map/ppermute | solution.py:78
  113.4 260.7 %all-gather.8.cloned.1.call-start = ((), (), s32[]{:S(2)}) async-start(), calls=%async_computation.9 | async-start | bytes 9437184 | tf_op jit(solution)/shard_map/all_gather | solution.py:126
  203.3 59.2 %all-to-all-start.1 = ((bf16[8,128,512]{2,1,0:T(8,128)(2,1)}), bf16[8,128,512]{2,1,0:T(8,128)(2,1)}, u32[]{:S(2)}, u32[]{:S(2)}) async-start(bf16[8,128,512]{2,1,0:T(8,128)(2,1)} %bitcast.191), calls=%async_computation.1 | async-start | bytes 2097152 | tf_op jit(solution)/shard_map/all_to_all | solution.py:828
  207.6 424.5 %reduce-scatter.8.cloned.1.call-start = ((), (), s32[]{:S(2)}) async-start(), calls=%async_computation.12 | async-start | bytes 10485760 | tf_op jit(solution)/shard_map/reduce_scatter | solution.py:912
  221.6 40.9 %collective-permute-start.19 = (bf16[256,2048]{1,0:T(8,128)(2,1)}, bf16[256,2048]{1,0:T(8,128)(2,1)}, u32[]{:S(2)}, u32[]{:S(2)}) collective-permute-start(bf16[256,2048]{1,0:T(8,128)(2,1)} %get-tuple-element.287), channel_id=1, source_target_pairs={{0,4},{1,5},{2,6},{3,7},{4,0},{5,1},{6,2},{7,3},{8,12},{9,13},{10,... | collective-permute-start | bytes 3145736 | tf_op jit(solution)/shard_map/ppermute | solution.py:78
  222.9 39.7 %collective-permute-start.18 = (bf16[256,2048]{1,0:T(8,128)(2,1)}, bf16[256,2048]{1,0:T(8,128)(2,1)}, u32[]{:S(2)}, u32[]{:S(2)}) collective-permute-start(bf16[256,2048]{1,0:T(8,128)(2,1)} %get-tuple-element.287), channel_id=1, source_target_pairs={{0,2},{1,3},{2,0},{3,1},{4,6},{5,7},{6,4},{7,5},{8,10},{9,11},{10,... | collective-permute-start | bytes 3145736 | tf_op jit(solution)/shard_map/ppermute | solution.py:75
  437.0 333.0 %reduce-scatter.6.cloned.1.call-start = ((), (), s32[]{:S(2)}) async-start(), calls=%async_computation.11 | async-start | bytes 5242880 | tf_op jit(solution)/shard_map/reduce_scatter | solution.py:912
  562.7 231.0 %reduce-scatter.4.cloned.1.call-start = ((), (), s32[]{:S(2)}) async-start(), calls=%async_computation.10 | async-start | bytes 3932160 | tf_op jit(solution)/shard_map/reduce_scatter | solution.py:912
  634.9 41.4 %collective-permute-start.53 = (bf16[256,2048]{1,0:T(8,128)(2,1)}, bf16[256,2048]{1,0:T(8,128)(2,1)S(1)}, u32[]{:S(2)}, u32[]{:S(2)}) collective-permute-start(bf16[256,2048]{1,0:T(8,128)(2,1)} %get-tuple-element.314), channel_id=1, source_target_pairs={{0,6},{1,7},{2,4},{3,5},{4,2},{5,3},{6,0},{7,1},{8,14},{9,15},{10,... | collective-permute-start | bytes 3145736 | tf_op jit(solution)/shard_map/ppermute | solution.py:88
  636.5 48.7 %collective-permute-start.51 = (bf16[256,2048]{1,0:T(8,128)(2,1)}, bf16[256,2048]{1,0:T(8,128)(2,1)S(1)}, u32[]{:S(2)}, u32[]{:S(2)}) collective-permute-start(bf16[256,2048]{1,0:T(8,128)(2,1)} %get-tuple-element.314), channel_id=1, source_target_pairs={{0,4},{1,5},{2,6},{3,7},{4,0},{5,1},{6,2},{7,3},{8,12},{9,13},{10,... | collective-permute-start | bytes 3145736 | tf_op jit(solution)/shard_map/ppermute | solution.py:78
  637.2 60.5 %collective-permute-start.49 = (bf16[256,2048]{1,0:T(8,128)(2,1)S(1)}, bf16[256,2048]{1,0:T(8,128)(2,1)}, u32[]{:S(2)}, u32[]{:S(2)}) collective-permute-start(bf16[256,2048]{1,0:T(8,128)(2,1)S(1)} %get-tuple-element.257.refs_0_), channel_id=1, source_target_pairs={{0,2},{1,3},{2,0},{3,1},{4,6},{5,7},{6,4},{7,5},{8,10},{9,11},{10,... | collective-permute-start | bytes 3145736 | tf_op jit(solution)/shard_map/ppermute | solution.py:75
  648.2 58.4 %collective-permute-start.47 = (bf16[2,256,1024]{2,1,0:T(8,128)(2,1)}, bf16[2,256,1024]{2,1,0:T(8,128)(2,1)}, u32[]{:S(2)}, u32[]{:S(2)}) collective-permute-start(bf16[2,256,1024]{2,1,0:T(8,128)(2,1)} %bitcast.64), channel_id=1, source_target_pairs={{0,4},{1,5},{2,6},{3,7},{4,0},{5,1},{6,2},{7,3},{8,12},{9,13},{10,... | collective-permute-start | bytes 3145736 | tf_op jit(solution)/shard_map/ppermute | solution.py:78
  653.2 53.4 %collective-permute-start.48 = (bf16[256,2048]{1,0:T(8,128)(2,1)S(1)}, bf16[256,2048]{1,0:T(8,128)(2,1)}, u32[]{:S(2)}, u32[]{:S(2)}) collective-permute-start(bf16[256,2048]{1,0:T(8,128)(2,1)S(1)} %get-tuple-element.257.refs_0_), channel_id=1, source_target_pairs={{0,1},{1,0},{2,3},{3,2},{4,5},{5,4},{6,7},{7,6},{8,9},{9,8},{10,11... | collective-permute-start | bytes 3145736 | tf_op jit(solution)/shard_map/ppermute | solution.py:81
  676.4 30.2 %collective-permute-start.54 = (bf16[256,2048]{1,0:T(8,128)(2,1)S(1)}, bf16[256,2048]{1,0:T(8,128)(2,1)}, u32[]{:S(2)}, u32[]{:S(2)}) collective-permute-start(bf16[256,2048]{1,0:T(8,128)(2,1)S(1)} %collective-permute-done.53.refs_6_), channel_id=1, source_target_pairs={{0,1},{1,0},{2,3},{3,2},{4,5},{5,4},{6,7},{7,6},{8,9},{9,8},{10,11... | collective-permute-start | bytes 3145736 | tf_op jit(solution)/shard_map/ppermute | solution.py:81
  697.6 47.6 %all-to-all-start.2 = ((bf16[8,128,512]{2,1,0:T(8,128)(2,1)}), bf16[8,128,512]{2,1,0:T(8,128)(2,1)}, u32[]{:S(2)}, u32[]{:S(2)}) async-start(bf16[8,128,512]{2,1,0:T(8,128)(2,1)} %bitcast.189), calls=%async_computation.5 | async-start | bytes 2097152 | tf_op jit(solution)/shard_map/all_to_all | solution.py:828
  709.5 35.7 %collective-permute-start.56 = (bf16[256,1024]{1,0:T(8,128)(2,1)}, bf16[256,1024]{1,0:T(8,128)(2,1)S(1)}, u32[]{:S(2)}, u32[]{:S(2)}) collective-permute-start(bf16[256,1024]{1,0:T(8,128)(2,1)} %get-tuple-element.294), channel_id=1, source_target_pairs={{0,2},{1,3},{2,0},{3,1},{4,6},{5,7},{6,4},{7,5},{8,10},{9,11},{10,... | collective-permute-start | bytes 1572872 | tf_op jit(solution)/shard_map/ppermute | solution.py:75
  710.5 34.7 %collective-permute-start.55 = (bf16[256,1024]{1,0:T(8,128)(2,1)}, bf16[256,1024]{1,0:T(8,128)(2,1)S(1)}, u32[]{:S(2)}, u32[]{:S(2)}) collective-permute-start(bf16[256,1024]{1,0:T(8,128)(2,1)} %get-tuple-element.295), channel_id=1, source_target_pairs={{0,4},{1,5},{2,6},{3,7},{4,0},{5,1},{6,2},{7,3},{8,12},{9,13},{10,... | collective-permute-start | bytes 1572872 | tf_op jit(solution)/shard_map/ppermute | solution.py:78
  771.5 61.5 %all-to-all-start.3 = ((bf16[8,128,512]{2,1,0:T(8,128)(2,1)}), bf16[8,128,512]{2,1,0:T(8,128)(2,1)S(1)}, u32[]{:S(2)}, u32[]{:S(2)}) async-start(bf16[8,128,512]{2,1,0:T(8,128)(2,1)} %bitcast.73), calls=%async_computation.6 | async-start | bytes 2097152 | tf_op jit(solution)/shard_map/all_to_all | solution.py:828
  797.2 28.2 %collective-permute-start.63 = (bf16[256,2048]{1,0:T(8,128)(2,1)S(1)}, bf16[256,2048]{1,0:T(8,128)(2,1)}, u32[]{:S(2)}, u32[]{:S(2)}) collective-permute-start(bf16[256,2048]{1,0:T(8,128)(2,1)S(1)} %collective-permute-done.61.refs_2_), channel_id=1, source_target_pairs={{0,1},{1,0},{2,3},{3,2},{4,5},{5,4},{6,7},{7,6},{8,9},{9,8},{10,11... | collective-permute-start | bytes 3145736 | tf_op jit(solution)/shard_map/ppermute | solution.py:81
  (135 other events, 1665.0 us)
Sparse Core Ops, SparseCore 0:
  54.9 63.0 all-gather.3
  120.1 172.0 all-gather.5
  293.9 80.1 all-gather.7
  437.1 142.9 reduce-scatter.7
  582.3 77.4 reduce-scatter.5
  662.6 75.2 reduce-scatter.3

commit v3 on v2

--- a/solution.py
+++ b/solution.py
@@ -145,9 +145,9 @@
 
 def estimate(flops, bytes_accessed, transcendentals):
     return pl.CostEstimate(
-        flops=flops // 16,
-        bytes_accessed=bytes_accessed // 16,
-        transcendentals=transcendentals // 16,
+        flops=flops // 1,
+        bytes_accessed=bytes_accessed // 1,
+        transcendentals=transcendentals // 1,
     )
 
 
@@ -280,11 +280,41 @@
             ],
             out_specs=(out, out),
         ),
-        compiler_params=pltpu.CompilerParams(vmem_limit_bytes=48 << 20),
         cost_estimate=estimate(
             flops=4 * m * k * n, bytes_accessed=4 * (m + n) * k + 2 * m * n, transcendentals=0
         ),
     )(rank_scalar(core), *lefts, weight, weight, weight, weight)
+
+
+def weight_product(left, right, other=None):
+    m, k = left.shape
+    n = right.shape[1]
+    tile = 256
+
+    def kernel(a, b, *refs):
+        total = mm(a[...], b[...])
+        if other is not None:
+            total = total + refs[0][...]
+        refs[-1][...] = total.astype(BF16)
+
+    out = pl.BlockSpec((m, tile), lambda i: (0, i))
+    more = () if other is None else (other,)
+    return pl.pallas_call(
+        kernel,
+        out_shape=jax.ShapeDtypeStruct((m, n), BF16),
+        grid=(n // tile,),
+        in_specs=[
+            pl.BlockSpec((m, k), lambda i: (0, 0)),
+            pl.BlockSpec((k, tile), lambda i: (0, i)),
+        ]
+        + [out] * len(more),
+        out_specs=out,
+        cost_estimate=estimate(
+            flops=2 * m * k * n,
+            bytes_accessed=2 * (m * k + k * n + (1 + len(more)) * m * n),
+            transcendentals=0,
+        ),
+    )(left, right, *more)
 
 
 def ff_front(half, n2, weight):
@@ -318,7 +348,6 @@
             ],
             out_specs=(out, out, out),
         ),
-        compiler_params=pltpu.CompilerParams(vmem_limit_bytes=48 << 20),
         cost_estimate=estimate(
             flops=4 * m * d * f, bytes_accessed=2 * m * d + 4 * d * f + 10 * m * f, transcendentals=m * f
         ),
@@ -363,7 +392,6 @@
             out_specs=pl.BlockSpec((m, tile), lambda i, r: (0, i)),
             scratch_shapes=[pltpu.VMEM((steps, m, tile), BF16)],
         ),
-        compiler_params=pltpu.CompilerParams(vmem_limit_bytes=48 << 20),
         cost_estimate=estimate(
             flops=2 * m * d * f, bytes_accessed=2 * (m + f) * d + 12 * m * f, transcendentals=m * f
         ),
@@ -398,7 +426,6 @@
             ],
             out_specs=(out, out),
         ),
-        compiler_params=pltpu.CompilerParams(vmem_limit_bytes=40 << 20),
         cost_estimate=estimate(
             flops=4 * m * k * n, bytes_accessed=4 * (m + n) * k + 2 * m * n, transcendentals=0
         ),
@@ -429,6 +456,32 @@
             flops=0, bytes_accessed=4 * count * groups * r * f, transcendentals=0
         ),
     )(slot, has, *streams)
+
+
+def take_blocks(slot, has, got):
+    slots = slot.shape[0]
+    _, _, r, f = got.shape
+
+    def kernel(slot_ref, has_ref, x, a, b):
+        keep = has_ref[pl.program_id(0)] > 0
+        for i, out in enumerate((a, b)):
+            v = x[0, i]
+            out[0] = jnp.where(keep, v, jnp.zeros_like(v))
+
+    out = pl.BlockSpec((1, r, f), lambda g, s, h: (g, 0, 0))
+    return pl.pallas_call(
+        kernel,
+        out_shape=(jax.ShapeDtypeStruct((slots, r, f), BF16),) * 2,
+        grid_spec=pltpu.PrefetchScalarGridSpec(
+            num_scalar_prefetch=2,
+            grid=(slots,),
+            in_specs=[pl.BlockSpec((1, 2, r, f), lambda g, s, h: (s[g], 0, 0, 0))],
+            out_specs=(out, out),
+        ),
+        cost_estimate=estimate(
+            flops=0, bytes_accessed=8 * slots * r * f, transcendentals=0
+        ),
+    )(slot, has, got)
 
 
 def assemble_rows(info, pieces, gain=None):
@@ -532,7 +585,6 @@
             table,
         ],
         out_specs=(out,) * 4,
-        compiler_params=pltpu.CompilerParams(vmem_limit_bytes=40 << 20),
         cost_estimate=estimate(
             flops=8 * rows * width * h, bytes_accessed=2 * rows * width + 8 * width * h, transcendentals=0
         ),
@@ -585,7 +637,6 @@
             out_spec,
             out_spec,
         ),
-        compiler_params=pltpu.CompilerParams(vmem_limit_bytes=40 << 20),
         cost_estimate=estimate(
             flops=8 * rows * rows * h + 8 * rows * h * half,
             bytes_accessed=12 * rows * h + 8 * h * half + 4 * rows * half,
@@ -658,7 +709,6 @@
         ],
         out_specs=(q_spec, q_spec, kv_spec, kv_spec),
         scratch_shapes=[pltpu.VMEM((rows, h), F32), pltpu.VMEM((rows, h), F32)],
-        compiler_params=pltpu.CompilerParams(vmem_limit_bytes=48 << 20),
         cost_estimate=estimate(
             flops=20 * rows * rows * h + 8 * rows * h * half,
             bytes_accessed=20 * rows * h + 8 * h * half + 4 * rows * half,
@@ -767,26 +817,25 @@
         rows = 2 * blk
         valid = (positions[:rows] < my_len).astype(F32)[:, None]
 
-        def send_layout(out_rows):
+        def send_layout(out_rows, count):
             left, right = out_rows[:, : 2 * quarter], out_rows[:, 2 * quarter :]
             keep = jnp.where(x_me == 0, left, right)
             got = links.x(jnp.where(x_me == 0, right, left))
-            send = pair(x_me, keep, got).reshape(4, blk, 2, quarter)
-            send = jnp.transpose(send, (0, 2, 1, 3))
+            send = pair(x_me, keep, got).reshape(2, count, 2, blk, 2, quarter)
+            send = jnp.transpose(send, (0, 2, 4, 1, 3, 5)).reshape(4, 2, count, blk, quarter)
             if planes > 4:
-                send = jnp.pad(send, ((0, planes - 4), (0, 0), (0, 0), (0, 0)))
+                send = jnp.pad(send, ((0, planes - 4),) + ((0, 0),) * 4)
                 send = jnp.roll(send, plane_own, axis=0)
-            return send.reshape(groups, blk, quarter)
-
-        def to_stream(got):
-            return send_blocks(seq_of, taken, [got])[:, 0]
-
-        def by_rank(g):
+            return send.reshape(groups, count, blk, quarter)
+
+        def by_chip(g):
             n = g.shape[1]
             own = lax.dynamic_slice(g, (y_me * shard, 0), (shard, n))
             other = lax.dynamic_slice(g, ((1 - y_me) * shard, 0), (shard, n))
-            parts = links.swap_chips([own, own, other, other])
-            return [links.c(parts[p // 2]) if p % 2 else parts[p // 2] for p in range(8)]
+            return links.swap_chips([own, own, other, other])
+
+        def by_rank(chips):
+            return [links.c(chips[p // 2]) if p % 2 else chips[p // 2] for p in range(8)]
 
         def plane_rows(own_part, far_part):
             got = links.y(far_part)
@@ -914,24 +963,19 @@
         half = width // 2
         down_far = far_part(act_far, down_in)
         sum_down = both_cores(act_own, down_in, links.c(down_far))
+        g_down = over_planes(sum_down)
         w_down, d_in = sync(w_down, down_in, sum_down)[:2]
         in_far = ff_back(1 - c_me, d_in, w_down, far_gate, far_up)
-        ff_far = mm(turned, in_far).astype(BF16)
+        ff_far = weight_product(turned, in_far)
         in_own = ff_back(c_me, after(d_in, ff_far), w_down, own_gate, own_up)
         ff_left, ff_right = forward_product(c_me, (after(act_own, in_own), act_far), w_down)
         in_own, ff_left, ff_right, ff_got = sync(in_own, ff_left, ff_right, links.c(ff_far))
         ff_l, ff_r = links.scatter_one(ff_left, ff_right)
-        sum_ff = (mm(turned, in_own) + ff_got).astype(BF16)
+        sum_ff = weight_product(turned, in_own, ff_got)
         g_ff = over_planes(sum_ff)
-        ff_l, ff_r, in_own, sum_ff = sync(ff_l, ff_r, in_own, sum_ff)
-        ff_lf, ff_rf = links.scatter_two(ff_left, ff_right, ff_l, ff_r)
-        g_down = over_planes(after(sum_down, sum_ff))
-        dn_left, dn_right = back_product(c_me, (in_own, in_far), w_ff)
-        dn_left, dn_right, ff_lf, ff_rf = sync(dn_left, dn_right, ff_lf, ff_rf)
-        out_rows = (
-            (hidden_one + links.scatter_end(ff_left, ff_right, ff_l, ff_r, ff_lf, ff_rf)) * valid
-        ).astype(BF16)
-        dn_l, dn_r, out_rows = sync(*links.scatter_one(dn_left, dn_right), out_rows)
+        dn_left, dn_right = back_product(c_me, (after(in_own, sum_ff), in_far), w_ff)
+        dn_left, dn_right, ff_l, ff_r, g_down = sync(dn_left, dn_right, ff_l, ff_r, g_down)
+        dn_l, dn_r = sync(*links.scatter_one(dn_left, dn_right))
         dn_lf, dn_rf = sync(*links.scatter_two(dn_left, dn_right, dn_l, dn_r))
         normed_two_grad = links.scatter_end(dn_left, dn_right, dn_l, dn_r, dn_lf, dn_rf)
 
@@ -941,9 +985,11 @@
         ax, ay = sync(*links.gather_one(a_own))
         dx, dy = sync(*links.gather_two(ax, ay))
         attn_in = jnp.concatenate([a_own, ax, ay, dx, dy], axis=0)
-        attn_in, out_rows = sync(attn_in, out_rows)
-        out_send = send_layout(out_rows)
-        ff_parts = by_rank(after(g_ff, attn_in))
+        attn_in, g_down = sync(attn_in, g_down)
+        down_x = links.x(g_down)
+        ff_lf, ff_rf = links.scatter_two(
+            after(ff_left, attn_in), after(ff_right, attn_in), ff_l, ff_r
+        )
         first = c_me == 0
         attn_own = jnp.where(first, attn_in[:, :half], attn_in[:, half:])
         attn_far = jnp.where(first, attn_in[:, half:], attn_in[:, :half])
@@ -959,12 +1005,11 @@
             + mm_nt(grad_odd, w_attn[1, :, : 2 * HEAD_SIZE])
         ).astype(BF16)
         o_parts = spread(lambda t: lax.dynamic_slice(g_out, (0, t * eighth), (2 * HEAD_SIZE, eighth)))
-        normed_part, out_send, grad_even, grad_odd, *o_parts = sync(
-            normed_part, out_send, grad_even, grad_odd, *o_parts
+        normed_part, grad_even, grad_odd, ff_lf, ff_rf, down_x, *o_parts = sync(
+            normed_part, grad_even, grad_odd, ff_lf, ff_rf, down_x, *o_parts
         )
         np_left, np_right = normed_part[:, :half], normed_part[:, half:]
         np_l, np_r = links.scatter_one(np_left, np_right)
-        got_out = exchange(out_send)
         g_o_cols = jnp.zeros((8 * HEAD_SIZE, eighth), BF16)
         for p, part in enumerate(o_parts):
             g_o_cols = lax.dynamic_update_slice(
@@ -975,31 +1020,35 @@
         g_qkv = both_cores(normed, d_own, links.c(far_part(normed, d_far)))
         attn_sum = jnp.concatenate([g_qkv, g_o_cols], axis=1)
         g_attn = over_planes(attn_sum)
-        np_l, np_r, attn_sum, *ff_parts = sync(np_l, np_r, attn_sum, *ff_parts)
-        np_lf, np_rf, got_out = sync(*links.scatter_two(np_left, np_right, np_l, np_r), got_out)
+        np_l, np_r, attn_sum = sync(np_l, np_r, attn_sum)
+        np_lf, np_rf = sync(*links.scatter_two(np_left, np_right, np_l, np_r))
+        out_rows = (
+            (hidden_one + links.scatter_end(ff_left, ff_right, ff_l, ff_r, ff_lf, ff_rf)) * valid
+        ).astype(BF16)
         normed_grad = links.scatter_end(np_left, np_right, np_l, np_r, np_lf, np_rf)
         pre_upstream, prenorm_part = norm_backward(normed_grad, hidden_zero, factor_pre, gain_pre)
         token_rows = ((hidden_one_grad + pre_upstream) * valid).astype(BF16)
         norm_plane = links.sum_plane(jnp.stack([prenorm_part, midnorm_part]))
-        token_send, norm_plane = sync(send_layout(token_rows), norm_plane)
-        got_grad = exchange(token_send)
-        g_down = after(g_down, token_send)
-        down_x = links.x(g_down)
+        token_send, norm_plane = sync(
+            send_layout(jnp.concatenate([token_rows, out_rows], axis=0), 2), norm_plane
+        )
+        got = exchange(token_send)
+        *ff_chips, g_attn = sync(*by_chip(after(g_ff, token_send)), g_attn)
+        attn_chips = by_chip(g_attn)
+        ff_parts = by_rank(ff_chips)
+        down_gradient = place_rows(
+            2 * x_me + c_me, [g_down, links.c(g_down), down_x, links.c(down_x)]
+        )
         gate_gradient = place_columns(rank, ff_parts, planes, piece, 0)
         up_gradient = place_columns(rank, ff_parts, planes, piece, 1)
-        out_tokens = to_stream(got_out)
-        g_attn, down_x, gate_gradient, up_gradient, out_tokens = sync(
-            g_attn, down_x, gate_gradient, up_gradient, out_tokens
-        )
-        attn_parts = by_rank(g_attn)
+        *attn_chips, down_gradient, gate_gradient, up_gradient = sync(
+            *attn_chips, down_gradient, gate_gradient, up_gradient
+        )
         norm_parts = links.sum_planes(norm_plane)
-        down_gradient = place_rows(
-            2 * x_me + c_me, [g_down, links.c(g_down), down_x, links.c(down_x)]
-        )
         query_gradient, key_gradient, value_gradient, output_gradient = place_attention(
-            rank, attn_parts
-        )
-        grad_tokens = to_stream(after(got_grad, down_gradient))
+            rank, by_rank(attn_chips)
+        )
+        grad_tokens, out_tokens = take_blocks(seq_of, taken, got)
         norm_own = lax.dynamic_slice(
             norm_parts, (0, group_me * prenorm_gain.shape[0]), (2, prenorm_gain.shape[0])
         )

time: 860 us -> 820 us (0.953)
  Pallas kernels: 181 us -> 220 us
  waiting for transfers between devices: 371 us -> 333 us
  matrix products: 61.3 us -> 37.6 us
  local copies, waits for them, and re-layouts: 79.6 us -> 58.6 us
  other arithmetic: 46.2 us -> 56.1 us
    all_to_all x4 -> x3, waiting for transfers between devices: 72.6 us -> 35.7 us  [exchange(): lax.all_to_all(send, ('z', 'c'), split_axis=0, concat_axis=0, tiled=True)]
    pallas_call x0 -> x3, Pallas kernels: none -> 36.1 us  [the longest x2 29.7 us: weight_product(): pl.pallas_call(kernel, out_shape=jax.ShapeDtypeStruct((m, n), BF16), grid...]
    dot_general x10 -> x8, matrix products: 61.3 us -> 37.6 us  [dot(): return lax.dot_general(a, b, (dims, ((), ())), preferred_element_type=F32)]
    unnamed x166 -> x98, local copies, waits for them, and re-layouts: 35 us -> 19.6 us
    pallas_call x4 -> x2, Pallas kernels: 23.9 us -> 11.8 us  [send_blocks(): pl.pallas_call(kernel, out_shape=jax.ShapeDtypeStruct((groups, count, r,...]
    ppermute x3, waiting for transfers between devices: 14.3 us -> 24.7 us  [sum_plane(): a = a + lax.ppermute(a, AXES, p)]
    ppermute x23 -> x22, waiting for transfers between devices: 117 us -> 120 us  [x(): return lax.ppermute(a, AXES, self.px)]
    ppermute x23 -> x22, starting transfers between devices: 26.9 us -> 25.5 us  [x(): return lax.ppermute(a, AXES, self.px)]
  transfers between devices with their start and end apart: 83 -> 81, of which waited for: 43 -> 39; matrix products, arithmetic and copies ran while one was open for 17% -> 18% of each run, Pallas kernels for 19% -> 23%
where the time goes in v3:
time: 820 us; the launch traced here: 810 us
  waiting for transfers between devices  333 us (41%)
  Pallas kernels  220 us (27%)
  starting transfers between devices  86.5 us (11%)
  local copies, waits for them, and re-layouts  58.6 us (7%)
  other arithmetic  56.1 us (7%)
  matrix products  37.6 us (5%)
  between operations  18.5 us (2%)
    ppermute x22, waiting for transfers between devices, x(): return lax.ppermute(a, AXES, self.px)  120 us
    ppermute x23, waiting for transfers between devices, y(): return lax.ppermute(a, AXES, self.py)  95.5 us
    dot_general x8, matrix products, dot(): return lax.dot_general(a, b, (dims, ((), ())), preferred_element_type=F32)  37.6 us
    all_to_all x3, waiting for transfers between devices, exchange(): lax.all_to_all(send, ('z', 'c'), split_axis=0, concat_axis=0, tiled=True)  35.7 us
    pallas_call x2, Pallas kernels, weight_product(): pl.pallas_call(kernel, out_shape=jax.ShapeDtypeStruct((m, n), BF16), grid...  29.7 us
    pallas_call x2, Pallas kernels, ff_front(): pl.pallas_call(kernel, out_shape=(jax.ShapeDtypeStruct((m, f), F32), jax....  28.5 us
    ppermute x4, waiting for transfers between devices, swap_chips(): lax.ppermute(chunks[3], AXES, self.pxy)  27.3 us
    ppermute x23, starting transfers between devices, y(): return lax.ppermute(a, AXES, self.py)  25.8 us
  transfers between devices with their start and end apart: 81, of which 39 were waited for; matrix products, arithmetic and copies ran while one was open for 18% of the time, Pallas kernels for 23%

profile of v3, /device:TPU:0, one launch (start us, length us, event | category | flops | bytes accessed | tf_op | source)
XLA Modules:
  0.0 809.7 jit_solution(14295321920659689111)
XLA Ops:
  64.8 16.5 %collective-permute-done.6.refs_2_ = bf16[4,2,128,512]{3,2,1,0:T(8,128)(2,1)S(1)} collective-permute-done((bf16[4,2,128,512]{3,2,1,0:T(8,128)(2,1)S(1)}, bf16[4,2,128,512]{3,2,1,0:T(8,128)(2,1)S(1)}, u32[]{:S(2)}, u32[]{:S(2)}) %collective-permute-start.6) | collective-permute-done | bytes 1048608 | tf_op jit(solution)/shard_map/ppermute | solution.py:78
  83.5 20.4 %collective-permute-done.9 = bf16[256,2048]{1,0:T(8,128)(2,1)} collective-permute-done((bf16[256,2048]{1,0:T(8,128)(2,1)}, bf16[256,2048]{1,0:T(8,128)(2,1)}, u32[]{:S(2)}, u32[]{:S(2)}) %collective-permute-start.9) | collective-permute-done | bytes 1048608 | tf_op jit(solution)/shard_map/ppermute | solution.py:78
  122.1 10.4 %shard_map.213 = (bf16[1024,2048]{1,0:T(8,128)(2,1)}, bf16[256,2048]{1,0:T(8,128)(2,1)}) custom-call(s32[10]{0:T(128)} %concatenate.54.info_ref, bf16[4,2,128,512]{3,2,1,0:T(8,128)(2,1)} %bitcast.165, bf16[4,2,128,512]{3,2,1,0:T(8,128)(2,1)} %copy-done.10, bf16[4,2,128,512]{3,2,1,0:T(8,128)(2,1)} %copy-done.9, ...), custom_call_target="tpu_custom_call" | custom-call | flops 4194304 | bytes 10485760 | tf_op jit(solution)/shard_map/pallas_call | solution.py:541
  161.6 11.3 %shard_map.216 = (bf16[1024,512]{1,0:T(8,128)(2,1)}, f32[2,1024,1]{2,1,0:T(8,128)}, bf16[1024,1024]{1,0:T(8,128)(2,1)}, bf16[1024,1024]{1,0:T(8,128)(2,1)}) custom-call(bf16[1024,256]{1,0:T(8,128)(2,1)} %get-tuple-element.168.q0_ref, bf16[1024,256]{1,0:T(8,128)(2,1)} %get-tuple-element.169.q1_ref, bf16[1024,256]{1,0:T(8,128)(2,1)} %get-tuple-element.170.k_ref, ...), custom_call_target="tpu_custom_call" | custom-call | flops 4294967296 | bytes 9437184 | tf_op jit(solution)/shard_map/pallas_call | solution.py:616
  176.8 23.8 %collective-permute-done.14 = bf16[2,256,1024]{2,1,0:T(8,128)(2,1)S(1)} collective-permute-done((bf16[2,256,1024]{2,1,0:T(8,128)(2,1)S(1)}, bf16[2,256,1024]{2,1,0:T(8,128)(2,1)S(1)}, u32[]{:S(2)}, u32[]{:S(2)}) %collective-permute-start.14) | collective-permute-done | bytes 1048608 | tf_op jit(solution)/shard_map/ppermute | solution.py:75
  227.0 35.7 %all-to-all-done.1 = bf16[8,128,512]{2,1,0:T(8,128)(2,1)} async-done(((bf16[8,128,512]{2,1,0:T(8,128)(2,1)}), bf16[8,128,512]{2,1,0:T(8,128)(2,1)}, u32[]{:S(2)}, u32[]{:S(2)}) %all-to-all-start.1) | async-done | bytes 1048608 | tf_op jit(solution)/shard_map/all_to_all | solution.py:877
  292.3 14.5 %shard_map.217 = (f32[1024,1024]{1,0:T(8,128)}, f32[1024,1024]{1,0:T(8,128)}, bf16[1024,1024]{1,0:T(8,128)(2,1)}) custom-call(s32[1]{0:T(128)} %bitcast.36.half_ref, bf16[1024,2048]{1,0:T(8,128)(2,1)} %constant_dynamic-update-slice_fusion.x, bf16[2,2048,2048]{2,1,0:T(8,128)(2,1)} %bitcast.146, bf16[2,2048,2048]{2,1,0:T(8,128)(2,1)} %bitcast.147), custom_call_target="tpu_custom_call" | custom-call | flops 8589934592 | bytes 23068672 | tf_op jit(solution)/shard_map/pallas_call | solution.py:334
  312.8 14.0 %shard_map.218 = (f32[1024,1024]{1,0:T(8,128)}, f32[1024,1024]{1,0:T(8,128)}, bf16[1024,1024]{1,0:T(8,128)(2,1)}) custom-call(s32[1]{0:T(128)} %bitcast.38.half_ref.core_ref, bf16[1024,2048]{1,0:T(8,128)(2,1)} %constant_dynamic-update-slice_fusion.x, bf16[2,2048,2048]{2,1,0:T(8,128)(2,1)} %bitcast.148, bf16[2,2048,2048]{2,1,0:T(8,128)(2,1)} %bitcast.149), custom_call_target="tpu_custom_call" | custom-call | flops 8589934592 | bytes 23068672 | tf_op jit(solution)/shard_map/pallas_call | solution.py:334
  352.6 10.6 %add_convert_fusion.1 = bf16[1024,2048]{1,0:T(8,128)(2,1)} fusion(bf16[1024,2048]{1,0:T(8,128)(2,1)} %collective-permute-done.26, bf16[1024,1024]{1,0:T(8,128)(2,1)} %get-tuple-element.206.a0, bf16[1024,2048]{1,0:T(8,128)(2,1)} %shard_map.219.g), kind=kOutput, calls=%fused_computation.1 | convolution fusion | flops 4301258752 | bytes 14680064 | tf_op jit(solution)/shard_map/dot_general | solution.py:24
  363.2 10.9 %all-gather.8.cloned.1.call-done = bf16[2048,2048]{1,0:T(8,128)(2,1)} async-done(((bf16[256,2048]{1,0:T(8,128)(2,1)}), bf16[2048,2048]{1,0:T(8,128)(2,1)}) %all-gather.8.cloned.1.call-update) | async-done | bytes 8388624 | tf_op jit(solution)/shard_map/all_gather | solution.py:126
  374.1 12.7 %shard_map.220.b.a1 = bf16[1024,2048]{1,0:T(8,128)(2,1)} custom-call(s32[1]{0:T(128)} %bitcast.36.half_ref, bf16[1024,2048]{1,0:T(8,128)(2,1)} %shard_map.219.g, bf16[2,1024,2048]{2,1,0:T(8,128)(2,1)} %bitcast.154, f32[1024,1024]{1,0:T(8,128)} %get-tuple-element.201.gate_ref, f32[1024,1024]{1,0:T(8,128)} %get-tuple-element.202.up_ref), custom_call_target="tpu_custom_call" | custom-call | flops 4294967296 | bytes 20971520 | tf_op jit(solution)/shard_map/pallas_call | solution.py:380
  386.8 14.0 %shard_map.221 = bf16[2048,2048]{1,0:T(8,128)(2,1)} custom-call(bf16[2048,1024]{1,0:T(8,128)(2,1)} %copy.45.a, bf16[1024,2048]{1,0:T(8,128)(2,1)} %shard_map.220.b.a1), custom_call_target="tpu_custom_call" | custom-call | flops 8589934592 | bytes 16777216 | tf_op jit(solution)/shard_map/pallas_call | solution.py:302
  401.2 12.7 %shard_map.222.b.a0 = bf16[1024,2048]{1,0:T(8,128)(2,1)} custom-call(s32[1]{0:T(128)} %bitcast.38.half_ref.core_ref, bf16[1024,2048]{1,0:T(8,128)(2,1)} %shard_map.219.g, bf16[2,1024,2048]{2,1,0:T(8,128)(2,1)} %bitcast.155, f32[1024,1024]{1,0:T(8,128)} %get-tuple-element.204.gate_ref, f32[1024,1024]{1,0:T(8,128)} %get-tuple-element.205.up_ref), custom_call_target="tpu_custom_call" | custom-call | flops 4294967296 | bytes 20971520 | tf_op jit(solution)/shard_map/pallas_call | solution.py:380
  413.9 13.8 %shard_map.223 = (bf16[1024,1024]{1,0:T(8,128)(2,1)}, bf16[1024,1024]{1,0:T(8,128)(2,1)}) custom-call(s32[1]{0:T(128)} %bitcast.38.half_ref.core_ref, bf16[1024,1024]{1,0:T(8,128)(2,1)} %get-tuple-element.206.a0, bf16[1024,1024]{1,0:T(8,128)(2,1)} %get-tuple-element.197.a1, bf16[2,1024,2048]{2,1,0:T(8,128)(2,1)} %bitcast.156, ...), custom_call_target="tpu_custom_call" | custom-call | flops 8589934592 | bytes 16777216 | tf_op jit(solution)/shard_map/pallas_call | solution.py:413
  427.7 15.7 %shard_map.224 = bf16[2048,2048]{1,0:T(8,128)(2,1)} custom-call(bf16[2048,1024]{1,0:T(8,128)(2,1)} %copy.45.a, bf16[1024,2048]{1,0:T(8,128)(2,1)} %shard_map.222.b.a0, bf16[2048,2048]{1,0:T(8,128)(2,1)} %collective-permute-done.27.refs_0_), custom_call_target="tpu_custom_call" | custom-call | flops 8589934592 | bytes 25165824 | tf_op jit(solution)/shard_map/pallas_call | solution.py:302
  450.0 24.5 %shard_map.225 = (bf16[1024,1024]{1,0:T(8,128)(2,1)}, bf16[1024,1024]{1,0:T(8,128)(2,1)}) custom-call(s32[1]{0:T(128)} %bitcast.38.half_ref.core_ref, bf16[1024,2048]{1,0:T(8,128)(2,1)} %shard_map.222.b.a0, bf16[1024,2048]{1,0:T(8,128)(2,1)} %shard_map.220.b.a1, bf16[2,2048,2048]{2,1,0:T(8,128)(2,1)} %bitcast.150, bf16[2,2048,2048]{2,1,0:T(8,128)(2,1)} %bitcast.151, ...), custom_call_target="tpu_custom_call" | custom-call | flops 17179869184 | bytes 29360128 | tf_op jit(solution)/shard_map/pallas_call | solution.py:267
  481.7 22.0 %collective-permute-done.30 = bf16[2,256,1024]{2,1,0:T(8,128)(2,1)S(1)} collective-permute-done((bf16[2,256,1024]{2,1,0:T(8,128)(2,1)S(1)}, bf16[2,256,1024]{2,1,0:T(8,128)(2,1)S(1)}, u32[]{:S(2)}, u32[]{:S(2)}) %collective-permute-start.30) | collective-permute-done | bytes 1048608 | tf_op jit(solution)/shard_map/ppermute | solution.py:75
  507.4 10.6 %collective-permute-done.33 = bf16[256,1024]{1,0:T(8,128)(2,1)S(1)} collective-permute-done((bf16[256,1024]{1,0:T(8,128)(2,1)S(1)}, bf16[256,1024]{1,0:T(8,128)(2,1)S(1)}, u32[]{:S(2)}, u32[]{:S(2)}) %collective-permute-start.33) | collective-permute-done | bytes 524320 | tf_op jit(solution)/shard_map/ppermute | solution.py:75
  525.6 19.9 %collective-permute-done.35 = bf16[256,2048]{1,0:T(8,128)(2,1)S(1)} collective-permute-done((bf16[256,2048]{1,0:T(8,128)(2,1)S(1)}, bf16[256,2048]{1,0:T(8,128)(2,1)S(1)}, u32[]{:S(2)}, u32[]{:S(2)}) %collective-permute-start.35) | collective-permute-done | bytes 1048608 | tf_op jit(solution)/shard_map/ppermute | solution.py:78
  569.3 15.7 %shard_map.226 = (bf16[1024,256]{1,0:T(8,128)(2,1)}, bf16[1024,256]{1,0:T(8,128)(2,1)}, bf16[1024,256]{1,0:T(8,128)(2,1)}, bf16[1024,256]{1,0:T(8,128)(2,1)}) custom-call(bf16[1024,2048]{1,0:T(8,128)(2,1)} %copy-done.5, bf16[2,512,1024]{2,1,0:T(8,128)(2,1)} %pad_maximum_fusion.2.w_ref, bf16[1024,256]{1,0:T(8,128)(2,1)} %get-tuple-element.168.q0_ref, ...), custom_call_target="tpu_custom_call" | custom-call | flops 7516192768 | bytes 11534336 | tf_op jit(solution)/shard_map/pallas_call | solution.py:691
  623.5 18.4 %collective-permute-done.45 = bf16[2,256,1024]{2,1,0:T(8,128)(2,1)} collective-permute-done((bf16[2,256,1024]{2,1,0:T(8,128)(2,1)}, bf16[2,256,1024]{2,1,0:T(8,128)(2,1)}, u32[]{:S(2)}, u32[]{:S(2)}) %collective-permute-start.45) | collective-permute-done | bytes 1048608 | tf_op jit(solution)/shard_map/ppermute | solution.py:75
  667.7 20.4 %collective-permute-done.52 = f32[2,2048]{1,0:T(2,128)S(1)} collective-permute-done((f32[2,2048]{1,0:T(2,128)S(1)}, f32[2,2048]{1,0:T(2,128)S(1)}, u32[]{:S(2)}, u32[]{:S(2)}) %collective-permute-start.52) | collective-permute-done | bytes 16416 | tf_op jit(solution)/shard_map/ppermute | solution.py:93
  707.3 23.2 %collective-permute-done.56.refs_6_ = bf16[256,2048]{1,0:T(8,128)(2,1)} collective-permute-done((bf16[256,2048]{1,0:T(8,128)(2,1)}, bf16[256,2048]{1,0:T(8,128)(2,1)}, u32[]{:S(2)}, u32[]{:S(2)}) %collective-permute-start.56) | collective-permute-done | bytes 1048608 | tf_op jit(solution)/shard_map/ppermute | solution.py:88
  730.5 21.8 %collective-permute-done.55.refs_4_ = bf16[256,2048]{1,0:T(8,128)(2,1)} collective-permute-done((bf16[256,2048]{1,0:T(8,128)(2,1)}, bf16[256,2048]{1,0:T(8,128)(2,1)}, u32[]{:S(2)}, u32[]{:S(2)}) %collective-permute-start.55) | collective-permute-done | bytes 1048608 | tf_op jit(solution)/shard_map/ppermute | solution.py:78
  (396 shorter events, 377.9 us)
Async XLA Ops:
  8.5 32.6 %collective-permute-start.1 = (bf16[2,256]{1,0:T(2,128)(2,1)S(1)}, bf16[2,256]{1,0:T(2,128)(2,1)S(1)}, u32[]{:S(2)}, u32[]{:S(2)}) collective-permute-start(bf16[2,256]{1,0:T(2,128)(2,1)S(1)} %pad_maximum_fusion.16), channel_id=1, source_target_pairs={{0,4},{1,5},{2,6},{3,7},{4,0},{5,1},{6,2},{7,3},{8,12},{9,13},{10,... | collective-permute-start | bytes 3080 | tf_op jit(solution)/shard_map/ppermute | solution.py:78
  22.2 32.9 %all-to-all-start = ((bf16[8,128,512]{2,1,0:T(8,128)(2,1)}), bf16[8,128,512]{2,1,0:T(8,128)(2,1)S(1)}, u32[]{:S(2)}, u32[]{:S(2)}) async-start(bf16[8,128,512]{2,1,0:T(8,128)(2,1)} %bitcast.166), calls=%async_computation | async-start | bytes 2097152 | tf_op jit(solution)/shard_map/all_to_all | solution.py:877
  27.1 105.4 %all-gather.4.cloned.1.call-start = ((), (), s32[]{:S(2)}) async-start(), calls=%async_computation.6 | async-start | bytes 7077888 | tf_op jit(solution)/shard_map/all_gather | solution.py:126
  55.1 237.2 %all-gather.6.cloned.1.call-start = ((), (), s32[]{:S(2)}) async-start(), calls=%async_computation.7 | async-start | bytes 18874368 | tf_op jit(solution)/shard_map/all_gather | solution.py:126
  57.2 46.7 %collective-permute-start.9 = (bf16[256,2048]{1,0:T(8,128)(2,1)}, bf16[256,2048]{1,0:T(8,128)(2,1)}, u32[]{:S(2)}, u32[]{:S(2)}) collective-permute-start(bf16[256,2048]{1,0:T(8,128)(2,1)} %get-tuple-element.156), channel_id=1, source_target_pairs={{0,4},{1,5},{2,6},{3,7},{4,0},{5,1},{6,2},{7,3},{8,12},{9,13},{10,... | collective-permute-start | bytes 3145736 | tf_op jit(solution)/shard_map/ppermute | solution.py:78
  82.9 30.8 %collective-permute-start.8 = (bf16[2,2,128,512]{3,2,1,0:T(8,128)(2,1)S(1)}, bf16[2,2,128,512]{3,2,1,0:T(8,128)(2,1)}, u32[]{:S(2)}, u32[]{:S(2)}) collective-permute-start(bf16[2,2,128,512]{3,2,1,0:T(8,128)(2,1)S(1)} %slice.232), channel_id=1, source_target_pairs={{0,4},{1,5},{2,6},{3,7},{4,0},{5,1},{6,2},{7,3},{8,12},{9,13},{10,... | collective-permute-start | bytes 1572872 | tf_op jit(solution)/shard_map/ppermute | solution.py:78
  113.7 260.4 %all-gather.8.cloned.1.call-start = ((), (), s32[]{:S(2)}) async-start(), calls=%async_computation.8 | async-start | bytes 9437184 | tf_op jit(solution)/shard_map/all_gather | solution.py:126
  206.6 56.1 %all-to-all-start.1 = ((bf16[8,128,512]{2,1,0:T(8,128)(2,1)}), bf16[8,128,512]{2,1,0:T(8,128)(2,1)}, u32[]{:S(2)}, u32[]{:S(2)}) async-start(bf16[8,128,512]{2,1,0:T(8,128)(2,1)} %bitcast.21), calls=%async_computation.1 | async-start | bytes 2097152 | tf_op jit(solution)/shard_map/all_to_all | solution.py:877
  210.9 265.7 %reduce-scatter.4.cloned.1.call-start = ((), (), s32[]{:S(2)}) async-start(), calls=%async_computation.9 | async-start | bytes 5242880 | tf_op jit(solution)/shard_map/reduce_scatter | solution.py:961
  224.8 38.0 %collective-permute-start.19 = (bf16[256,2048]{1,0:T(8,128)(2,1)}, bf16[256,2048]{1,0:T(8,128)(2,1)S(1)}, u32[]{:S(2)}, u32[]{:S(2)}) collective-permute-start(bf16[256,2048]{1,0:T(8,128)(2,1)} %get-tuple-element.287), channel_id=1, source_target_pairs={{0,4},{1,5},{2,6},{3,7},{4,0},{5,1},{6,2},{7,3},{8,12},{9,13},{10,... | collective-permute-start | bytes 3145736 | tf_op jit(solution)/shard_map/ppermute | solution.py:78
  226.0 36.7 %collective-permute-start.18 = (bf16[256,2048]{1,0:T(8,128)(2,1)}, bf16[256,2048]{1,0:T(8,128)(2,1)}, u32[]{:S(2)}, u32[]{:S(2)}) collective-permute-start(bf16[256,2048]{1,0:T(8,128)(2,1)} %get-tuple-element.287), channel_id=1, source_target_pairs={{0,2},{1,3},{2,0},{3,1},{4,6},{5,7},{6,4},{7,5},{8,10},{9,11},{10,... | collective-permute-start | bytes 3145736 | tf_op jit(solution)/shard_map/ppermute | solution.py:75
  401.1 299.5 %reduce-scatter.6.cloned.1.call-start = ((), (), s32[]{:S(2)}) async-start(), calls=%async_computation.10 | async-start | bytes 10485760 | tf_op jit(solution)/shard_map/reduce_scatter | solution.py:961
  443.4 263.9 %reduce-scatter.8.cloned.1.call-start = ((), (), s32[]{:S(2)}) async-start(), calls=%async_computation.11 | async-start | bytes 3932160 | tf_op jit(solution)/shard_map/reduce_scatter | solution.py:961
  447.0 29.6 %collective-permute-start.28 = (bf16[2,256,1024]{2,1,0:T(8,128)(2,1)}, bf16[2,256,1024]{2,1,0:T(8,128)(2,1)S(1)}, u32[]{:S(2)}, u32[]{:S(2)}) collective-permute-start(bf16[2,256,1024]{2,1,0:T(8,128)(2,1)} %pad_maximum_fusion.8), channel_id=1, source_target_pairs={{0,2},{1,3},{2,0},{3,1},{4,6},{5,7},{6,4},{7,5},{8,10},{9,11},{10,... | collective-permute-start | bytes 3145736 | tf_op jit(solution)/shard_map/ppermute | solution.py:75
  448.5 28.1 %collective-permute-start.29 = (bf16[2,256,1024]{2,1,0:T(8,128)(2,1)}, bf16[2,256,1024]{2,1,0:T(8,128)(2,1)}, u32[]{:S(2)}, u32[]{:S(2)}) collective-permute-start(bf16[2,256,1024]{2,1,0:T(8,128)(2,1)} %bitcast.43), channel_id=1, source_target_pairs={{0,4},{1,5},{2,6},{3,7},{4,0},{5,1},{6,2},{7,3},{8,12},{9,13},{10,... | collective-permute-start | bytes 3145736 | tf_op jit(solution)/shard_map/ppermute | solution.py:78
  563.1 33.6 %collective-permute-start.40 = (bf16[256,1024]{1,0:T(8,128)(2,1)}, bf16[256,1024]{1,0:T(8,128)(2,1)}, u32[]{:S(2)}, u32[]{:S(2)}) collective-permute-start(bf16[256,1024]{1,0:T(8,128)(2,1)} %fusion.31), channel_id=1, source_target_pairs={{0,2},{1,3},{2,0},{3,1},{4,6},{5,7},{6,4},{7,5},{8,10},{9,11},{10,... | collective-permute-start | bytes 1572872 | tf_op jit(solution)/shard_map/ppermute | solution.py:75
  566.0 35.9 %collective-permute-start.39 = (bf16[256,1024]{1,0:T(8,128)(2,1)}, bf16[256,1024]{1,0:T(8,128)(2,1)}, u32[]{:S(2)}, u32[]{:S(2)}) collective-permute-start(bf16[256,1024]{1,0:T(8,128)(2,1)} %fusion.32), channel_id=1, source_target_pairs={{0,4},{1,5},{2,6},{3,7},{4,0},{5,1},{6,2},{7,3},{8,12},{9,13},{10,... | collective-permute-start | bytes 1572872 | tf_op jit(solution)/shard_map/ppermute | solution.py:78
  566.6 35.4 %collective-permute-start.41 = (bf16[256,2048]{1,0:T(8,128)(2,1)}, bf16[256,2048]{1,0:T(8,128)(2,1)}, u32[]{:S(2)}, u32[]{:S(2)}) collective-permute-start(bf16[256,2048]{1,0:T(8,128)(2,1)} %reduce-scatter.4.cloned.1.call-done.refs_0_), channel_id=1, source_target_pairs={{0,2},{1,3},{2,0},{3,1},{4,6},{5,7},{6,4},{7,5},{8,10},{9,11},{10,... | collective-permute-start | bytes 3145736 | tf_op jit(solution)/shard_map/ppermute | solution.py:75
  696.3 92.2 %all-to-all-start.2 = ((bf16[8,2,128,512]{3,2,1,0:T(8,128)(2,1)}), bf16[8,2,128,512]{3,2,1,0:T(8,128)(2,1)S(1)}, u32[]{:S(2)}, u32[]{:S(2)}) async-start(bf16[8,2,128,512]{3,2,1,0:T(8,128)(2,1)} %bitcast.162), calls=%async_computation.3 | async-start | bytes 4194304 | tf_op jit(solution)/shard_map/all_to_all | solution.py:877
  704.3 48.0 %collective-permute-start.55 = (bf16[256,2048]{1,0:T(8,128)(2,1)}, bf16[256,2048]{1,0:T(8,128)(2,1)}, u32[]{:S(2)}, u32[]{:S(2)}) collective-permute-start(bf16[256,2048]{1,0:T(8,128)(2,1)} %get-tuple-element.316), channel_id=1, source_target_pairs={{0,4},{1,5},{2,6},{3,7},{4,0},{5,1},{6,2},{7,3},{8,12},{9,13},{10,... | collective-permute-start | bytes 3145736 | tf_op jit(solution)/shard_map/ppermute | solution.py:78
  705.7 46.6 %collective-permute-start.54 = (bf16[256,2048]{1,0:T(8,128)(2,1)S(1)}, bf16[256,2048]{1,0:T(8,128)(2,1)}, u32[]{:S(2)}, u32[]{:S(2)}) collective-permute-start(bf16[256,2048]{1,0:T(8,128)(2,1)S(1)} %get-tuple-element.261.refs_0_), channel_id=1, source_target_pairs={{0,2},{1,3},{2,0},{3,1},{4,6},{5,7},{6,4},{7,5},{8,10},{9,11},{10,... | collective-permute-start | bytes 3145736 | tf_op jit(solution)/shard_map/ppermute | solution.py:75
  706.8 46.0 %collective-permute-start.60 = (bf16[256,2048]{1,0:T(8,128)(2,1)}, bf16[256,2048]{1,0:T(8,128)(2,1)}, u32[]{:S(2)}, u32[]{:S(2)}) collective-permute-start(bf16[256,2048]{1,0:T(8,128)(2,1)} %reduce-scatter.4.cloned.1.call-done.refs_0_), channel_id=1, source_target_pairs={{0,1},{1,0},{2,3},{3,2},{4,5},{5,4},{6,7},{7,6},{8,9},{9,8},{10,11... | collective-permute-start | bytes 3145736 | tf_op jit(solution)/shard_map/ppermute | solution.py:81
  706.8 46.5 %collective-permute-start.61 = (bf16[256,2048]{1,0:T(8,128)(2,1)}, bf16[256,2048]{1,0:T(8,128)(2,1)}, u32[]{:S(2)}, u32[]{:S(2)}) collective-permute-start(bf16[256,2048]{1,0:T(8,128)(2,1)} %collective-permute-done.41.refs_2_), channel_id=1, source_target_pairs={{0,1},{1,0},{2,3},{3,2},{4,5},{5,4},{6,7},{7,6},{8,9},{9,8},{10,11... | collective-permute-start | bytes 3145736 | tf_op jit(solution)/shard_map/ppermute | solution.py:81
  757.1 28.3 %collective-permute-start.59 = (bf16[256,768]{1,0:T(8,128)(2,1)}, bf16[256,768]{1,0:T(8,128)(2,1)}, u32[]{:S(2)}, u32[]{:S(2)}) collective-permute-start(bf16[256,768]{1,0:T(8,128)(2,1)} %get-tuple-element.343), channel_id=1, source_target_pairs={{0,6},{1,7},{2,4},{3,5},{4,2},{5,3},{6,0},{7,1},{8,14},{9,15},{10,... | collective-permute-start | bytes 1179656 | tf_op jit(solution)/shard_map/ppermute | solution.py:88
  (99 other events, 1480.2 us)
Sparse Core Ops, SparseCore 0:
  55.2 62.7 all-gather.3
  120.1 172.0 all-gather.5
  293.9 80.1 all-gather.7
  401.2 75.2 reduce-scatter.3
  479.5 144.9 reduce-scatter.5
  627.3 60.9 reduce-scatter.7

commit v4 on v3

--- a/solution.py
+++ b/solution.py
@@ -118,6 +118,7 @@
 
     def scatter_end(self, left, right, gl, gr, l_far, r_far):
         n = left.shape[0] // 4
+        gl, gr, l_far, r_far = sync(gl, gr, l_far, r_far)
         l_own = left[:n].astype(F32) + gl[0] + l_far
         r_own = right[:n].astype(F32) + gr[0] + r_far
         return jnp.concatenate([l_own, r_own], axis=1)
@@ -145,9 +146,7 @@
 
 def estimate(flops, bytes_accessed, transcendentals):
     return pl.CostEstimate(
-        flops=flops // 1,
-        bytes_accessed=bytes_accessed // 1,
-        transcendentals=transcendentals // 1,
+        flops=flops, bytes_accessed=bytes_accessed, transcendentals=transcendentals
     )
 
 
@@ -166,7 +165,7 @@
             part = part.reshape(n, planes, 1, piece).astype(F32)
             out = lax.dynamic_update_slice(out, part, (0, 0, jnp.bitwise_xor(rank, p), 0))
         return out.reshape(n, total)
-    tile = min(n, 64)
+    tile = min(n, 128)
 
     def kernel(rank_ref, *refs):
         out = refs[8]
@@ -191,32 +190,31 @@
 
 def place_rows(order, parts):
     n, d = parts[0].shape
-    tile = min(d, 256)
+    tile = min(n, 128)
 
     def kernel(order_ref, *refs):
-        out = refs[4]
         for p in range(4):
-            t = jnp.bitwise_xor(order_ref[0], p)
-            out[pl.ds(pl.multiple_of(t * n, 8), n), :] = refs[p][...].astype(F32)
-
-    return pl.pallas_call(
-        kernel,
-        out_shape=jax.ShapeDtypeStruct((4 * n, d), F32),
+            refs[4][jnp.bitwise_xor(order_ref[0], p)] = refs[p][...].astype(F32)
+
+    out = pl.pallas_call(
+        kernel,
+        out_shape=jax.ShapeDtypeStruct((4, n, d), F32),
         grid_spec=pltpu.PrefetchScalarGridSpec(
             num_scalar_prefetch=1,
-            grid=(d // tile,),
-            in_specs=[pl.BlockSpec((n, tile), lambda i, r: (0, i))] * 4,
-            out_specs=pl.BlockSpec((4 * n, tile), lambda i, r: (0, i)),
+            grid=(n // tile,),
+            in_specs=[pl.BlockSpec((tile, d), lambda i, r: (i, 0))] * 4,
+            out_specs=pl.BlockSpec((4, tile, d), lambda i, r: (0, i, 0)),
         ),
         cost_estimate=estimate(flops=0, bytes_accessed=24 * n * d, transcendentals=0),
     )(rank_scalar(order), *parts)
+    return out.reshape(4 * n, d)
 
 
 def place_attention(rank, parts):
     n, width = parts[0].shape
     h = HEAD_SIZE
     o = width - 2 * h
-    tile = min(n, 64)
+    tile = min(n, 128)
 
     def kernel(rank_ref, *refs):
         q_out, k_out, v_out, o_out = refs[8:]
@@ -432,56 +430,59 @@
     )(rank_scalar(core), *lefts, weight, weight, weight, weight)
 
 
-def send_blocks(slot, has, streams):
+def send_blocks(slot, has, stream):
     groups = slot.shape[0]
-    _, r, f = streams[0].shape
-    count = len(streams)
+    _, r, f = stream.shape
+    count = 8
 
     def kernel(slot_ref, has_ref, *refs):
-        keep = has_ref[pl.program_id(0)] > 0
         for i in range(count):
             v = refs[i][0]
-            refs[count][0, i] = jnp.where(keep, v, jnp.zeros_like(v))
-
-    return pl.pallas_call(
-        kernel,
-        out_shape=jax.ShapeDtypeStruct((groups, count, r, f), BF16),
+            keep = has_ref[pl.program_id(0) * count + i] > 0
+            refs[count][i] = jnp.where(keep, v, jnp.zeros_like(v))
+
+    return pl.pallas_call(
+        kernel,
+        out_shape=jax.ShapeDtypeStruct((groups, r, f), BF16),
         grid_spec=pltpu.PrefetchScalarGridSpec(
             num_scalar_prefetch=2,
-            grid=(groups,),
-            in_specs=[pl.BlockSpec((1, r, f), lambda g, s, h: (s[g], 0, 0))] * count,
-            out_specs=pl.BlockSpec((1, count, r, f), lambda g, s, h: (g, 0, 0, 0)),
-        ),
-        cost_estimate=estimate(
-            flops=0, bytes_accessed=4 * count * groups * r * f, transcendentals=0
-        ),
-    )(slot, has, *streams)
+            grid=(groups // count,),
+            in_specs=[
+                pl.BlockSpec((1, r, f), lambda g, s, h, i=i: (s[g * count + i], 0, 0))
+                for i in range(count)
+            ],
+            out_specs=pl.BlockSpec((count, r, f), lambda g, s, h: (g, 0, 0)),
+        ),
+        cost_estimate=estimate(flops=0, bytes_accessed=4 * groups * r * f, transcendentals=0),
+    )(slot, has, *[stream] * count)
 
 
 def take_blocks(slot, has, got):
     slots = slot.shape[0]
     _, _, r, f = got.shape
 
-    def kernel(slot_ref, has_ref, x, a, b):
-        keep = has_ref[pl.program_id(0)] > 0
-        for i, out in enumerate((a, b)):
-            v = x[0, i]
-            out[0] = jnp.where(keep, v, jnp.zeros_like(v))
-
-    out = pl.BlockSpec((1, r, f), lambda g, s, h: (g, 0, 0))
+    def kernel(slot_ref, has_ref, *refs):
+        for i in range(slots):
+            keep = has_ref[i] > 0
+            for k in range(2):
+                v = refs[i][0, k]
+                refs[slots + k][i] = jnp.where(keep, v, jnp.zeros_like(v))
+
+    out = pl.BlockSpec((slots, r, f), lambda g, s, h: (0, 0, 0))
     return pl.pallas_call(
         kernel,
         out_shape=(jax.ShapeDtypeStruct((slots, r, f), BF16),) * 2,
         grid_spec=pltpu.PrefetchScalarGridSpec(
             num_scalar_prefetch=2,
-            grid=(slots,),
-            in_specs=[pl.BlockSpec((1, 2, r, f), lambda g, s, h: (s[g], 0, 0, 0))],
+            grid=(1,),
+            in_specs=[
+                pl.BlockSpec((1, 2, r, f), lambda g, s, h, i=i: (s[i], 0, 0, 0))
+                for i in range(slots)
+            ],
             out_specs=(out, out),
         ),
-        cost_estimate=estimate(
-            flops=0, bytes_accessed=8 * slots * r * f, transcendentals=0
-        ),
-    )(slot, has, got)
+        cost_estimate=estimate(flops=0, bytes_accessed=8 * slots * r * f, transcendentals=0),
+    )(slot, has, *[got] * slots)
 
 
 def assemble_rows(info, pieces, gain=None):
@@ -817,21 +818,27 @@
         rows = 2 * blk
         valid = (positions[:rows] < my_len).astype(F32)[:, None]
 
-        def send_layout(out_rows, count):
+        def send_layout(out_rows):
             left, right = out_rows[:, : 2 * quarter], out_rows[:, 2 * quarter :]
             keep = jnp.where(x_me == 0, left, right)
             got = links.x(jnp.where(x_me == 0, right, left))
-            send = pair(x_me, keep, got).reshape(2, count, 2, blk, 2, quarter)
-            send = jnp.transpose(send, (0, 2, 4, 1, 3, 5)).reshape(4, 2, count, blk, quarter)
+            send = pair(x_me, keep, got).reshape(4, blk, 2, quarter)
+            send = jnp.transpose(send, (0, 2, 1, 3))
             if planes > 4:
-                send = jnp.pad(send, ((0, planes - 4),) + ((0, 0),) * 4)
+                send = jnp.pad(send, ((0, planes - 4), (0, 0), (0, 0), (0, 0)))
                 send = jnp.roll(send, plane_own, axis=0)
-            return send.reshape(groups, count, blk, quarter)
-
-        def by_chip(g):
+            return send.reshape(groups, blk, quarter)
+
+        def own_and_other(g):
             n = g.shape[1]
             own = lax.dynamic_slice(g, (y_me * shard, 0), (shard, n))
             other = lax.dynamic_slice(g, ((1 - y_me) * shard, 0), (shard, n))
+            return own, other
+
+        def after_both(two, later):
+            return sync(*two, later)[:2]
+
+        def by_chip(own, other):
             return links.swap_chips([own, own, other, other])
 
         def by_rank(chips):
@@ -864,8 +871,7 @@
         gains = links.gather_gains(jnp.stack([prenorm_gain, midnorm_gain])).astype(F32)
 
         def to_sequences(stream):
-            send = send_blocks(slot_of, has.astype(jnp.int32), [stream])
-            return send[:, 0]
+            return send_blocks(slot_of, has.astype(jnp.int32), stream)
 
         def arranged(got):
             got = got.reshape(planes, 2, blk, quarter)
@@ -965,18 +971,27 @@
         sum_down = both_cores(act_own, down_in, links.c(down_far))
         g_down = over_planes(sum_down)
         w_down, d_in = sync(w_down, down_in, sum_down)[:2]
+        ff_left, ff_right = forward_product(c_me, (act_own, act_far), w_down)
+        ff_left, ff_right, d_in = sync(ff_left, ff_right, d_in)
+        ff_l, ff_r = links.scatter_one(ff_left, ff_right)
         in_far = ff_back(1 - c_me, d_in, w_down, far_gate, far_up)
         ff_far = weight_product(turned, in_far)
+        ff_l, ff_r, ff_far, in_far = sync(ff_l, ff_r, ff_far, in_far)
+        ff_lf, ff_rf = links.scatter_two(ff_left, ff_right, ff_l, ff_r)
         in_own = ff_back(c_me, after(d_in, ff_far), w_down, own_gate, own_up)
-        ff_left, ff_right = forward_product(c_me, (after(act_own, in_own), act_far), w_down)
-        in_own, ff_left, ff_right, ff_got = sync(in_own, ff_left, ff_right, links.c(ff_far))
-        ff_l, ff_r = links.scatter_one(ff_left, ff_right)
+        dn_left, dn_right = back_product(c_me, (in_own, in_far), w_ff)
+        dn_left, dn_right, in_own, ff_lf, ff_rf, ff_got = sync(
+            dn_left, dn_right, in_own, ff_lf, ff_rf, links.c(ff_far)
+        )
+        dn_l, dn_r = links.scatter_one(dn_left, dn_right)
         sum_ff = weight_product(turned, in_own, ff_got)
+        dn_l, dn_r, sum_ff = sync(dn_l, dn_r, sum_ff)
         g_ff = over_planes(sum_ff)
-        dn_left, dn_right = back_product(c_me, (after(in_own, sum_ff), in_far), w_ff)
-        dn_left, dn_right, ff_l, ff_r, g_down = sync(dn_left, dn_right, ff_l, ff_r, g_down)
-        dn_l, dn_r = sync(*links.scatter_one(dn_left, dn_right))
-        dn_lf, dn_rf = sync(*links.scatter_two(dn_left, dn_right, dn_l, dn_r))
+        dn_lf, dn_rf = links.scatter_two(dn_left, dn_right, dn_l, dn_r)
+        out_rows = (
+            (hidden_one + links.scatter_end(ff_left, ff_right, ff_l, ff_r, ff_lf, ff_rf)) * valid
+        ).astype(BF16)
+        dn_lf, dn_rf, g_down, out_rows = sync(dn_lf, dn_rf, g_down, out_rows)
         normed_two_grad = links.scatter_end(dn_left, dn_right, dn_l, dn_r, dn_lf, dn_rf)
 
         mid_upstream, midnorm_part = norm_backward(normed_two_grad, hidden_one, factor_mid, gain_mid)
@@ -985,19 +1000,18 @@
         ax, ay = sync(*links.gather_one(a_own))
         dx, dy = sync(*links.gather_two(ax, ay))
         attn_in = jnp.concatenate([a_own, ax, ay, dx, dy], axis=0)
-        attn_in, g_down = sync(attn_in, g_down)
+        attn_in, g_down, out_rows = sync(attn_in, g_down, out_rows)
+        out_send = send_layout(out_rows)
         down_x = links.x(g_down)
-        ff_lf, ff_rf = links.scatter_two(
-            after(ff_left, attn_in), after(ff_right, attn_in), ff_l, ff_r
-        )
         first = c_me == 0
-        attn_own = jnp.where(first, attn_in[:, :half], attn_in[:, half:])
-        attn_far = jnp.where(first, attn_in[:, half:], attn_in[:, :half])
-        out_far = far_part(mixed, attn_far)
+        g_both = mm_tn(mixed, attn_in)
+        g_low, g_high = g_both[:, :half], g_both[:, half:]
+        out_far = jnp.where(first, g_high, g_low).astype(BF16)
+        out_own = jnp.where(first, g_low, g_high)
         dq0, dq1, dk, dv = attend_back(
             after(attn_in, out_far), w_o, q0, q1, keys, values, lse, at_q, at_k, cos_t, sin_t
         )
-        g_out = both_cores(mixed, after(attn_own, dq0), links.c(out_far))
+        g_out = (out_own + links.c(out_far)).astype(BF16)
         grad_even = jnp.concatenate([dq0, dk], axis=1)
         grad_odd = jnp.concatenate([dq1, dv], axis=1)
         normed_part = (
@@ -1005,8 +1019,8 @@
             + mm_nt(grad_odd, w_attn[1, :, : 2 * HEAD_SIZE])
         ).astype(BF16)
         o_parts = spread(lambda t: lax.dynamic_slice(g_out, (0, t * eighth), (2 * HEAD_SIZE, eighth)))
-        normed_part, grad_even, grad_odd, ff_lf, ff_rf, down_x, *o_parts = sync(
-            normed_part, grad_even, grad_odd, ff_lf, ff_rf, down_x, *o_parts
+        normed_part, grad_even, grad_odd, out_send, down_x, *o_parts = sync(
+            normed_part, grad_even, grad_odd, out_send, down_x, *o_parts
         )
         np_left, np_right = normed_part[:, :half], normed_part[:, half:]
         np_l, np_r = links.scatter_one(np_left, np_right)
@@ -1019,22 +1033,18 @@
         d_far = jnp.where(first, grad_odd, grad_even)
         g_qkv = both_cores(normed, d_own, links.c(far_part(normed, d_far)))
         attn_sum = jnp.concatenate([g_qkv, g_o_cols], axis=1)
+        np_l, np_r, attn_sum = sync(np_l, np_r, attn_sum)
         g_attn = over_planes(attn_sum)
-        np_l, np_r, attn_sum = sync(np_l, np_r, attn_sum)
         np_lf, np_rf = sync(*links.scatter_two(np_left, np_right, np_l, np_r))
-        out_rows = (
-            (hidden_one + links.scatter_end(ff_left, ff_right, ff_l, ff_r, ff_lf, ff_rf)) * valid
-        ).astype(BF16)
+        ff_rows = own_and_other(after(g_ff, np_l))
         normed_grad = links.scatter_end(np_left, np_right, np_l, np_r, np_lf, np_rf)
         pre_upstream, prenorm_part = norm_backward(normed_grad, hidden_zero, factor_pre, gain_pre)
         token_rows = ((hidden_one_grad + pre_upstream) * valid).astype(BF16)
         norm_plane = links.sum_plane(jnp.stack([prenorm_part, midnorm_part]))
-        token_send, norm_plane = sync(
-            send_layout(jnp.concatenate([token_rows, out_rows], axis=0), 2), norm_plane
-        )
-        got = exchange(token_send)
-        *ff_chips, g_attn = sync(*by_chip(after(g_ff, token_send)), g_attn)
-        attn_chips = by_chip(g_attn)
+        token_send, norm_plane, *ff_rows = sync(send_layout(token_rows), norm_plane, *ff_rows)
+        got = exchange(jnp.stack([token_send, out_send], axis=1))
+        *ff_chips, g_attn = sync(*by_chip(*after_both(ff_rows, token_send)), g_attn)
+        attn_chips = by_chip(*own_and_other(g_attn))
         ff_parts = by_rank(ff_chips)
         down_gradient = place_rows(
             2 * x_me + c_me, [g_down, links.c(g_down), down_x, links.c(down_x)]
@@ -1044,7 +1054,7 @@
         *attn_chips, down_gradient, gate_gradient, up_gradient = sync(
             *attn_chips, down_gradient, gate_gradient, up_gradient
         )
-        norm_parts = links.sum_planes(norm_plane)
+        norm_parts = links.sum_planes(after(norm_plane, attn_chips[1]))
         query_gradient, key_gradient, value_gradient, output_gradient = place_attention(
             rank, by_rank(attn_chips)
         )

time: 820 us -> 803 us (0.979)
  waiting for transfers between devices: 333 us -> 312 us
  Pallas kernels: 220 us -> 205 us
  local copies, waits for them, and re-layouts: 58.6 us -> 69.9 us
    ppermute x23, waiting for transfers between devices: 95.5 us -> 76.9 us  [y(): return lax.ppermute(a, AXES, self.py)]
    ppermute x3, waiting for transfers between devices: 24.7 us -> 15 us  [sum_plane(): a = a + lax.ppermute(a, AXES, p)]
    ppermute x22 -> x23, waiting for transfers between devices: 120 us -> 114 us  [x(): return lax.ppermute(a, AXES, self.px)]
    ppermute x22 -> x23, starting transfers between devices: 25.5 us -> 25.2 us  [x(): return lax.ppermute(a, AXES, self.px)]
    dot_general x8 -> x7, matrix products: 37.6 us -> 37.5 us  [dot(): return lax.dot_general(a, b, (dims, ((), ())), preferred_element_type=F32)]
  transfers between devices with their start and end apart: 81 -> 82, of which waited for: 39 -> 41; matrix products, arithmetic and copies ran while one was open for 18% -> 20% of each run, Pallas kernels for 23% -> 24%
where the time goes in v4:
time: 803 us; the launch traced here: 793 us
  waiting for transfers between devices  312 us (39%)
  Pallas kernels  205 us (26%)
  starting transfers between devices  86.2 us (11%)
  local copies, waits for them, and re-layouts  69.9 us (9%)
  other arithmetic  63.7 us (8%)
  matrix products  37.5 us (5%)
  between operations  18.5 us (2%)
    ppermute x23, waiting for transfers between devices, x(): return lax.ppermute(a, AXES, self.px)  114 us
    ppermute x23, waiting for transfers between devices, y(): return lax.ppermute(a, AXES, self.py)  76.9 us
    all_to_all x3, waiting for transfers between devices, exchange(): lax.all_to_all(send, ('z', 'c'), split_axis=0, concat_axis=0, tiled=True)  38.8 us
    dot_general x7, matrix products, dot(): return lax.dot_general(a, b, (dims, ((), ())), preferred_element_type=F32)  37.5 us
    pallas_call x2, Pallas kernels, weight_product(): pl.pallas_call(kernel, out_shape=jax.ShapeDtypeStruct((m, n), BF16), grid...  29.6 us
    pallas_call x2, Pallas kernels, ff_front(): pl.pallas_call(kernel, out_shape=(jax.ShapeDtypeStruct((m, f), F32), jax....  28.4 us
    ppermute x23, starting transfers between devices, y(): return lax.ppermute(a, AXES, self.py)  26 us
    pallas_call x2, Pallas kernels, ff_back(): pl.pallas_call(kernel, out_shape=jax.ShapeDtypeStruct((m, 2 * f), BF16),...  25.5 us
  transfers between devices with their start and end apart: 82, of which 41 were waited for; matrix products, arithmetic and copies ran while one was open for 20% of the time, Pallas kernels for 24%

profile of v4, /device:TPU:0, one launch (start us, length us, event | category | flops | bytes accessed | tf_op | source)
XLA Modules:
  0.0 793.0 jit_solution(775432733902285679)
XLA Ops:
  61.9 16.5 %collective-permute-done.6.refs_2_ = bf16[4,2,128,512]{3,2,1,0:T(8,128)(2,1)S(1)} collective-permute-done((bf16[4,2,128,512]{3,2,1,0:T(8,128)(2,1)S(1)}, bf16[4,2,128,512]{3,2,1,0:T(8,128)(2,1)S(1)}, u32[]{:S(2)}, u32[]{:S(2)}) %collective-permute-start.6) | collective-permute-done | bytes 1048608 | tf_op jit(solution)/shard_map/ppermute | solution.py:78
  80.5 20.4 %collective-permute-done.9 = bf16[256,2048]{1,0:T(8,128)(2,1)} collective-permute-done((bf16[256,2048]{1,0:T(8,128)(2,1)}, bf16[256,2048]{1,0:T(8,128)(2,1)}, u32[]{:S(2)}, u32[]{:S(2)}) %collective-permute-start.9) | collective-permute-done | bytes 1048608 | tf_op jit(solution)/shard_map/ppermute | solution.py:78
  116.4 9.9 %shard_map.213 = (bf16[1024,2048]{1,0:T(8,128)(2,1)}, bf16[256,2048]{1,0:T(8,128)(2,1)}) custom-call(s32[10]{0:T(128)} %concatenate.50.info_ref, bf16[4,2,128,512]{3,2,1,0:T(8,128)(2,1)} %bitcast.176, bf16[4,2,128,512]{3,2,1,0:T(8,128)(2,1)} %copy-done.12, bf16[4,2,128,512]{3,2,1,0:T(8,128)(2,1)} %copy-done.11, ...), custom_call_target="tpu_custom_call" | custom-call | flops 4194304 | bytes 10485760 | tf_op jit(solution)/shard_map/pallas_call | solution.py:542
  155.9 11.3 %shard_map.216 = (bf16[1024,512]{1,0:T(8,128)(2,1)}, f32[2,1024,1]{2,1,0:T(8,128)}, bf16[1024,1024]{1,0:T(8,128)(2,1)}, bf16[1024,1024]{1,0:T(8,128)(2,1)}) custom-call(bf16[1024,256]{1,0:T(8,128)(2,1)} %get-tuple-element.192.q0_ref, bf16[1024,256]{1,0:T(8,128)(2,1)} %get-tuple-element.193.q1_ref, bf16[1024,256]{1,0:T(8,128)(2,1)} %get-tuple-element.194.k_ref, ...), custom_call_target="tpu_custom_call" | custom-call | flops 4294967296 | bytes 9437184 | tf_op jit(solution)/shard_map/pallas_call | solution.py:617
  171.1 24.0 %collective-permute-done.14 = bf16[2,256,1024]{2,1,0:T(8,128)(2,1)S(1)} collective-permute-done((bf16[2,256,1024]{2,1,0:T(8,128)(2,1)S(1)}, bf16[2,256,1024]{2,1,0:T(8,128)(2,1)S(1)}, u32[]{:S(2)}, u32[]{:S(2)}) %collective-permute-start.14) | collective-permute-done | bytes 1048608 | tf_op jit(solution)/shard_map/ppermute | solution.py:75
  220.9 38.8 %all-to-all-done.1 = bf16[8,128,512]{2,1,0:T(8,128)(2,1)} async-done(((bf16[8,128,512]{2,1,0:T(8,128)(2,1)}), bf16[8,128,512]{2,1,0:T(8,128)(2,1)}, u32[]{:S(2)}, u32[]{:S(2)}) %all-to-all-start.1) | async-done | bytes 1048608 | tf_op jit(solution)/shard_map/all_to_all | solution.py:883
  279.3 10.0 %all-gather.6.cloned.1.call-done = bf16[4096,2048]{1,0:T(8,128)(2,1)} async-done(((bf16[512,2048]{1,0:T(8,128)(2,1)}), bf16[4096,2048]{1,0:T(8,128)(2,1)}) %all-gather.6.cloned.1.call-update) | async-done | bytes 16777232 | tf_op jit(solution)/shard_map/all_gather | solution.py:127
  289.3 14.4 %shard_map.217 = (f32[1024,1024]{1,0:T(8,128)}, f32[1024,1024]{1,0:T(8,128)}, bf16[1024,1024]{1,0:T(8,128)(2,1)}) custom-call(s32[1]{0:T(128)} %bitcast.34.half_ref, bf16[1024,2048]{1,0:T(8,128)(2,1)} %constant_dynamic-update-slice_fusion.x, bf16[2,2048,2048]{2,1,0:T(8,128)(2,1)} %bitcast.157, bf16[2,2048,2048]{2,1,0:T(8,128)(2,1)} %bitcast.158), custom_call_target="tpu_custom_call" | custom-call | flops 8589934592 | bytes 23068672 | tf_op jit(solution)/shard_map/pallas_call | solution.py:332
  309.8 14.0 %shard_map.218 = (f32[1024,1024]{1,0:T(8,128)}, f32[1024,1024]{1,0:T(8,128)}, bf16[1024,1024]{1,0:T(8,128)(2,1)}) custom-call(s32[1]{0:T(128)} %bitcast.36.half_ref.core_ref, bf16[1024,2048]{1,0:T(8,128)(2,1)} %constant_dynamic-update-slice_fusion.x, bf16[2,2048,2048]{2,1,0:T(8,128)(2,1)} %bitcast.159, bf16[2,2048,2048]{2,1,0:T(8,128)(2,1)} %bitcast.160), custom_call_target="tpu_custom_call" | custom-call | flops 8589934592 | bytes 23068672 | tf_op jit(solution)/shard_map/pallas_call | solution.py:332
  349.1 10.6 %add_convert_fusion.1 = bf16[1024,2048]{1,0:T(8,128)(2,1)} fusion(bf16[1024,2048]{1,0:T(8,128)(2,1)} %collective-permute-done.26, bf16[1024,1024]{1,0:T(8,128)(2,1)} %get-tuple-element.222.a0, bf16[1024,2048]{1,0:T(8,128)(2,1)} %shard_map.219.g), kind=kOutput, calls=%fused_computation.1 | convolution fusion | flops 4301258752 | bytes 14680064 | tf_op jit(solution)/shard_map/dot_general | solution.py:24
  359.7 11.5 %all-gather.8.cloned.1.call-done = bf16[2048,2048]{1,0:T(8,128)(2,1)} async-done(((bf16[256,2048]{1,0:T(8,128)(2,1)}), bf16[2048,2048]{1,0:T(8,128)(2,1)}) %all-gather.8.cloned.1.call-update) | async-done | bytes 8388624 | tf_op jit(solution)/shard_map/all_gather | solution.py:127
  371.2 13.7 %shard_map.220 = (bf16[1024,1024]{1,0:T(8,128)(2,1)}, bf16[1024,1024]{1,0:T(8,128)(2,1)}) custom-call(s32[1]{0:T(128)} %bitcast.36.half_ref.core_ref, bf16[1024,1024]{1,0:T(8,128)(2,1)} %get-tuple-element.222.a0, bf16[1024,1024]{1,0:T(8,128)(2,1)} %get-tuple-element.223.a1, bf16[2,1024,2048]{2,1,0:T(8,128)(2,1)} %bitcast.165, ...), custom_call_target="tpu_custom_call" | custom-call | flops 8589934592 | bytes 16777216 | tf_op jit(solution)/shard_map/pallas_call | solution.py:411
  391.4 12.6 %shard_map.221.b.a1 = bf16[1024,2048]{1,0:T(8,128)(2,1)} custom-call(s32[1]{0:T(128)} %bitcast.34.half_ref, bf16[1024,2048]{1,0:T(8,128)(2,1)} %shard_map.219.g, bf16[2,1024,2048]{2,1,0:T(8,128)(2,1)} %bitcast.169, f32[1024,1024]{1,0:T(8,128)} %get-tuple-element.234.gate_ref, f32[1024,1024]{1,0:T(8,128)} %get-tuple-element.235.up_ref), custom_call_target="tpu_custom_call" | custom-call | flops 4294967296 | bytes 20971520 | tf_op jit(solution)/shard_map/pallas_call | solution.py:378
  404.0 14.0 %shard_map.222 = bf16[2048,2048]{1,0:T(8,128)(2,1)} custom-call(bf16[2048,1024]{1,0:T(8,128)(2,1)} %copy.45.a, bf16[1024,2048]{1,0:T(8,128)(2,1)} %shard_map.221.b.a1), custom_call_target="tpu_custom_call" | custom-call | flops 8589934592 | bytes 16777216 | tf_op jit(solution)/shard_map/pallas_call | solution.py:300
  423.5 12.9 %shard_map.223.a0.b = bf16[1024,2048]{1,0:T(8,128)(2,1)} custom-call(s32[1]{0:T(128)} %bitcast.36.half_ref.core_ref, bf16[1024,2048]{1,0:T(8,128)(2,1)} %shard_map.219.g, bf16[2,1024,2048]{2,1,0:T(8,128)(2,1)} %bitcast.170, f32[1024,1024]{1,0:T(8,128)} %get-tuple-element.238.gate_ref, f32[1024,1024]{1,0:T(8,128)} %get-tuple-element.239.up_ref), custom_call_target="tpu_custom_call" | custom-call | flops 4294967296 | bytes 20971520 | tf_op jit(solution)/shard_map/pallas_call | solution.py:378
  436.4 24.2 %shard_map.224 = (bf16[1024,1024]{1,0:T(8,128)(2,1)}, bf16[1024,1024]{1,0:T(8,128)(2,1)}) custom-call(s32[1]{0:T(128)} %bitcast.36.half_ref.core_ref, bf16[1024,2048]{1,0:T(8,128)(2,1)} %shard_map.223.a0.b, bf16[1024,2048]{1,0:T(8,128)(2,1)} %shard_map.221.b.a1, bf16[2,2048,2048]{2,1,0:T(8,128)(2,1)} %bitcast.161, bf16[2,2048,2048]{2,1,0:T(8,128)(2,1)} %bitcast.162, ...), custom_call_target="tpu_custom_call" | custom-call | flops 17179869184 | bytes 29360128 | tf_op jit(solution)/shard_map/pallas_call | solution.py:265
  467.4 15.6 %shard_map.225 = bf16[2048,2048]{1,0:T(8,128)(2,1)} custom-call(bf16[2048,1024]{1,0:T(8,128)(2,1)} %copy.45.a, bf16[1024,2048]{1,0:T(8,128)(2,1)} %shard_map.223.a0.b, bf16[2048,2048]{1,0:T(8,128)(2,1)} %collective-permute-done.31.refs_0_), custom_call_target="tpu_custom_call" | custom-call | flops 8589934592 | bytes 25165824 | tf_op jit(solution)/shard_map/pallas_call | solution.py:300
  523.1 19.6 %collective-permute-done.37 = bf16[256,2048]{1,0:T(8,128)(2,1)S(1)} collective-permute-done((bf16[256,2048]{1,0:T(8,128)(2,1)S(1)}, bf16[256,2048]{1,0:T(8,128)(2,1)S(1)}, u32[]{:S(2)}, u32[]{:S(2)}) %collective-permute-start.37) | collective-permute-done | bytes 1048608 | tf_op jit(solution)/shard_map/ppermute | solution.py:78
  570.4 15.5 %shard_map.226 = (bf16[1024,256]{1,0:T(8,128)(2,1)}, bf16[1024,256]{1,0:T(8,128)(2,1)}, bf16[1024,256]{1,0:T(8,128)(2,1)}, bf16[1024,256]{1,0:T(8,128)(2,1)}) custom-call(bf16[1024,2048]{1,0:T(8,128)(2,1)} %constant_dynamic-update-slice_fusion.5.g_ref, bf16[2,512,1024]{2,1,0:T(8,128)(2,1)} %pad_maximum_fusion.2.w_ref, ...), custom_call_target="tpu_custom_call" | custom-call | flops 7516192768 | bytes 11534336 | tf_op jit(solution)/shard_map/pallas_call | solution.py:692
  626.5 18.6 %collective-permute-done.46 = bf16[2,256,1024]{2,1,0:T(8,128)(2,1)S(1)} collective-permute-done((bf16[2,256,1024]{2,1,0:T(8,128)(2,1)}, bf16[2,256,1024]{2,1,0:T(8,128)(2,1)S(1)}, u32[]{:S(2)}, u32[]{:S(2)}) %collective-permute-start.46) | collective-permute-done | bytes 1048608 | tf_op jit(solution)/shard_map/ppermute | solution.py:75
  649.1 11.2 %collective-permute-done.50 = bf16[256,1024]{1,0:T(8,128)(2,1)S(1)} collective-permute-done((bf16[256,1024]{1,0:T(8,128)(2,1)S(1)}, bf16[256,1024]{1,0:T(8,128)(2,1)S(1)}, u32[]{:S(2)}, u32[]{:S(2)}) %collective-permute-start.50) | collective-permute-done | bytes 524320 | tf_op jit(solution)/shard_map/ppermute | solution.py:75
  667.6 12.0 %collective-permute-done.53 = f32[2,2048]{1,0:T(2,128)S(1)} collective-permute-done((f32[2,2048]{1,0:T(2,128)S(1)}, f32[2,2048]{1,0:T(2,128)S(1)}, u32[]{:S(2)}, u32[]{:S(2)}) %collective-permute-start.53) | collective-permute-done | bytes 16416 | tf_op jit(solution)/shard_map/ppermute | solution.py:93
  707.4 12.5 %collective-permute-done.55.refs_2_ = bf16[256,2048]{1,0:T(8,128)(2,1)} collective-permute-done((bf16[256,2048]{1,0:T(8,128)(2,1)S(1)}, bf16[256,2048]{1,0:T(8,128)(2,1)}, u32[]{:S(2)}, u32[]{:S(2)}) %collective-permute-start.55) | collective-permute-done | bytes 1048608 | tf_op jit(solution)/shard_map/ppermute | solution.py:75
  719.9 22.2 %collective-permute-done.57.refs_6_ = bf16[256,2048]{1,0:T(8,128)(2,1)} collective-permute-done((bf16[256,2048]{1,0:T(8,128)(2,1)}, bf16[256,2048]{1,0:T(8,128)(2,1)}, u32[]{:S(2)}, u32[]{:S(2)}) %collective-permute-start.57) | collective-permute-done | bytes 1048608 | tf_op jit(solution)/shard_map/ppermute | solution.py:88
  (403 shorter events, 388.4 us)
Async XLA Ops:
  8.5 29.7 %collective-permute-start.1 = (bf16[2,256]{1,0:T(2,128)(2,1)S(1)}, bf16[2,256]{1,0:T(2,128)(2,1)S(1)}, u32[]{:S(2)}, u32[]{:S(2)}) collective-permute-start(bf16[2,256]{1,0:T(2,128)(2,1)S(1)} %pad_maximum_fusion.17), channel_id=1, source_target_pairs={{0,4},{1,5},{2,6},{3,7},{4,0},{5,1},{6,2},{7,3},{8,12},{9,13},{10,... | collective-permute-start | bytes 3080 | tf_op jit(solution)/shard_map/ppermute | solution.py:78
  19.3 32.8 %all-to-all-start = ((bf16[8,128,512]{2,1,0:T(8,128)(2,1)}), bf16[8,128,512]{2,1,0:T(8,128)(2,1)S(1)}, u32[]{:S(2)}, u32[]{:S(2)}) async-start(bf16[8,128,512]{2,1,0:T(8,128)(2,1)} %shard_map.212), calls=%async_computation | async-start | bytes 2097152 | tf_op jit(solution)/shard_map/all_to_all | solution.py:883
  24.2 102.1 %all-gather.4.cloned.1.call-start = ((), (), s32[]{:S(2)}) async-start(), calls=%async_computation.6 | async-start | bytes 7077888 | tf_op jit(solution)/shard_map/all_gather | solution.py:127
  52.2 237.2 %all-gather.6.cloned.1.call-start = ((), (), s32[]{:S(2)}) async-start(), calls=%async_computation.7 | async-start | bytes 18874368 | tf_op jit(solution)/shard_map/all_gather | solution.py:127
  54.3 46.7 %collective-permute-start.9 = (bf16[256,2048]{1,0:T(8,128)(2,1)}, bf16[256,2048]{1,0:T(8,128)(2,1)}, u32[]{:S(2)}, u32[]{:S(2)}) collective-permute-start(bf16[256,2048]{1,0:T(8,128)(2,1)} %get-tuple-element.180), channel_id=1, source_target_pairs={{0,4},{1,5},{2,6},{3,7},{4,0},{5,1},{6,2},{7,3},{8,12},{9,13},{10,... | collective-permute-start | bytes 3145736 | tf_op jit(solution)/shard_map/ppermute | solution.py:78
  80.0 30.8 %collective-permute-start.8 = (bf16[2,2,128,512]{3,2,1,0:T(8,128)(2,1)S(1)}, bf16[2,2,128,512]{3,2,1,0:T(8,128)(2,1)}, u32[]{:S(2)}, u32[]{:S(2)}) collective-permute-start(bf16[2,2,128,512]{3,2,1,0:T(8,128)(2,1)S(1)} %slice.236), channel_id=1, source_target_pairs={{0,4},{1,5},{2,6},{3,7},{4,0},{5,1},{6,2},{7,3},{8,12},{9,13},{10,... | collective-permute-start | bytes 1572872 | tf_op jit(solution)/shard_map/ppermute | solution.py:78
  110.8 260.4 %all-gather.8.cloned.1.call-start = ((), (), s32[]{:S(2)}) async-start(), calls=%async_computation.8 | async-start | bytes 9437184 | tf_op jit(solution)/shard_map/all_gather | solution.py:127
  200.8 59.0 %all-to-all-start.1 = ((bf16[8,128,512]{2,1,0:T(8,128)(2,1)}), bf16[8,128,512]{2,1,0:T(8,128)(2,1)}, u32[]{:S(2)}, u32[]{:S(2)}) async-start(bf16[8,128,512]{2,1,0:T(8,128)(2,1)} %shard_map.214), calls=%async_computation.1 | async-start | bytes 2097152 | tf_op jit(solution)/shard_map/all_to_all | solution.py:883
  205.1 296.7 %reduce-scatter.4.cloned.1.call-start = ((), (), s32[]{:S(2)}) async-start(), calls=%async_computation.9 | async-start | bytes 5242880 | tf_op jit(solution)/shard_map/reduce_scatter | solution.py:967
  219.3 40.5 %collective-permute-start.19 = (bf16[256,2048]{1,0:T(8,128)(2,1)}, bf16[256,2048]{1,0:T(8,128)(2,1)S(1)}, u32[]{:S(2)}, u32[]{:S(2)}) collective-permute-start(bf16[256,2048]{1,0:T(8,128)(2,1)} %get-tuple-element.335), channel_id=1, source_target_pairs={{0,4},{1,5},{2,6},{3,7},{4,0},{5,1},{6,2},{7,3},{8,12},{9,13},{10,... | collective-permute-start | bytes 3145736 | tf_op jit(solution)/shard_map/ppermute | solution.py:78
  220.1 39.6 %collective-permute-start.18 = (bf16[256,2048]{1,0:T(8,128)(2,1)}, bf16[256,2048]{1,0:T(8,128)(2,1)}, u32[]{:S(2)}, u32[]{:S(2)}) collective-permute-start(bf16[256,2048]{1,0:T(8,128)(2,1)} %get-tuple-element.335), channel_id=1, source_target_pairs={{0,2},{1,3},{2,0},{3,1},{4,6},{5,7},{6,4},{7,5},{8,10},{9,11},{10,... | collective-permute-start | bytes 3145736 | tf_op jit(solution)/shard_map/ppermute | solution.py:75
  388.4 29.6 %collective-permute-start.27 = (bf16[2,256,1024]{2,1,0:T(8,128)(2,1)}, bf16[2,256,1024]{2,1,0:T(8,128)(2,1)S(1)}, u32[]{:S(2)}, u32[]{:S(2)}) collective-permute-start(bf16[2,256,1024]{2,1,0:T(8,128)(2,1)} %pad_maximum_fusion.7), channel_id=1, source_target_pairs={{0,2},{1,3},{2,0},{3,1},{4,6},{5,7},{6,4},{7,5},{8,10},{9,11},{10,... | collective-permute-start | bytes 3145736 | tf_op jit(solution)/shard_map/ppermute | solution.py:75
  389.9 28.1 %collective-permute-start.28 = (bf16[2,256,1024]{2,1,0:T(8,128)(2,1)}, bf16[2,256,1024]{2,1,0:T(8,128)(2,1)}, u32[]{:S(2)}, u32[]{:S(2)}) collective-permute-start(bf16[2,256,1024]{2,1,0:T(8,128)(2,1)} %bitcast.41), channel_id=1, source_target_pairs={{0,4},{1,5},{2,6},{3,7},{4,0},{5,1},{6,2},{7,3},{8,12},{9,13},{10,... | collective-permute-start | bytes 3145736 | tf_op jit(solution)/shard_map/ppermute | solution.py:78
  418.0 42.6 %collective-permute-start.31 = (bf16[2048,2048]{1,0:T(8,128)(2,1)}, bf16[2048,2048]{1,0:T(8,128)(2,1)}, u32[]{:S(2)}, u32[]{:S(2)}) collective-permute-start(bf16[2048,2048]{1,0:T(8,128)(2,1)} %shard_map.222), channel_id=1, source_target_pairs={{0,1},{1,0},{2,3},{3,2},{4,5},{5,4},{6,7},{7,6},{8,9},{9,8},{10,11... | collective-permute-start | bytes 25165832 | tf_op jit(solution)/shard_map/ppermute | solution.py:81
  418.1 267.5 %reduce-scatter.6.cloned.1.call-start = ((), (), s32[]{:S(2)}) async-start(), calls=%async_computation.10 | async-start | bytes 10485760 | tf_op jit(solution)/shard_map/reduce_scatter | solution.py:967
  420.4 40.3 %collective-permute-start.30 = (bf16[256,1024]{1,0:T(8,128)(2,1)}, bf16[256,1024]{1,0:T(8,128)(2,1)}, u32[]{:S(2)}, u32[]{:S(2)}) collective-permute-start(bf16[256,1024]{1,0:T(8,128)(2,1)} %fusion.26), channel_id=1, source_target_pairs={{0,2},{1,3},{2,0},{3,1},{4,6},{5,7},{6,4},{7,5},{8,10},{9,11},{10,... | collective-permute-start | bytes 1572872 | tf_op jit(solution)/shard_map/ppermute | solution.py:75
  423.1 37.5 %collective-permute-start.29 = (bf16[256,1024]{1,0:T(8,128)(2,1)}, bf16[256,1024]{1,0:T(8,128)(2,1)}, u32[]{:S(2)}, u32[]{:S(2)}) collective-permute-start(bf16[256,1024]{1,0:T(8,128)(2,1)} %fusion.27), channel_id=1, source_target_pairs={{0,4},{1,5},{2,6},{3,7},{4,0},{5,1},{6,2},{7,3},{8,12},{9,13},{10,... | collective-permute-start | bytes 1572872 | tf_op jit(solution)/shard_map/ppermute | solution.py:78
  490.8 216.6 %reduce-scatter.8.cloned.1.call-start = ((), (), s32[]{:S(2)}) async-start(), calls=%async_computation.11 | async-start | bytes 3932160 | tf_op jit(solution)/shard_map/reduce_scatter | solution.py:967
  569.0 39.6 %collective-permute-start.42 = (bf16[256,2048]{1,0:T(8,128)(2,1)}, bf16[256,2048]{1,0:T(8,128)(2,1)}, u32[]{:S(2)}, u32[]{:S(2)}) collective-permute-start(bf16[256,2048]{1,0:T(8,128)(2,1)} %reduce-scatter.4.cloned.1.call-done.refs_0_), channel_id=1, source_target_pairs={{0,2},{1,3},{2,0},{3,1},{4,6},{5,7},{6,4},{7,5},{8,10},{9,11},{10,... | collective-permute-start | bytes 3145736 | tf_op jit(solution)/shard_map/ppermute | solution.py:75
  690.2 90.6 %all-to-all-start.2 = ((bf16[8,2,128,512]{3,2,1,0:T(8,128)(2,1)}), bf16[8,2,128,512]{3,2,1,0:T(8,128)(2,1)S(1)}, u32[]{:S(2)}, u32[]{:S(2)}) async-start(bf16[8,2,128,512]{3,2,1,0:T(8,128)(2,1)} %pad_maximum_fusion.5), calls=%async_computation.4 | async-start | bytes 4194304 | tf_op jit(solution)/shard_map/all_to_all | solution.py:883
  694.6 47.4 %collective-permute-start.57 = (bf16[256,2048]{1,0:T(8,128)(2,1)}, bf16[256,2048]{1,0:T(8,128)(2,1)}, u32[]{:S(2)}, u32[]{:S(2)}) collective-permute-start(bf16[256,2048]{1,0:T(8,128)(2,1)} %get-tuple-element.304), channel_id=1, source_target_pairs={{0,6},{1,7},{2,4},{3,5},{4,2},{5,3},{6,0},{7,1},{8,14},{9,15},{10,... | collective-permute-start | bytes 3145736 | tf_op jit(solution)/shard_map/ppermute | solution.py:88
  696.0 47.6 %collective-permute-start.56 = (bf16[256,2048]{1,0:T(8,128)(2,1)}, bf16[256,2048]{1,0:T(8,128)(2,1)}, u32[]{:S(2)}, u32[]{:S(2)}) collective-permute-start(bf16[256,2048]{1,0:T(8,128)(2,1)} %get-tuple-element.304), channel_id=1, source_target_pairs={{0,4},{1,5},{2,6},{3,7},{4,0},{5,1},{6,2},{7,3},{8,12},{9,13},{10,... | collective-permute-start | bytes 3145736 | tf_op jit(solution)/shard_map/ppermute | solution.py:78
  697.3 46.8 %collective-permute-start.61 = (bf16[256,2048]{1,0:T(8,128)(2,1)}, bf16[256,2048]{1,0:T(8,128)(2,1)}, u32[]{:S(2)}, u32[]{:S(2)}) collective-permute-start(bf16[256,2048]{1,0:T(8,128)(2,1)} %reduce-scatter.4.cloned.1.call-done.refs_0_), channel_id=1, source_target_pairs={{0,1},{1,0},{2,3},{3,2},{4,5},{5,4},{6,7},{7,6},{8,9},{9,8},{10,11... | collective-permute-start | bytes 3145736 | tf_op jit(solution)/shard_map/ppermute | solution.py:81
  697.3 49.3 %collective-permute-start.62 = (bf16[256,2048]{1,0:T(8,128)(2,1)}, bf16[256,2048]{1,0:T(8,128)(2,1)}, u32[]{:S(2)}, u32[]{:S(2)}) collective-permute-start(bf16[256,2048]{1,0:T(8,128)(2,1)} %collective-permute-done.42.refs_2_), channel_id=1, source_target_pairs={{0,1},{1,0},{2,3},{3,2},{4,5},{5,4},{6,7},{7,6},{8,9},{9,8},{10,11... | collective-permute-start | bytes 3145736 | tf_op jit(solution)/shard_map/ppermute | solution.py:81
  (100 other events, 1311.1 us)
Sparse Core Ops, SparseCore 0:
  52.3 62.7 all-gather.3
  117.2 172.0 all-gather.5
  290.9 80.1 all-gather.7
  418.3 73.5 reduce-scatter.3
  494.8 144.9 reduce-scatter.5
  645.4 62.0 reduce-scatter.7

commit v5 on v4

--- a/solution.py
+++ b/solution.py
@@ -835,9 +835,6 @@
             other = lax.dynamic_slice(g, ((1 - y_me) * shard, 0), (shard, n))
             return own, other
 
-        def after_both(two, later):
-            return sync(*two, later)[:2]
-
         def by_chip(own, other):
             return links.swap_chips([own, own, other, other])
 
@@ -1033,17 +1030,23 @@
         d_far = jnp.where(first, grad_odd, grad_even)
         g_qkv = both_cores(normed, d_own, links.c(far_part(normed, d_far)))
         attn_sum = jnp.concatenate([g_qkv, g_o_cols], axis=1)
-        np_l, np_r, attn_sum = sync(np_l, np_r, attn_sum)
+        np_l, np_r, attn_sum, ff_own, ff_other = sync(
+            np_l, np_r, attn_sum, *own_and_other(g_ff)
+        )
         g_attn = over_planes(attn_sum)
-        np_lf, np_rf = sync(*links.scatter_two(np_left, np_right, np_l, np_r))
-        ff_rows = own_and_other(after(g_ff, np_l))
+        np_lf, np_rf = links.scatter_two(np_left, np_right, np_l, np_r)
+        ff_x, ff_y = links.x(ff_own), links.y(ff_other)
+        np_lf, np_rf = sync(np_lf, np_rf)
         normed_grad = links.scatter_end(np_left, np_right, np_l, np_r, np_lf, np_rf)
         pre_upstream, prenorm_part = norm_backward(normed_grad, hidden_zero, factor_pre, gain_pre)
         token_rows = ((hidden_one_grad + pre_upstream) * valid).astype(BF16)
         norm_plane = links.sum_plane(jnp.stack([prenorm_part, midnorm_part]))
-        token_send, norm_plane, *ff_rows = sync(send_layout(token_rows), norm_plane, *ff_rows)
+        token_send, norm_plane, ff_x, ff_y, ff_own, ff_other = sync(
+            send_layout(token_rows), norm_plane, ff_x, ff_y, ff_own, ff_other
+        )
         got = exchange(jnp.stack([token_send, out_send], axis=1))
-        *ff_chips, g_attn = sync(*by_chip(*after_both(ff_rows, token_send)), g_attn)
+        ff_d, g_attn = sync(lax.ppermute(ff_other, AXES, links.pxy), g_attn)
+        ff_chips = [ff_own, ff_x, ff_y, ff_d]
         attn_chips = by_chip(*own_and_other(g_attn))
         ff_parts = by_rank(ff_chips)
         down_gradient = place_rows(

time: 803 us -> 800 us (level)
  waiting for transfers between devices: 312 us -> 296 us
    ppermute x0 -> x1, waiting for transfers between devices: none -> 24.4 us  [body(): ff_d, g_attn = sync(lax.ppermute(ff_other, AXES, links.pxy), g_attn)]
    ppermute x23, waiting for transfers between devices: 114 us -> 90.3 us  [x(): return lax.ppermute(a, AXES, self.px)]
    ppermute x4 -> x3, waiting for transfers between devices: 25.1 us -> 0.91 us  [swap_chips(): lax.ppermute(chunks[3], AXES, self.pxy)]
    ppermute x3, waiting for transfers between devices: 15 us -> 27.4 us  [sum_plane(): a = a + lax.ppermute(a, AXES, p)]
    unnamed x98 -> x102, local copies, waits for them, and re-layouts: 24.3 us -> 24.3 us
  transfers between devices with their start and end apart: 82 -> 82, of which waited for: 41 -> 37; matrix products, arithmetic and copies ran while one was open for 20% -> 21% of each run, Pallas kernels for 24% -> 24%
where the time goes in v5:
time: 800 us; the launch traced here: 790 us
  waiting for transfers between devices  296 us (37%)
  Pallas kernels  205 us (26%)
  starting transfers between devices  85.9 us (11%)
  local copies, waits for them, and re-layouts  75.1 us (9%)
  other arithmetic  66.2 us (8%)
  matrix products  42.4 us (5%)
  between operations  18.5 us (2%)
    ppermute x23, waiting for transfers between devices, x(): return lax.ppermute(a, AXES, self.px)  90.3 us
    ppermute x23, waiting for transfers between devices, y(): return lax.ppermute(a, AXES, self.py)  76.9 us
    dot_general x7, matrix products, dot(): return lax.dot_general(a, b, (dims, ((), ())), preferred_element_type=F32)  42.4 us
    all_to_all x3, waiting for transfers between devices, exchange(): lax.all_to_all(send, ('z', 'c'), split_axis=0, concat_axis=0, tiled=True)  38.9 us
    pallas_call x2, Pallas kernels, weight_product(): pl.pallas_call(kernel, out_shape=jax.ShapeDtypeStruct((m, n), BF16), grid...  29.6 us
    pallas_call x2, Pallas kernels, ff_front(): pl.pallas_call(kernel, out_shape=(jax.ShapeDtypeStruct((m, f), F32), jax....  28.4 us
    ppermute x3, waiting for transfers between devices, sum_plane(): a = a + lax.ppermute(a, AXES, p)  27.4 us
    ppermute x23, starting transfers between devices, y(): return lax.ppermute(a, AXES, self.py)  26.8 us
  transfers between devices with their start and end apart: 82, of which 37 were waited for; matrix products, arithmetic and copies ran while one was open for 21% of the time, Pallas kernels for 24%

profile of v5, /device:TPU:0, one launch (start us, length us, event | category | flops | bytes accessed | tf_op | source)
XLA Modules:
  0.0 789.8 jit_solution(12608402142470685488)
XLA Ops:
  61.9 16.5 %collective-permute-done.6.refs_2_ = bf16[4,2,128,512]{3,2,1,0:T(8,128)(2,1)S(1)} collective-permute-done((bf16[4,2,128,512]{3,2,1,0:T(8,128)(2,1)S(1)}, bf16[4,2,128,512]{3,2,1,0:T(8,128)(2,1)S(1)}, u32[]{:S(2)}, u32[]{:S(2)}) %collective-permute-start.6) | collective-permute-done | bytes 1048608 | tf_op jit(solution)/shard_map/ppermute | solution.py:78
  80.5 20.4 %collective-permute-done.9 = bf16[256,2048]{1,0:T(8,128)(2,1)} collective-permute-done((bf16[256,2048]{1,0:T(8,128)(2,1)}, bf16[256,2048]{1,0:T(8,128)(2,1)}, u32[]{:S(2)}, u32[]{:S(2)}) %collective-permute-start.9) | collective-permute-done | bytes 1048608 | tf_op jit(solution)/shard_map/ppermute | solution.py:78
  116.3 9.9 %shard_map.213 = (bf16[1024,2048]{1,0:T(8,128)(2,1)}, bf16[256,2048]{1,0:T(8,128)(2,1)}) custom-call(s32[10]{0:T(128)} %concatenate.50.info_ref, bf16[4,2,128,512]{3,2,1,0:T(8,128)(2,1)} %bitcast.176, bf16[4,2,128,512]{3,2,1,0:T(8,128)(2,1)} %copy-done.11, bf16[4,2,128,512]{3,2,1,0:T(8,128)(2,1)} %copy-done.10, ...), custom_call_target="tpu_custom_call" | custom-call | flops 4194304 | bytes 10485760 | tf_op jit(solution)/shard_map/pallas_call | solution.py:542
  145.2 8.9 %shard_map.215 = (bf16[1024,256]{1,0:T(8,128)(2,1)}, bf16[1024,256]{1,0:T(8,128)(2,1)}, bf16[1024,256]{1,0:T(8,128)(2,1)}, bf16[1024,256]{1,0:T(8,128)(2,1)}) custom-call(bf16[1024,2048]{1,0:T(8,128)(2,1)} %get-tuple-element.186.x_ref, bf16[2,2048,768]{2,1,0:T(8,128)(2,1)} %bitcast.181, f32[1024,128]{1,0:T(8,128)} %get-tuple-element.188.c_ref.ca_ref, ...), custom_call_target="tpu_custom_call" | custom-call | flops 4294967296 | bytes 8388608 | tf_op jit(solution)/shard_map/pallas_call | solution.py:578
  155.7 11.3 %shard_map.216 = (bf16[1024,512]{1,0:T(8,128)(2,1)}, f32[2,1024,1]{2,1,0:T(8,128)}, bf16[1024,1024]{1,0:T(8,128)(2,1)}, bf16[1024,1024]{1,0:T(8,128)(2,1)}) custom-call(bf16[1024,256]{1,0:T(8,128)(2,1)} %get-tuple-element.190.q0_ref, bf16[1024,256]{1,0:T(8,128)(2,1)} %get-tuple-element.191.q1_ref, bf16[1024,256]{1,0:T(8,128)(2,1)} %get-tuple-element.192.k_ref, ...), custom_call_target="tpu_custom_call" | custom-call | flops 4294967296 | bytes 9437184 | tf_op jit(solution)/shard_map/pallas_call | solution.py:617
  170.8 24.0 %collective-permute-done.14 = bf16[2,256,1024]{2,1,0:T(8,128)(2,1)S(1)} collective-permute-done((bf16[2,256,1024]{2,1,0:T(8,128)(2,1)S(1)}, bf16[2,256,1024]{2,1,0:T(8,128)(2,1)S(1)}, u32[]{:S(2)}, u32[]{:S(2)}) %collective-permute-start.14) | collective-permute-done | bytes 1048608 | tf_op jit(solution)/shard_map/ppermute | solution.py:75
  220.8 38.9 %all-to-all-done.1 = bf16[8,128,512]{2,1,0:T(8,128)(2,1)} async-done(((bf16[8,128,512]{2,1,0:T(8,128)(2,1)}), bf16[8,128,512]{2,1,0:T(8,128)(2,1)}, u32[]{:S(2)}, u32[]{:S(2)}) %all-to-all-start.1) | async-done | bytes 1048608 | tf_op jit(solution)/shard_map/all_to_all | solution.py:880
  279.2 10.1 %all-gather.6.cloned.1.call-done = bf16[4096,2048]{1,0:T(8,128)(2,1)} async-done(((bf16[512,2048]{1,0:T(8,128)(2,1)}), bf16[4096,2048]{1,0:T(8,128)(2,1)}) %all-gather.6.cloned.1.call-update) | async-done | bytes 16777232 | tf_op jit(solution)/shard_map/all_gather | solution.py:127
  289.3 14.5 %shard_map.217 = (f32[1024,1024]{1,0:T(8,128)}, f32[1024,1024]{1,0:T(8,128)}, bf16[1024,1024]{1,0:T(8,128)(2,1)}) custom-call(s32[1]{0:T(128)} %bitcast.34.half_ref, bf16[1024,2048]{1,0:T(8,128)(2,1)} %constant_dynamic-update-slice_fusion.x, bf16[2,2048,2048]{2,1,0:T(8,128)(2,1)} %bitcast.157, bf16[2,2048,2048]{2,1,0:T(8,128)(2,1)} %bitcast.158), custom_call_target="tpu_custom_call" | custom-call | flops 8589934592 | bytes 23068672 | tf_op jit(solution)/shard_map/pallas_call | solution.py:332
  309.8 14.0 %shard_map.218 = (f32[1024,1024]{1,0:T(8,128)}, f32[1024,1024]{1,0:T(8,128)}, bf16[1024,1024]{1,0:T(8,128)(2,1)}) custom-call(s32[1]{0:T(128)} %bitcast.36.half_ref.core_ref, bf16[1024,2048]{1,0:T(8,128)(2,1)} %constant_dynamic-update-slice_fusion.x, bf16[2,2048,2048]{2,1,0:T(8,128)(2,1)} %bitcast.159, bf16[2,2048,2048]{2,1,0:T(8,128)(2,1)} %bitcast.160), custom_call_target="tpu_custom_call" | custom-call | flops 8589934592 | bytes 23068672 | tf_op jit(solution)/shard_map/pallas_call | solution.py:332
  332.3 9.4 %convolution_convert_fusion = bf16[1024,2048]{1,0:T(8,128)(2,1)} fusion(bf16[1024,1024]{1,0:T(8,128)(2,1)} %get-tuple-element.221.a1, bf16[1024,2048]{1,0:T(8,128)(2,1)} %shard_map.219.g), kind=kOutput, calls=%fused_computation.8 | convolution fusion | flops 4297064448 | bytes 10485760 | tf_op jit(solution)/shard_map/dot_general | solution.py:24
  349.2 10.6 %add_convert_fusion.1 = bf16[1024,2048]{1,0:T(8,128)(2,1)} fusion(bf16[1024,2048]{1,0:T(8,128)(2,1)} %collective-permute-done.26, bf16[1024,1024]{1,0:T(8,128)(2,1)} %get-tuple-element.220.a0, bf16[1024,2048]{1,0:T(8,128)(2,1)} %shard_map.219.g), kind=kOutput, calls=%fused_computation.1 | convolution fusion | flops 4301258752 | bytes 14680064 | tf_op jit(solution)/shard_map/dot_general | solution.py:24
  359.7 11.4 %all-gather.8.cloned.1.call-done = bf16[2048,2048]{1,0:T(8,128)(2,1)} async-done(((bf16[256,2048]{1,0:T(8,128)(2,1)}), bf16[2048,2048]{1,0:T(8,128)(2,1)}) %all-gather.8.cloned.1.call-update) | async-done | bytes 8388624 | tf_op jit(solution)/shard_map/all_gather | solution.py:127
  371.1 13.7 %shard_map.220 = (bf16[1024,1024]{1,0:T(8,128)(2,1)}, bf16[1024,1024]{1,0:T(8,128)(2,1)}) custom-call(s32[1]{0:T(128)} %bitcast.36.half_ref.core_ref, bf16[1024,1024]{1,0:T(8,128)(2,1)} %get-tuple-element.220.a0, bf16[1024,1024]{1,0:T(8,128)(2,1)} %get-tuple-element.221.a1, bf16[2,1024,2048]{2,1,0:T(8,128)(2,1)} %bitcast.165, ...), custom_call_target="tpu_custom_call" | custom-call | flops 8589934592 | bytes 16777216 | tf_op jit(solution)/shard_map/pallas_call | solution.py:411
  391.3 12.6 %shard_map.221.b.a1 = bf16[1024,2048]{1,0:T(8,128)(2,1)} custom-call(s32[1]{0:T(128)} %bitcast.34.half_ref, bf16[1024,2048]{1,0:T(8,128)(2,1)} %shard_map.219.g, bf16[2,1024,2048]{2,1,0:T(8,128)(2,1)} %bitcast.169, f32[1024,1024]{1,0:T(8,128)} %get-tuple-element.232.gate_ref, f32[1024,1024]{1,0:T(8,128)} %get-tuple-element.233.up_ref), custom_call_target="tpu_custom_call" | custom-call | flops 4294967296 | bytes 20971520 | tf_op jit(solution)/shard_map/pallas_call | solution.py:378
  404.0 14.0 %shard_map.222 = bf16[2048,2048]{1,0:T(8,128)(2,1)} custom-call(bf16[2048,1024]{1,0:T(8,128)(2,1)} %copy.45.a, bf16[1024,2048]{1,0:T(8,128)(2,1)} %shard_map.221.b.a1), custom_call_target="tpu_custom_call" | custom-call | flops 8589934592 | bytes 16777216 | tf_op jit(solution)/shard_map/pallas_call | solution.py:300
  423.5 12.9 %shard_map.223.a0.b = bf16[1024,2048]{1,0:T(8,128)(2,1)} custom-call(s32[1]{0:T(128)} %bitcast.36.half_ref.core_ref, bf16[1024,2048]{1,0:T(8,128)(2,1)} %shard_map.219.g, bf16[2,1024,2048]{2,1,0:T(8,128)(2,1)} %bitcast.170, f32[1024,1024]{1,0:T(8,128)} %get-tuple-element.236.gate_ref, f32[1024,1024]{1,0:T(8,128)} %get-tuple-element.237.up_ref), custom_call_target="tpu_custom_call" | custom-call | flops 4294967296 | bytes 20971520 | tf_op jit(solution)/shard_map/pallas_call | solution.py:378
  436.4 24.2 %shard_map.224 = (bf16[1024,1024]{1,0:T(8,128)(2,1)}, bf16[1024,1024]{1,0:T(8,128)(2,1)}) custom-call(s32[1]{0:T(128)} %bitcast.36.half_ref.core_ref, bf16[1024,2048]{1,0:T(8,128)(2,1)} %shard_map.223.a0.b, bf16[1024,2048]{1,0:T(8,128)(2,1)} %shard_map.221.b.a1, bf16[2,2048,2048]{2,1,0:T(8,128)(2,1)} %bitcast.161, bf16[2,2048,2048]{2,1,0:T(8,128)(2,1)} %bitcast.162, ...), custom_call_target="tpu_custom_call" | custom-call | flops 17179869184 | bytes 29360128 | tf_op jit(solution)/shard_map/pallas_call | solution.py:265
  467.4 15.6 %shard_map.225 = bf16[2048,2048]{1,0:T(8,128)(2,1)} custom-call(bf16[2048,1024]{1,0:T(8,128)(2,1)} %copy.45.a, bf16[1024,2048]{1,0:T(8,128)(2,1)} %shard_map.223.a0.b, bf16[2048,2048]{1,0:T(8,128)(2,1)} %collective-permute-done.31.refs_0_), custom_call_target="tpu_custom_call" | custom-call | flops 8589934592 | bytes 25165824 | tf_op jit(solution)/shard_map/pallas_call | solution.py:300
  523.0 19.7 %collective-permute-done.37 = bf16[256,2048]{1,0:T(8,128)(2,1)S(1)} collective-permute-done((bf16[256,2048]{1,0:T(8,128)(2,1)S(1)}, bf16[256,2048]{1,0:T(8,128)(2,1)S(1)}, u32[]{:S(2)}, u32[]{:S(2)}) %collective-permute-start.37) | collective-permute-done | bytes 1048608 | tf_op jit(solution)/shard_map/ppermute | solution.py:78
  570.3 15.5 %shard_map.226 = (bf16[1024,256]{1,0:T(8,128)(2,1)}, bf16[1024,256]{1,0:T(8,128)(2,1)}, bf16[1024,256]{1,0:T(8,128)(2,1)}, bf16[1024,256]{1,0:T(8,128)(2,1)}) custom-call(bf16[1024,2048]{1,0:T(8,128)(2,1)} %constant_dynamic-update-slice_fusion.5.g_ref, bf16[2,512,1024]{2,1,0:T(8,128)(2,1)} %pad_maximum_fusion.2.w_ref, ...), custom_call_target="tpu_custom_call" | custom-call | flops 7516192768 | bytes 11534336 | tf_op jit(solution)/shard_map/pallas_call | solution.py:692
  657.1 10.9 %collective-permute-done.50 = bf16[256,1024]{1,0:T(8,128)(2,1)} collective-permute-done((bf16[256,1024]{1,0:T(8,128)(2,1)}, bf16[256,1024]{1,0:T(8,128)(2,1)}, u32[]{:S(2)}, u32[]{:S(2)}) %collective-permute-start.50) | collective-permute-done | bytes 524320 | tf_op jit(solution)/shard_map/ppermute | solution.py:75
  676.3 24.4 %collective-permute-done.53 = f32[2,2048]{1,0:T(2,128)S(1)} collective-permute-done((f32[2,2048]{1,0:T(2,128)S(1)}, f32[2,2048]{1,0:T(2,128)S(1)}, u32[]{:S(2)}, u32[]{:S(2)}) %collective-permute-start.53) | collective-permute-done | bytes 16416 | tf_op jit(solution)/shard_map/ppermute | solution.py:93
  717.7 24.4 %collective-permute-done.57.refs_6_ = bf16[256,2048]{1,0:T(8,128)(2,1)} collective-permute-done((bf16[256,2048]{1,0:T(8,128)(2,1)}, bf16[256,2048]{1,0:T(8,128)(2,1)}, u32[]{:S(2)}, u32[]{:S(2)}) %collective-permute-start.57) | collective-permute-done | bytes 1048608 | tf_op jit(solution)/shard_map/ppermute | solution.py:1048
  (407 shorter events, 383.5 us)
Async XLA Ops:
  8.5 29.7 %collective-permute-start.1 = (bf16[2,256]{1,0:T(2,128)(2,1)S(1)}, bf16[2,256]{1,0:T(2,128)(2,1)S(1)}, u32[]{:S(2)}, u32[]{:S(2)}) collective-permute-start(bf16[2,256]{1,0:T(2,128)(2,1)S(1)} %pad_maximum_fusion.17), channel_id=1, source_target_pairs={{0,4},{1,5},{2,6},{3,7},{4,0},{5,1},{6,2},{7,3},{8,12},{9,13},{10,... | collective-permute-start | bytes 3080 | tf_op jit(solution)/shard_map/ppermute | solution.py:78
  19.3 32.8 %all-to-all-start = ((bf16[8,128,512]{2,1,0:T(8,128)(2,1)}), bf16[8,128,512]{2,1,0:T(8,128)(2,1)S(1)}, u32[]{:S(2)}, u32[]{:S(2)}) async-start(bf16[8,128,512]{2,1,0:T(8,128)(2,1)} %shard_map.212), calls=%async_computation | async-start | bytes 2097152 | tf_op jit(solution)/shard_map/all_to_all | solution.py:880
  24.2 102.0 %all-gather.4.cloned.1.call-start = ((), (), s32[]{:S(2)}) async-start(), calls=%async_computation.6 | async-start | bytes 7077888 | tf_op jit(solution)/shard_map/all_gather | solution.py:127
  52.1 237.2 %all-gather.6.cloned.1.call-start = ((), (), s32[]{:S(2)}) async-start(), calls=%async_computation.7 | async-start | bytes 18874368 | tf_op jit(solution)/shard_map/all_gather | solution.py:127
  54.3 46.7 %collective-permute-start.9 = (bf16[256,2048]{1,0:T(8,128)(2,1)}, bf16[256,2048]{1,0:T(8,128)(2,1)}, u32[]{:S(2)}, u32[]{:S(2)}) collective-permute-start(bf16[256,2048]{1,0:T(8,128)(2,1)} %get-tuple-element.178), channel_id=1, source_target_pairs={{0,4},{1,5},{2,6},{3,7},{4,0},{5,1},{6,2},{7,3},{8,12},{9,13},{10,... | collective-permute-start | bytes 3145736 | tf_op jit(solution)/shard_map/ppermute | solution.py:78
  80.0 30.8 %collective-permute-start.8 = (bf16[2,2,128,512]{3,2,1,0:T(8,128)(2,1)S(1)}, bf16[2,2,128,512]{3,2,1,0:T(8,128)(2,1)}, u32[]{:S(2)}, u32[]{:S(2)}) collective-permute-start(bf16[2,2,128,512]{3,2,1,0:T(8,128)(2,1)S(1)} %slice.236), channel_id=1, source_target_pairs={{0,4},{1,5},{2,6},{3,7},{4,0},{5,1},{6,2},{7,3},{8,12},{9,13},{10,... | collective-permute-start | bytes 1572872 | tf_op jit(solution)/shard_map/ppermute | solution.py:78
  110.8 260.4 %all-gather.8.cloned.1.call-start = ((), (), s32[]{:S(2)}) async-start(), calls=%async_computation.8 | async-start | bytes 9437184 | tf_op jit(solution)/shard_map/all_gather | solution.py:127
  200.6 59.1 %all-to-all-start.1 = ((bf16[8,128,512]{2,1,0:T(8,128)(2,1)}), bf16[8,128,512]{2,1,0:T(8,128)(2,1)}, u32[]{:S(2)}, u32[]{:S(2)}) async-start(bf16[8,128,512]{2,1,0:T(8,128)(2,1)} %shard_map.214), calls=%async_computation.1 | async-start | bytes 2097152 | tf_op jit(solution)/shard_map/all_to_all | solution.py:880
  204.9 296.8 %reduce-scatter.4.cloned.1.call-start = ((), (), s32[]{:S(2)}) async-start(), calls=%async_computation.9 | async-start | bytes 5242880 | tf_op jit(solution)/shard_map/reduce_scatter | solution.py:964
  219.0 40.7 %collective-permute-start.19 = (bf16[256,2048]{1,0:T(8,128)(2,1)}, bf16[256,2048]{1,0:T(8,128)(2,1)S(1)}, u32[]{:S(2)}, u32[]{:S(2)}) collective-permute-start(bf16[256,2048]{1,0:T(8,128)(2,1)} %get-tuple-element.331), channel_id=1, source_target_pairs={{0,4},{1,5},{2,6},{3,7},{4,0},{5,1},{6,2},{7,3},{8,12},{9,13},{10,... | collective-permute-start | bytes 3145736 | tf_op jit(solution)/shard_map/ppermute | solution.py:78
  220.0 39.6 %collective-permute-start.18 = (bf16[256,2048]{1,0:T(8,128)(2,1)}, bf16[256,2048]{1,0:T(8,128)(2,1)}, u32[]{:S(2)}, u32[]{:S(2)}) collective-permute-start(bf16[256,2048]{1,0:T(8,128)(2,1)} %get-tuple-element.331), channel_id=1, source_target_pairs={{0,2},{1,3},{2,0},{3,1},{4,6},{5,7},{6,4},{7,5},{8,10},{9,11},{10,... | collective-permute-start | bytes 3145736 | tf_op jit(solution)/shard_map/ppermute | solution.py:75
  388.4 29.6 %collective-permute-start.27 = (bf16[2,256,1024]{2,1,0:T(8,128)(2,1)}, bf16[2,256,1024]{2,1,0:T(8,128)(2,1)S(1)}, u32[]{:S(2)}, u32[]{:S(2)}) collective-permute-start(bf16[2,256,1024]{2,1,0:T(8,128)(2,1)} %pad_maximum_fusion.7), channel_id=1, source_target_pairs={{0,2},{1,3},{2,0},{3,1},{4,6},{5,7},{6,4},{7,5},{8,10},{9,11},{10,... | collective-permute-start | bytes 3145736 | tf_op jit(solution)/shard_map/ppermute | solution.py:75
  418.0 42.6 %collective-permute-start.31 = (bf16[2048,2048]{1,0:T(8,128)(2,1)}, bf16[2048,2048]{1,0:T(8,128)(2,1)}, u32[]{:S(2)}, u32[]{:S(2)}) collective-permute-start(bf16[2048,2048]{1,0:T(8,128)(2,1)} %shard_map.222), channel_id=1, source_target_pairs={{0,1},{1,0},{2,3},{3,2},{4,5},{5,4},{6,7},{7,6},{8,9},{9,8},{10,11... | collective-permute-start | bytes 25165832 | tf_op jit(solution)/shard_map/ppermute | solution.py:81
  418.1 221.7 %reduce-scatter.6.cloned.1.call-start = ((), (), s32[]{:S(2)}) async-start(), calls=%async_computation.10 | async-start | bytes 10485760 | tf_op jit(solution)/shard_map/reduce_scatter | solution.py:964
  420.3 40.3 %collective-permute-start.30 = (bf16[256,1024]{1,0:T(8,128)(2,1)}, bf16[256,1024]{1,0:T(8,128)(2,1)}, u32[]{:S(2)}, u32[]{:S(2)}) collective-permute-start(bf16[256,1024]{1,0:T(8,128)(2,1)} %fusion.26), channel_id=1, source_target_pairs={{0,2},{1,3},{2,0},{3,1},{4,6},{5,7},{6,4},{7,5},{8,10},{9,11},{10,... | collective-permute-start | bytes 1572872 | tf_op jit(solution)/shard_map/ppermute | solution.py:75
  423.1 37.5 %collective-permute-start.29 = (bf16[256,1024]{1,0:T(8,128)(2,1)}, bf16[256,1024]{1,0:T(8,128)(2,1)}, u32[]{:S(2)}, u32[]{:S(2)}) collective-permute-start(bf16[256,1024]{1,0:T(8,128)(2,1)} %fusion.27), channel_id=1, source_target_pairs={{0,4},{1,5},{2,6},{3,7},{4,0},{5,1},{6,2},{7,3},{8,12},{9,13},{10,... | collective-permute-start | bytes 1572872 | tf_op jit(solution)/shard_map/ppermute | solution.py:78
  490.8 251.4 %reduce-scatter.8.cloned.1.call-start = ((), (), s32[]{:S(2)}) async-start(), calls=%async_computation.11 | async-start | bytes 3932160 | tf_op jit(solution)/shard_map/reduce_scatter | solution.py:964
  569.0 41.5 %collective-permute-start.42 = (bf16[256,2048]{1,0:T(8,128)(2,1)}, bf16[256,2048]{1,0:T(8,128)(2,1)}, u32[]{:S(2)}, u32[]{:S(2)}) collective-permute-start(bf16[256,2048]{1,0:T(8,128)(2,1)} %reduce-scatter.4.cloned.1.call-done.refs_0_), channel_id=1, source_target_pairs={{0,2},{1,3},{2,0},{3,1},{4,6},{5,7},{6,4},{7,5},{8,10},{9,11},{10,... | collective-permute-start | bytes 3145736 | tf_op jit(solution)/shard_map/ppermute | solution.py:75
  655.0 54.9 %collective-permute-start.55 = (bf16[256,2048]{1,0:T(8,128)(2,1)S(1)}, bf16[256,2048]{1,0:T(8,128)(2,1)S(1)}, u32[]{:S(2)}, u32[]{:S(2)}) collective-permute-start(bf16[256,2048]{1,0:T(8,128)(2,1)S(1)} %get-tuple-element.304.refs_0_), channel_id=1, source_target_pairs={{0,2},{1,3},{2,0},{3,1},{4,6},{5,7},{6,4},{7,5},{8,10},{9,11},{10,... | collective-permute-start | bytes 3145736 | tf_op jit(solution)/shard_map/ppermute | solution.py:75
  655.6 54.3 %collective-permute-start.56 = (bf16[256,2048]{1,0:T(8,128)(2,1)}, bf16[256,2048]{1,0:T(8,128)(2,1)S(1)}, u32[]{:S(2)}, u32[]{:S(2)}) collective-permute-start(bf16[256,2048]{1,0:T(8,128)(2,1)} %get-tuple-element.300), channel_id=1, source_target_pairs={{0,4},{1,5},{2,6},{3,7},{4,0},{5,1},{6,2},{7,3},{8,12},{9,13},{10,... | collective-permute-start | bytes 3145736 | tf_op jit(solution)/shard_map/ppermute | solution.py:78
  674.2 30.4 %collective-permute-start.51 = (bf16[256,1024]{1,0:T(8,128)(2,1)S(1)}, bf16[256,1024]{1,0:T(8,128)(2,1)S(1)}, u32[]{:S(2)}, u32[]{:S(2)}) collective-permute-start(bf16[256,1024]{1,0:T(8,128)(2,1)S(1)} %broadcast_select_fusion), channel_id=1, source_target_pairs={{0,2},{1,3},{2,0},{3,1},{4,6},{5,7},{6,4},{7,5},{8,10},{9,11},{10,... | collective-permute-start | bytes 1572872 | tf_op jit(solution)/shard_map/ppermute | solution.py:75
  711.9 60.5 %all-to-all-start.2 = ((bf16[8,2,128,512]{3,2,1,0:T(8,128)(2,1)}), bf16[8,2,128,512]{3,2,1,0:T(8,128)(2,1)S(1)}, u32[]{:S(2)}, u32[]{:S(2)}) async-start(bf16[8,2,128,512]{3,2,1,0:T(8,128)(2,1)} %pad_maximum_fusion.5), calls=%async_computation.4 | async-start | bytes 4194304 | tf_op jit(solution)/shard_map/all_to_all | solution.py:880
  717.2 28.5 %collective-permute-start.63 = (bf16[256,2048]{1,0:T(8,128)(2,1)S(1)}, bf16[256,2048]{1,0:T(8,128)(2,1)}, u32[]{:S(2)}, u32[]{:S(2)}) collective-permute-start(bf16[256,2048]{1,0:T(8,128)(2,1)S(1)} %get-tuple-element.304.refs_0_), channel_id=1, source_target_pairs={{0,1},{1,0},{2,3},{3,2},{4,5},{5,4},{6,7},{7,6},{8,9},{9,8},{10,11... | collective-permute-start | bytes 3145736 | tf_op jit(solution)/shard_map/ppermute | solution.py:81
  717.3 29.8 %collective-permute-start.64 = (bf16[256,2048]{1,0:T(8,128)(2,1)}, bf16[256,2048]{1,0:T(8,128)(2,1)}, u32[]{:S(2)}, u32[]{:S(2)}) collective-permute-start(bf16[256,2048]{1,0:T(8,128)(2,1)} %copy-done.6), channel_id=1, source_target_pairs={{0,1},{1,0},{2,3},{3,2},{4,5},{5,4},{6,7},{7,6},{8,9},{9,8},{10,11... | collective-permute-start | bytes 3145736 | tf_op jit(solution)/shard_map/ppermute | solution.py:81
  (102 other events, 1430.7 us)
Sparse Core Ops, SparseCore 0:
  52.3 62.7 all-gather.3
  117.2 172.0 all-gather.5
  290.9 80.1 all-gather.7
  418.2 73.5 reduce-scatter.3
  494.7 144.9 reduce-scatter.5
  655.1 58.3 reduce-scatter.7

commit v6 on v5

--- a/solution.py
+++ b/solution.py
@@ -105,22 +105,18 @@
         m = ax.shape[0] // 2
         return self.x(ay[:m]), self.y(ax[m:])
 
-    def scatter_one(self, left, right):
-        n = left.shape[0] // 4
-        l4 = left.reshape(4, n, left.shape[1])
-        return self.x(jnp.stack([l4[1], l4[3]])), self.y(right[2 * n :].reshape(2, n, right.shape[1]))
-
-    def scatter_two(self, left, right, gl, gr):
-        n = left.shape[0] // 4
-        l_far = self.y((left[2 * n : 3 * n].astype(F32) + gl[1]).astype(BF16))
-        r_far = self.x((right[n : 2 * n].astype(F32) + gr[1]).astype(BF16))
+    def scatter_one(self, p):
+        return self.x(p[1]), self.y(p[3])
+
+    def scatter_two(self, p, gl, gr):
+        l_far = self.y((p[0][1].astype(F32) + gl[1]).astype(BF16))
+        r_far = self.x((p[2][1].astype(F32) + gr[1]).astype(BF16))
         return l_far, r_far
 
-    def scatter_end(self, left, right, gl, gr, l_far, r_far):
-        n = left.shape[0] // 4
+    def scatter_end(self, p, gl, gr, l_far, r_far):
         gl, gr, l_far, r_far = sync(gl, gr, l_far, r_far)
-        l_own = left[:n].astype(F32) + gl[0] + l_far
-        r_own = right[:n].astype(F32) + gr[0] + r_far
+        l_own = p[0][0].astype(F32) + gl[0] + l_far
+        r_own = p[2][0].astype(F32) + gr[0] + r_far
         return jnp.concatenate([l_own, r_own], axis=1)
 
     def gather_planes(self, a):
@@ -148,6 +144,25 @@
     return pl.CostEstimate(
         flops=flops, bytes_accessed=bytes_accessed, transcendentals=transcendentals
     )
+
+
+def split_parts(left, right):
+    n, h = left.shape[0] // 4, left.shape[1]
+    l4, r4 = left.reshape(4, n, h), right.reshape(4, n, h)
+    return (
+        jnp.stack([l4[0], l4[2]]),
+        jnp.stack([l4[1], l4[3]]),
+        r4[:2],
+        r4[2:],
+    )
+
+
+def store_parts(outs, left, right):
+    n = left.shape[0] // 4
+    for i in range(4):
+        rows = slice(i * n, (i + 1) * n)
+        outs[i % 2][i // 2] = left[rows]
+        outs[2 + i // 2][i % 2] = right[rows]
 
 
 def rank_scalar(rank):
@@ -256,15 +271,16 @@
     tile = min(n // 2, 256)
     steps = n // 2 // tile
 
-    def kernel(core_ref, a0, a1, l0, l1, r0, r1, left, right):
-        left[...] = (mm_nt(a0[...], l0[...]) + mm_nt(a1[...], l1[...])).astype(BF16)
-        right[...] = (mm_nt(a0[...], r0[...]) + mm_nt(a1[...], r1[...])).astype(BF16)
+    def kernel(core_ref, a0, a1, l0, l1, r0, r1, *outs):
+        left = (mm_nt(a0[...], l0[...]) + mm_nt(a1[...], l1[...])).astype(BF16)
+        right = (mm_nt(a0[...], r0[...]) + mm_nt(a1[...], r1[...])).astype(BF16)
+        store_parts(outs, left, right)
 
     whole = pl.BlockSpec((m, k), lambda i, r: (0, 0))
-    out = pl.BlockSpec((m, tile), lambda i, r: (0, i))
+    out = pl.BlockSpec((2, m // 4, tile), lambda i, r: (0, 0, i))
     return pl.pallas_call(
         kernel,
-        out_shape=(jax.ShapeDtypeStruct((m, n // 2), BF16),) * 2,
+        out_shape=(jax.ShapeDtypeStruct((2, m // 4, n // 2), BF16),) * 4,
         grid_spec=pltpu.PrefetchScalarGridSpec(
             num_scalar_prefetch=1,
             grid=(steps,),
@@ -276,7 +292,7 @@
                 pl.BlockSpec((None, tile, k), lambda i, r: (r[0], i + steps, 0)),
                 pl.BlockSpec((None, tile, k), lambda i, r: (1 - r[0], i + steps, 0)),
             ],
-            out_specs=(out, out),
+            out_specs=(out,) * 4,
         ),
         cost_estimate=estimate(
             flops=4 * m * k * n, bytes_accessed=4 * (m + n) * k + 2 * m * n, transcendentals=0
@@ -402,15 +418,16 @@
     tile = 256
     steps = n // 2 // tile
 
-    def kernel(core_ref, a0, a1, l0, l1, r0, r1, left, right):
-        left[...] = (mm(a0[...], l0[...]) + mm(a1[...], l1[...])).astype(BF16)
-        right[...] = (mm(a0[...], r0[...]) + mm(a1[...], r1[...])).astype(BF16)
+    def kernel(core_ref, a0, a1, l0, l1, r0, r1, *outs):
+        left = (mm(a0[...], l0[...]) + mm(a1[...], l1[...])).astype(BF16)
+        right = (mm(a0[...], r0[...]) + mm(a1[...], r1[...])).astype(BF16)
+        store_parts(outs, left, right)
 
     whole = pl.BlockSpec((m, k), lambda i, r: (0, 0))
-    out = pl.BlockSpec((m, tile), lambda i, r: (0, i))
+    out = pl.BlockSpec((2, m // 4, tile), lambda i, r: (0, 0, i))
     return pl.pallas_call(
         kernel,
-        out_shape=(jax.ShapeDtypeStruct((m, n // 2), BF16),) * 2,
+        out_shape=(jax.ShapeDtypeStruct((2, m // 4, n // 2), BF16),) * 4,
         grid_spec=pltpu.PrefetchScalarGridSpec(
             num_scalar_prefetch=1,
             grid=(steps,),
@@ -422,7 +439,7 @@
                 pl.BlockSpec((None, k, tile), lambda i, r: (r[0], 0, i + steps)),
                 pl.BlockSpec((None, k, tile), lambda i, r: (1 - r[0], 0, i + steps)),
             ],
-            out_specs=(out, out),
+            out_specs=(out,) * 4,
         ),
         cost_estimate=estimate(
             flops=4 * m * k * n, bytes_accessed=4 * (m + n) * k + 2 * m * n, transcendentals=0
@@ -937,9 +954,10 @@
         mixed, lse, attn_left, attn_right = attend(q0, q1, keys, values, w_o, at_q, at_k)
         hidden_zero = rows_in.astype(F32)
         factor_pre = norm_factor(hidden_zero)
-        gl, gr = sync(*links.scatter_one(attn_left, attn_right))
-        l_far, r_far = sync(*links.scatter_two(attn_left, attn_right, gl, gr))
-        hidden_one = hidden_zero + links.scatter_end(attn_left, attn_right, gl, gr, l_far, r_far)
+        attn_p = split_parts(attn_left, attn_right)
+        gl, gr = sync(*links.scatter_one(attn_p))
+        l_far, r_far = sync(*links.scatter_two(attn_p, gl, gr))
+        hidden_one = hidden_zero + links.scatter_end(attn_p, gl, gr, l_far, r_far)
         factor_mid = norm_factor(hidden_one)
         n_own = (hidden_one * factor_mid * gain_mid).astype(BF16)
         ax, ay, got_cot = sync(*links.gather_one(n_own), got_cot)
@@ -968,28 +986,25 @@
         sum_down = both_cores(act_own, down_in, links.c(down_far))
         g_down = over_planes(sum_down)
         w_down, d_in = sync(w_down, down_in, sum_down)[:2]
-        ff_left, ff_right = forward_product(c_me, (act_own, act_far), w_down)
-        ff_left, ff_right, d_in = sync(ff_left, ff_right, d_in)
-        ff_l, ff_r = links.scatter_one(ff_left, ff_right)
+        *ff_p, d_in = sync(*forward_product(c_me, (act_own, act_far), w_down), d_in)
+        ff_l, ff_r = links.scatter_one(ff_p)
         in_far = ff_back(1 - c_me, d_in, w_down, far_gate, far_up)
         ff_far = weight_product(turned, in_far)
         ff_l, ff_r, ff_far, in_far = sync(ff_l, ff_r, ff_far, in_far)
-        ff_lf, ff_rf = links.scatter_two(ff_left, ff_right, ff_l, ff_r)
+        ff_lf, ff_rf = links.scatter_two(ff_p, ff_l, ff_r)
         in_own = ff_back(c_me, after(d_in, ff_far), w_down, own_gate, own_up)
-        dn_left, dn_right = back_product(c_me, (in_own, in_far), w_ff)
-        dn_left, dn_right, in_own, ff_lf, ff_rf, ff_got = sync(
-            dn_left, dn_right, in_own, ff_lf, ff_rf, links.c(ff_far)
-        )
-        dn_l, dn_r = links.scatter_one(dn_left, dn_right)
+        dn_p = back_product(c_me, (in_own, in_far), w_ff)
+        in_own, ff_lf, ff_rf, ff_got, *dn_p = sync(in_own, ff_lf, ff_rf, links.c(ff_far), *dn_p)
+        dn_l, dn_r = links.scatter_one(dn_p)
         sum_ff = weight_product(turned, in_own, ff_got)
         dn_l, dn_r, sum_ff = sync(dn_l, dn_r, sum_ff)
         g_ff = over_planes(sum_ff)
-        dn_lf, dn_rf = links.scatter_two(dn_left, dn_right, dn_l, dn_r)
+        dn_lf, dn_rf = links.scatter_two(dn_p, dn_l, dn_r)
         out_rows = (
-            (hidden_one + links.scatter_end(ff_left, ff_right, ff_l, ff_r, ff_lf, ff_rf)) * valid
+            (hidden_one + links.scatter_end(ff_p, ff_l, ff_r, ff_lf, ff_rf)) * valid
         ).astype(BF16)
         dn_lf, dn_rf, g_down, out_rows = sync(dn_lf, dn_rf, g_down, out_rows)
-        normed_two_grad = links.scatter_end(dn_left, dn_right, dn_l, dn_r, dn_lf, dn_rf)
+        normed_two_grad = links.scatter_end(dn_p, dn_l, dn_r, dn_lf, dn_rf)
 
         mid_upstream, midnorm_part = norm_backward(normed_two_grad, hidden_one, factor_mid, gain_mid)
         hidden_one_grad = down_in[:rows].astype(F32) + mid_upstream
@@ -1019,8 +1034,8 @@
         normed_part, grad_even, grad_odd, out_send, down_x, *o_parts = sync(
             normed_part, grad_even, grad_odd, out_send, down_x, *o_parts
         )
-        np_left, np_right = normed_part[:, :half], normed_part[:, half:]
-        np_l, np_r = links.scatter_one(np_left, np_right)
+        np_p = split_parts(normed_part[:, :half], normed_part[:, half:])
+        np_l, np_r = links.scatter_one(np_p)
         g_o_cols = jnp.zeros((8 * HEAD_SIZE, eighth), BF16)
         for p, part in enumerate(o_parts):
             g_o_cols = lax.dynamic_update_slice(
@@ -1034,10 +1049,10 @@
             np_l, np_r, attn_sum, *own_and_other(g_ff)
         )
         g_attn = over_planes(attn_sum)
-        np_lf, np_rf = links.scatter_two(np_left, np_right, np_l, np_r)
+        np_lf, np_rf = links.scatter_two(np_p, np_l, np_r)
         ff_x, ff_y = links.x(ff_own), links.y(ff_other)
         np_lf, np_rf = sync(np_lf, np_rf)
-        normed_grad = links.scatter_end(np_left, np_right, np_l, np_r, np_lf, np_rf)
+        normed_grad = links.scatter_end(np_p, np_l, np_r, np_lf, np_rf)
         pre_upstream, prenorm_part = norm_backward(normed_grad, hidden_zero, factor_pre, gain_pre)
         token_rows = ((hidden_one_grad + pre_upstream) * valid).astype(BF16)
         norm_plane = links.sum_plane(jnp.stack([prenorm_part, midnorm_part]))

time: 800 us -> 792 us (0.990)
    unnamed x102 -> x106, local copies, waits for them, and re-layouts: 24.3 us -> 24.2 us
where the time goes in v6:
time: 792 us; the launch traced here: 782 us
  waiting for transfers between devices  296 us (37%)
  Pallas kernels  205 us (26%)
  starting transfers between devices  85.5 us (11%)
  local copies, waits for them, and re-layouts  70.2 us (9%)
  other arithmetic  64.2 us (8%)
  matrix products  42.4 us (5%)
  between operations  18.5 us (2%)
    ppermute x23, waiting for transfers between devices, x(): return lax.ppermute(a, AXES, self.px)  86.1 us
    ppermute x23, waiting for transfers between devices, y(): return lax.ppermute(a, AXES, self.py)  76.6 us
    dot_general x7, matrix products, dot(): return lax.dot_general(a, b, (dims, ((), ())), preferred_element_type=F32)  42.4 us
    all_to_all x3, waiting for transfers between devices, exchange(): lax.all_to_all(send, ('z', 'c'), split_axis=0, concat_axis=0, tiled=True)  38.9 us
    pallas_call x2, Pallas kernels, weight_product(): pl.pallas_call(kernel, out_shape=jax.ShapeDtypeStruct((m, n), BF16), grid...  29.6 us
    pallas_call x2, Pallas kernels, ff_front(): pl.pallas_call(kernel, out_shape=(jax.ShapeDtypeStruct((m, f), F32), jax....  28.4 us
    ppermute x3, waiting for transfers between devices, sum_plane(): a = a + lax.ppermute(a, AXES, p)  27.4 us
    ppermute x23, starting transfers between devices, y(): return lax.ppermute(a, AXES, self.py)  26.5 us
  transfers between devices with their start and end apart: 82, of which 37 were waited for; matrix products, arithmetic and copies ran while one was open for 21% of the time, Pallas kernels for 24%

profile of v6, /device:TPU:0, one launch (start us, length us, event | category | flops | bytes accessed | tf_op | source)
XLA Modules:
  0.0 781.6 jit_solution(10831290080138031669)
XLA Ops:
  61.9 16.5 %collective-permute-done.6.refs_2_ = bf16[4,2,128,512]{3,2,1,0:T(8,128)(2,1)S(1)} collective-permute-done((bf16[4,2,128,512]{3,2,1,0:T(8,128)(2,1)S(1)}, bf16[4,2,128,512]{3,2,1,0:T(8,128)(2,1)S(1)}, u32[]{:S(2)}, u32[]{:S(2)}) %collective-permute-start.6) | collective-permute-done | bytes 1048608 | tf_op jit(solution)/shard_map/ppermute | solution.py:78
  80.6 20.4 %collective-permute-done.9 = bf16[256,2048]{1,0:T(8,128)(2,1)} collective-permute-done((bf16[256,2048]{1,0:T(8,128)(2,1)}, bf16[256,2048]{1,0:T(8,128)(2,1)}, u32[]{:S(2)}, u32[]{:S(2)}) %collective-permute-start.9) | collective-permute-done | bytes 1048608 | tf_op jit(solution)/shard_map/ppermute | solution.py:78
  116.4 9.9 %shard_map.213 = (bf16[1024,2048]{1,0:T(8,128)(2,1)}, bf16[256,2048]{1,0:T(8,128)(2,1)}) custom-call(s32[10]{0:T(128)} %concatenate.50.info_ref, bf16[4,2,128,512]{3,2,1,0:T(8,128)(2,1)} %bitcast.158, bf16[4,2,128,512]{3,2,1,0:T(8,128)(2,1)} %copy-done.11, bf16[4,2,128,512]{3,2,1,0:T(8,128)(2,1)} %copy-done.10, ...), custom_call_target="tpu_custom_call" | custom-call | flops 4194304 | bytes 10485760 | tf_op jit(solution)/shard_map/pallas_call | solution.py:559
  156.0 11.3 %shard_map.216 = (bf16[1024,512]{1,0:T(8,128)(2,1)}, f32[2,1024,1]{2,1,0:T(8,128)}, bf16[1024,1024]{1,0:T(8,128)(2,1)}, bf16[1024,1024]{1,0:T(8,128)(2,1)}) custom-call(bf16[1024,256]{1,0:T(8,128)(2,1)} %get-tuple-element.198.q0_ref, bf16[1024,256]{1,0:T(8,128)(2,1)} %get-tuple-element.199.q1_ref, bf16[1024,256]{1,0:T(8,128)(2,1)} %get-tuple-element.200.k_ref, ...), custom_call_target="tpu_custom_call" | custom-call | flops 4294967296 | bytes 9437184 | tf_op jit(solution)/shard_map/pallas_call | solution.py:634
  171.1 24.0 %collective-permute-done.14 = bf16[2,256,1024]{2,1,0:T(8,128)(2,1)S(1)} collective-permute-done((bf16[2,256,1024]{2,1,0:T(8,128)(2,1)S(1)}, bf16[2,256,1024]{2,1,0:T(8,128)(2,1)S(1)}, u32[]{:S(2)}, u32[]{:S(2)}) %collective-permute-start.14) | collective-permute-done | bytes 1048608 | tf_op jit(solution)/shard_map/ppermute | solution.py:75
  221.0 38.9 %all-to-all-done.1 = bf16[8,128,512]{2,1,0:T(8,128)(2,1)} async-done(((bf16[8,128,512]{2,1,0:T(8,128)(2,1)}), bf16[8,128,512]{2,1,0:T(8,128)(2,1)}, u32[]{:S(2)}, u32[]{:S(2)}) %all-to-all-start.1) | async-done | bytes 1048608 | tf_op jit(solution)/shard_map/all_to_all | solution.py:897
  279.4 10.0 %all-gather.6.cloned.1.call-done = bf16[4096,2048]{1,0:T(8,128)(2,1)} async-done(((bf16[512,2048]{1,0:T(8,128)(2,1)}), bf16[4096,2048]{1,0:T(8,128)(2,1)}) %all-gather.6.cloned.1.call-update) | async-done | bytes 16777232 | tf_op jit(solution)/shard_map/all_gather | solution.py:123
  289.4 14.5 %shard_map.217 = (f32[1024,1024]{1,0:T(8,128)}, f32[1024,1024]{1,0:T(8,128)}, bf16[1024,1024]{1,0:T(8,128)(2,1)}) custom-call(s32[1]{0:T(128)} %bitcast.34.half_ref, bf16[1024,2048]{1,0:T(8,128)(2,1)} %constant_dynamic-update-slice_fusion.x, bf16[2,2048,2048]{2,1,0:T(8,128)(2,1)} %bitcast.139, bf16[2,2048,2048]{2,1,0:T(8,128)(2,1)} %bitcast.140), custom_call_target="tpu_custom_call" | custom-call | flops 8589934592 | bytes 23068672 | tf_op jit(solution)/shard_map/pallas_call | solution.py:348
  309.9 14.0 %shard_map.218 = (f32[1024,1024]{1,0:T(8,128)}, f32[1024,1024]{1,0:T(8,128)}, bf16[1024,1024]{1,0:T(8,128)(2,1)}) custom-call(s32[1]{0:T(128)} %bitcast.36.half_ref.core_ref, bf16[1024,2048]{1,0:T(8,128)(2,1)} %constant_dynamic-update-slice_fusion.x, bf16[2,2048,2048]{2,1,0:T(8,128)(2,1)} %bitcast.141, bf16[2,2048,2048]{2,1,0:T(8,128)(2,1)} %bitcast.142), custom_call_target="tpu_custom_call" | custom-call | flops 8589934592 | bytes 23068672 | tf_op jit(solution)/shard_map/pallas_call | solution.py:348
  332.4 9.4 %convolution_convert_fusion = bf16[1024,2048]{1,0:T(8,128)(2,1)} fusion(bf16[1024,1024]{1,0:T(8,128)(2,1)} %get-tuple-element.229.a1, bf16[1024,2048]{1,0:T(8,128)(2,1)} %shard_map.219.g), kind=kOutput, calls=%fused_computation.8 | convolution fusion | flops 4297064448 | bytes 10485760 | tf_op jit(solution)/shard_map/dot_general | solution.py:24
  349.2 10.6 %add_convert_fusion.1 = bf16[1024,2048]{1,0:T(8,128)(2,1)} fusion(bf16[1024,2048]{1,0:T(8,128)(2,1)} %collective-permute-done.26, bf16[1024,1024]{1,0:T(8,128)(2,1)} %get-tuple-element.228.a0, bf16[1024,2048]{1,0:T(8,128)(2,1)} %shard_map.219.g), kind=kOutput, calls=%fused_computation.1 | convolution fusion | flops 4301258752 | bytes 14680064 | tf_op jit(solution)/shard_map/dot_general | solution.py:24
  359.8 11.4 %all-gather.8.cloned.1.call-done = bf16[2048,2048]{1,0:T(8,128)(2,1)} async-done(((bf16[256,2048]{1,0:T(8,128)(2,1)}), bf16[2048,2048]{1,0:T(8,128)(2,1)}) %all-gather.8.cloned.1.call-update) | async-done | bytes 8388624 | tf_op jit(solution)/shard_map/all_gather | solution.py:123
  371.2 13.6 %shard_map.220 = (bf16[2,256,1024]{2,1,0:T(8,128)(2,1)}, bf16[2,256,1024]{2,1,0:T(8,128)(2,1)}, bf16[2,256,1024]{2,1,0:T(8,128)(2,1)}, bf16[2,256,1024]{2,1,0:T(8,128)(2,1)}) custom-call(s32[1]{0:T(128)} %bitcast.36.half_ref.core_ref, bf16[1024,1024]{1,0:T(8,128)(2,1)} %get-tuple-element.228.a0, bf16[1024,1024]{1,0:T(8,128)(2,1)} %get-tuple-element.229.a1, ...), custom_call_target="tpu_custom_call" | custom-call | flops 8589934592 | bytes 16777216 | tf_op jit(solution)/shard_map/pallas_call | solution.py:428
  387.8 12.6 %shard_map.221.b.a1 = bf16[1024,2048]{1,0:T(8,128)(2,1)} custom-call(s32[1]{0:T(128)} %bitcast.34.half_ref, bf16[1024,2048]{1,0:T(8,128)(2,1)} %shard_map.219.g, bf16[2,1024,2048]{2,1,0:T(8,128)(2,1)} %bitcast.151, f32[1024,1024]{1,0:T(8,128)} %get-tuple-element.242.gate_ref, f32[1024,1024]{1,0:T(8,128)} %get-tuple-element.243.up_ref), custom_call_target="tpu_custom_call" | custom-call | flops 4294967296 | bytes 20971520 | tf_op jit(solution)/shard_map/pallas_call | solution.py:394
  400.4 14.0 %shard_map.222 = bf16[2048,2048]{1,0:T(8,128)(2,1)} custom-call(bf16[2048,1024]{1,0:T(8,128)(2,1)} %copy.45.a, bf16[1024,2048]{1,0:T(8,128)(2,1)} %shard_map.221.b.a1), custom_call_target="tpu_custom_call" | custom-call | flops 8589934592 | bytes 16777216 | tf_op jit(solution)/shard_map/pallas_call | solution.py:316
  420.0 12.7 %shard_map.223.a0.b = bf16[1024,2048]{1,0:T(8,128)(2,1)} custom-call(s32[1]{0:T(128)} %bitcast.36.half_ref.core_ref, bf16[1024,2048]{1,0:T(8,128)(2,1)} %shard_map.219.g, bf16[2,1024,2048]{2,1,0:T(8,128)(2,1)} %bitcast.152, f32[1024,1024]{1,0:T(8,128)} %get-tuple-element.246.gate_ref, f32[1024,1024]{1,0:T(8,128)} %get-tuple-element.247.up_ref), custom_call_target="tpu_custom_call" | custom-call | flops 4294967296 | bytes 20971520 | tf_op jit(solution)/shard_map/pallas_call | solution.py:394
  432.7 24.2 %shard_map.224 = (bf16[2,256,1024]{2,1,0:T(8,128)(2,1)}, bf16[2,256,1024]{2,1,0:T(8,128)(2,1)}, bf16[2,256,1024]{2,1,0:T(8,128)(2,1)}, bf16[2,256,1024]{2,1,0:T(8,128)(2,1)}) custom-call(s32[1]{0:T(128)} %bitcast.36.half_ref.core_ref, bf16[1024,2048]{1,0:T(8,128)(2,1)} %shard_map.223.a0.b, bf16[1024,2048]{1,0:T(8,128)(2,1)} %shard_map.221.b.a1, ...), custom_call_target="tpu_custom_call" | custom-call | flops 17179869184 | bytes 29360128 | tf_op jit(solution)/shard_map/pallas_call | solution.py:281
  460.2 15.6 %shard_map.225 = bf16[2048,2048]{1,0:T(8,128)(2,1)} custom-call(bf16[2048,1024]{1,0:T(8,128)(2,1)} %copy.45.a, bf16[1024,2048]{1,0:T(8,128)(2,1)} %shard_map.223.a0.b, bf16[2048,2048]{1,0:T(8,128)(2,1)} %collective-permute-done.31.refs_0_), custom_call_target="tpu_custom_call" | custom-call | flops 8589934592 | bytes 25165824 | tf_op jit(solution)/shard_map/pallas_call | solution.py:316
  515.4 19.6 %collective-permute-done.37 = bf16[256,2048]{1,0:T(8,128)(2,1)S(1)} collective-permute-done((bf16[256,2048]{1,0:T(8,128)(2,1)S(1)}, bf16[256,2048]{1,0:T(8,128)(2,1)S(1)}, u32[]{:S(2)}, u32[]{:S(2)}) %collective-permute-start.37) | collective-permute-done | bytes 1048608 | tf_op jit(solution)/shard_map/ppermute | solution.py:78
  562.4 15.5 %shard_map.226 = (bf16[1024,256]{1,0:T(8,128)(2,1)}, bf16[1024,256]{1,0:T(8,128)(2,1)}, bf16[1024,256]{1,0:T(8,128)(2,1)}, bf16[1024,256]{1,0:T(8,128)(2,1)}) custom-call(bf16[1024,2048]{1,0:T(8,128)(2,1)} %constant_dynamic-update-slice_fusion.5.g_ref, bf16[2,512,1024]{2,1,0:T(8,128)(2,1)} %pad_maximum_fusion.2.w_ref, ...), custom_call_target="tpu_custom_call" | custom-call | flops 7516192768 | bytes 11534336 | tf_op jit(solution)/shard_map/pallas_call | solution.py:709
  623.8 12.4 %reduce-scatter.6.cloned.1.call-done = bf16[512,2048]{1,0:T(8,128)(2,1)} async-done(((bf16[2048,2048]{1,0:T(8,128)(2,1)}), bf16[512,2048]{1,0:T(8,128)(2,1)}) %reduce-scatter.6.cloned.1.call-update) | async-done | bytes 2097168 | tf_op jit(solution)/shard_map/reduce_scatter | solution.py:982
  649.1 11.0 %collective-permute-done.50 = bf16[256,1024]{1,0:T(8,128)(2,1)} collective-permute-done((bf16[256,1024]{1,0:T(8,128)(2,1)}, bf16[256,1024]{1,0:T(8,128)(2,1)}, u32[]{:S(2)}, u32[]{:S(2)}) %collective-permute-start.50) | collective-permute-done | bytes 524320 | tf_op jit(solution)/shard_map/ppermute | solution.py:75
  668.4 24.3 %collective-permute-done.53 = f32[2,2048]{1,0:T(2,128)S(1)} collective-permute-done((f32[2,2048]{1,0:T(2,128)S(1)}, f32[2,2048]{1,0:T(2,128)S(1)}, u32[]{:S(2)}, u32[]{:S(2)}) %collective-permute-start.53) | collective-permute-done | bytes 16416 | tf_op jit(solution)/shard_map/ppermute | solution.py:93
  709.7 24.5 %collective-permute-done.57.refs_6_ = bf16[256,2048]{1,0:T(8,128)(2,1)} collective-permute-done((bf16[256,2048]{1,0:T(8,128)(2,1)}, bf16[256,2048]{1,0:T(8,128)(2,1)}, u32[]{:S(2)}, u32[]{:S(2)}) %collective-permute-start.57) | collective-permute-done | bytes 1048608 | tf_op jit(solution)/shard_map/ppermute | solution.py:1063
  (405 shorter events, 372.4 us)
Async XLA Ops:
  8.5 29.7 %collective-permute-start.1 = (bf16[2,256]{1,0:T(2,128)(2,1)S(1)}, bf16[2,256]{1,0:T(2,128)(2,1)S(1)}, u32[]{:S(2)}, u32[]{:S(2)}) collective-permute-start(bf16[2,256]{1,0:T(2,128)(2,1)S(1)} %pad_maximum_fusion.15), channel_id=1, source_target_pairs={{0,4},{1,5},{2,6},{3,7},{4,0},{5,1},{6,2},{7,3},{8,12},{9,13},{10,... | collective-permute-start | bytes 3080 | tf_op jit(solution)/shard_map/ppermute | solution.py:78
  19.3 32.8 %all-to-all-start = ((bf16[8,128,512]{2,1,0:T(8,128)(2,1)}), bf16[8,128,512]{2,1,0:T(8,128)(2,1)S(1)}, u32[]{:S(2)}, u32[]{:S(2)}) async-start(bf16[8,128,512]{2,1,0:T(8,128)(2,1)} %shard_map.212), calls=%async_computation | async-start | bytes 2097152 | tf_op jit(solution)/shard_map/all_to_all | solution.py:897
  24.2 102.1 %all-gather.4.cloned.1.call-start = ((), (), s32[]{:S(2)}) async-start(), calls=%async_computation.6 | async-start | bytes 7077888 | tf_op jit(solution)/shard_map/all_gather | solution.py:123
  52.2 237.2 %all-gather.6.cloned.1.call-start = ((), (), s32[]{:S(2)}) async-start(), calls=%async_computation.7 | async-start | bytes 18874368 | tf_op jit(solution)/shard_map/all_gather | solution.py:123
  54.3 46.7 %collective-permute-start.9 = (bf16[256,2048]{1,0:T(8,128)(2,1)}, bf16[256,2048]{1,0:T(8,128)(2,1)}, u32[]{:S(2)}, u32[]{:S(2)}) collective-permute-start(bf16[256,2048]{1,0:T(8,128)(2,1)} %get-tuple-element.186), channel_id=1, source_target_pairs={{0,4},{1,5},{2,6},{3,7},{4,0},{5,1},{6,2},{7,3},{8,12},{9,13},{10,... | collective-permute-start | bytes 3145736 | tf_op jit(solution)/shard_map/ppermute | solution.py:78
  80.1 30.8 %collective-permute-start.8 = (bf16[2,2,128,512]{3,2,1,0:T(8,128)(2,1)S(1)}, bf16[2,2,128,512]{3,2,1,0:T(8,128)(2,1)}, u32[]{:S(2)}, u32[]{:S(2)}) collective-permute-start(bf16[2,2,128,512]{3,2,1,0:T(8,128)(2,1)S(1)} %slice.227), channel_id=1, source_target_pairs={{0,4},{1,5},{2,6},{3,7},{4,0},{5,1},{6,2},{7,3},{8,12},{9,13},{10,... | collective-permute-start | bytes 1572872 | tf_op jit(solution)/shard_map/ppermute | solution.py:78
  110.8 260.4 %all-gather.8.cloned.1.call-start = ((), (), s32[]{:S(2)}) async-start(), calls=%async_computation.8 | async-start | bytes 9437184 | tf_op jit(solution)/shard_map/all_gather | solution.py:123
  200.9 59.0 %all-to-all-start.1 = ((bf16[8,128,512]{2,1,0:T(8,128)(2,1)}), bf16[8,128,512]{2,1,0:T(8,128)(2,1)}, u32[]{:S(2)}, u32[]{:S(2)}) async-start(bf16[8,128,512]{2,1,0:T(8,128)(2,1)} %shard_map.214), calls=%async_computation.1 | async-start | bytes 2097152 | tf_op jit(solution)/shard_map/all_to_all | solution.py:897
  205.1 289.2 %reduce-scatter.4.cloned.1.call-start = ((), (), s32[]{:S(2)}) async-start(), calls=%async_computation.9 | async-start | bytes 5242880 | tf_op jit(solution)/shard_map/reduce_scatter | solution.py:982
  219.3 40.5 %collective-permute-start.19 = (bf16[256,2048]{1,0:T(8,128)(2,1)}, bf16[256,2048]{1,0:T(8,128)(2,1)S(1)}, u32[]{:S(2)}, u32[]{:S(2)}) collective-permute-start(bf16[256,2048]{1,0:T(8,128)(2,1)} %get-tuple-element.347), channel_id=1, source_target_pairs={{0,4},{1,5},{2,6},{3,7},{4,0},{5,1},{6,2},{7,3},{8,12},{9,13},{10,... | collective-permute-start | bytes 3145736 | tf_op jit(solution)/shard_map/ppermute | solution.py:78
  220.2 39.6 %collective-permute-start.18 = (bf16[256,2048]{1,0:T(8,128)(2,1)}, bf16[256,2048]{1,0:T(8,128)(2,1)}, u32[]{:S(2)}, u32[]{:S(2)}) collective-permute-start(bf16[256,2048]{1,0:T(8,128)(2,1)} %get-tuple-element.347), channel_id=1, source_target_pairs={{0,2},{1,3},{2,0},{3,1},{4,6},{5,7},{6,4},{7,5},{8,10},{9,11},{10,... | collective-permute-start | bytes 3145736 | tf_op jit(solution)/shard_map/ppermute | solution.py:75
  384.8 29.7 %collective-permute-start.27 = (bf16[2,256,1024]{2,1,0:T(8,128)(2,1)}, bf16[2,256,1024]{2,1,0:T(8,128)(2,1)}, u32[]{:S(2)}, u32[]{:S(2)}) collective-permute-start(bf16[2,256,1024]{2,1,0:T(8,128)(2,1)} %get-tuple-element.239), channel_id=1, source_target_pairs={{0,2},{1,3},{2,0},{3,1},{4,6},{5,7},{6,4},{7,5},{8,10},{9,11},{10,... | collective-permute-start | bytes 3145736 | tf_op jit(solution)/shard_map/ppermute | solution.py:75
  414.4 42.5 %collective-permute-start.31 = (bf16[2048,2048]{1,0:T(8,128)(2,1)}, bf16[2048,2048]{1,0:T(8,128)(2,1)}, u32[]{:S(2)}, u32[]{:S(2)}) collective-permute-start(bf16[2048,2048]{1,0:T(8,128)(2,1)} %shard_map.222), channel_id=1, source_target_pairs={{0,1},{1,0},{2,3},{3,2},{4,5},{5,4},{6,7},{7,6},{8,9},{9,8},{10,11... | collective-permute-start | bytes 25165832 | tf_op jit(solution)/shard_map/ppermute | solution.py:81
  414.5 221.7 %reduce-scatter.6.cloned.1.call-start = ((), (), s32[]{:S(2)}) async-start(), calls=%async_computation.10 | async-start | bytes 10485760 | tf_op jit(solution)/shard_map/reduce_scatter | solution.py:982
  416.9 40.1 %collective-permute-start.30 = (bf16[256,1024]{1,0:T(8,128)(2,1)}, bf16[256,1024]{1,0:T(8,128)(2,1)}, u32[]{:S(2)}, u32[]{:S(2)}) collective-permute-start(bf16[256,1024]{1,0:T(8,128)(2,1)} %fusion.29), channel_id=1, source_target_pairs={{0,2},{1,3},{2,0},{3,1},{4,6},{5,7},{6,4},{7,5},{8,10},{9,11},{10,... | collective-permute-start | bytes 1572872 | tf_op jit(solution)/shard_map/ppermute | solution.py:75
  419.6 37.3 %collective-permute-start.29 = (bf16[256,1024]{1,0:T(8,128)(2,1)}, bf16[256,1024]{1,0:T(8,128)(2,1)}, u32[]{:S(2)}, u32[]{:S(2)}) collective-permute-start(bf16[256,1024]{1,0:T(8,128)(2,1)} %fusion.28), channel_id=1, source_target_pairs={{0,4},{1,5},{2,6},{3,7},{4,0},{5,1},{6,2},{7,3},{8,12},{9,13},{10,... | collective-permute-start | bytes 1572872 | tf_op jit(solution)/shard_map/ppermute | solution.py:78
  483.6 250.6 %reduce-scatter.8.cloned.1.call-start = ((), (), s32[]{:S(2)}) async-start(), calls=%async_computation.11 | async-start | bytes 3932160 | tf_op jit(solution)/shard_map/reduce_scatter | solution.py:982
  561.0 41.6 %collective-permute-start.42 = (bf16[256,2048]{1,0:T(8,128)(2,1)}, bf16[256,2048]{1,0:T(8,128)(2,1)}, u32[]{:S(2)}, u32[]{:S(2)}) collective-permute-start(bf16[256,2048]{1,0:T(8,128)(2,1)} %reduce-scatter.4.cloned.1.call-done.refs_0_), channel_id=1, source_target_pairs={{0,2},{1,3},{2,0},{3,1},{4,6},{5,7},{6,4},{7,5},{8,10},{9,11},{10,... | collective-permute-start | bytes 3145736 | tf_op jit(solution)/shard_map/ppermute | solution.py:75
  646.9 54.9 %collective-permute-start.55 = (bf16[256,2048]{1,0:T(8,128)(2,1)S(1)}, bf16[256,2048]{1,0:T(8,128)(2,1)S(1)}, u32[]{:S(2)}, u32[]{:S(2)}) collective-permute-start(bf16[256,2048]{1,0:T(8,128)(2,1)S(1)} %get-tuple-element.320.refs_0_), channel_id=1, source_target_pairs={{0,2},{1,3},{2,0},{3,1},{4,6},{5,7},{6,4},{7,5},{8,10},{9,11},{10,... | collective-permute-start | bytes 3145736 | tf_op jit(solution)/shard_map/ppermute | solution.py:75
  647.7 54.2 %collective-permute-start.56 = (bf16[256,2048]{1,0:T(8,128)(2,1)}, bf16[256,2048]{1,0:T(8,128)(2,1)S(1)}, u32[]{:S(2)}, u32[]{:S(2)}) collective-permute-start(bf16[256,2048]{1,0:T(8,128)(2,1)} %get-tuple-element.316), channel_id=1, source_target_pairs={{0,4},{1,5},{2,6},{3,7},{4,0},{5,1},{6,2},{7,3},{8,12},{9,13},{10,... | collective-permute-start | bytes 3145736 | tf_op jit(solution)/shard_map/ppermute | solution.py:78
  666.3 30.3 %collective-permute-start.51 = (bf16[256,1024]{1,0:T(8,128)(2,1)S(1)}, bf16[256,1024]{1,0:T(8,128)(2,1)S(1)}, u32[]{:S(2)}, u32[]{:S(2)}) collective-permute-start(bf16[256,1024]{1,0:T(8,128)(2,1)S(1)} %broadcast_select_fusion), channel_id=1, source_target_pairs={{0,2},{1,3},{2,0},{3,1},{4,6},{5,7},{6,4},{7,5},{8,10},{9,11},{10,... | collective-permute-start | bytes 1572872 | tf_op jit(solution)/shard_map/ppermute | solution.py:75
  703.9 60.4 %all-to-all-start.2 = ((bf16[8,2,128,512]{3,2,1,0:T(8,128)(2,1)}), bf16[8,2,128,512]{3,2,1,0:T(8,128)(2,1)S(1)}, u32[]{:S(2)}, u32[]{:S(2)}) async-start(bf16[8,2,128,512]{3,2,1,0:T(8,128)(2,1)} %pad_maximum_fusion.5), calls=%async_computation.4 | async-start | bytes 4194304 | tf_op jit(solution)/shard_map/all_to_all | solution.py:897
  709.2 28.5 %collective-permute-start.63 = (bf16[256,2048]{1,0:T(8,128)(2,1)S(1)}, bf16[256,2048]{1,0:T(8,128)(2,1)}, u32[]{:S(2)}, u32[]{:S(2)}) collective-permute-start(bf16[256,2048]{1,0:T(8,128)(2,1)S(1)} %get-tuple-element.320.refs_0_), channel_id=1, source_target_pairs={{0,1},{1,0},{2,3},{3,2},{4,5},{5,4},{6,7},{7,6},{8,9},{9,8},{10,11... | collective-permute-start | bytes 3145736 | tf_op jit(solution)/shard_map/ppermute | solution.py:81
  709.2 29.9 %collective-permute-start.64 = (bf16[256,2048]{1,0:T(8,128)(2,1)}, bf16[256,2048]{1,0:T(8,128)(2,1)}, u32[]{:S(2)}, u32[]{:S(2)}) collective-permute-start(bf16[256,2048]{1,0:T(8,128)(2,1)} %copy-done.6), channel_id=1, source_target_pairs={{0,1},{1,0},{2,3},{3,2},{4,5},{5,4},{6,7},{7,6},{8,9},{9,8},{10,11... | collective-permute-start | bytes 3145736 | tf_op jit(solution)/shard_map/ppermute | solution.py:81
  (104 other events, 1442.3 us)
Sparse Core Ops, SparseCore 0:
  52.3 62.7 all-gather.3
  117.2 172.1 all-gather.5
  291.0 80.1 all-gather.7
  414.7 73.5 reduce-scatter.3
  491.2 144.9 reduce-scatter.5
  647.0 58.9 reduce-scatter.7
